TPU v7x, 32 devices: a whole 2x2x4 slice. The times are simulated.
32 devices in a mesh: head: 8 (over z, x), row: 4 (over y, core).
Axes of the slice: x: 2, y: 2, z: 4, core: 2. Of those that a mesh axis runs over, the one named last changes fastest.
Arguments:
- tokens: bfloat16 [4, 2048, 2048], P('row', 'head'), may hold values from -6 to 6
- w_query: float32 [2048, 2048], P('row', 'head'), may hold values from -0.125 to 0.125
- w_key: float32 [2048, 2048], P('row', 'head'), may hold values from -0.125 to 0.125
- w_value: float32 [2048, 4096], P('row', 'head'), may hold values from -0.125 to 0.125
- w_outgate: float32 [2048, 4096], P('row', 'head'), may hold values from -0.125 to 0.125
- w_alpha: float32 [2048, 16], P('row', 'head'), may hold values from -0.125 to 0.125
- w_beta: float32 [2048, 16], P('row', 'head'), may hold values from -0.125 to 0.125
- conv_query: float32 [4, 2048], P(None, ('head', 'row')), may hold values from -3 to 3
- conv_key: float32 [4, 2048], P(None, ('head', 'row')), may hold values from -3 to 3
- conv_value: float32 [4, 4096], P(None, ('head', 'row')), may hold values from -3 to 3
- a_log: float32 [16], replicated, may hold values from -6 to -1
- dt_bias: float32 [16], replicated, may hold values from -4 to -1
- o_gain: float32 [256], replicated, may hold values from 0.5 to 1.5
- w_out: float32 [4096, 2048], P('head', 'row'), may hold values from -0.125 to 0.125
- gain_in: float32 [2048], replicated, may hold values from 0.5 to 1.5
- gain_ffn: float32 [2048], replicated, may hold values from 0.5 to 1.5
- w_gate: float32 [2048, 5632], P('head', 'row'), may hold values from -0.125 to 0.125
- w_up: float32 [2048, 5632], P('head', 'row'), may hold values from -0.125 to 0.125
- w_down: float32 [5632, 2048], P('row', 'head'), may hold values from -0.109375 to 0.109375
- segments: int32 [4, 2048], P('row'), may hold values from 0 to 2, never falling along the last dimension, each value on 1 to 1024 neighbouring positions
- valid_len: int32 [4], P('row'), may hold values from 1024 to 2048, as said below
- cotangent: bfloat16 [4, 2048, 2048], P('row', 'head'), may hold values from -6 to 6
Outputs:
- output: bfloat16 [4, 2048, 2048], P('row', 'head')
- grad_tokens: float32 [4, 2048, 2048], P('row', 'head')
- grad_w_query: float32 [2048, 2048], P('row', 'head')
- grad_w_key: float32 [2048, 2048], P('row', 'head')
- grad_w_value: float32 [2048, 4096], P('row', 'head')
- grad_w_outgate: float32 [2048, 4096], P('row', 'head')
- grad_w_alpha: float32 [2048, 16], P('row', 'head')
- grad_w_beta: float32 [2048, 16], P('row', 'head')
- grad_conv_query: float32 [4, 2048], P(None, ('head', 'row'))
- grad_conv_key: float32 [4, 2048], P(None, ('head', 'row'))
- grad_conv_value: float32 [4, 4096], P(None, ('head', 'row'))
- grad_a_log: float32 [16], replicated
- grad_dt_bias: float32 [16], replicated
- grad_o_gain: float32 [256], replicated
- grad_w_out: float32 [4096, 2048], P('head', 'row')
- grad_gain_in: float32 [2048], replicated
- grad_gain_ffn: float32 [2048], replicated
- grad_w_gate: float32 [2048, 5632], P('head', 'row')
- grad_w_up: float32 [2048, 5632], P('head', 'row')
- grad_w_down: float32 [5632, 2048], P('row', 'head')
Inputs may be any that keep to these rules, and one draw needn't show every extreme that they name: `segments`: within each row group segment numbers run 0, 1, 2 without falling, and the group's longest sequence has exactly 1024 tokens. The first valid_len tokens of a row group are real and the rest are padding; at least one group has no padding.
All inputs are finite; a program needn't handle non-finite values.
Results may differ from a plain program's by a relative error of at most 0.015.
The roundings to bfloat16 on the way count: a program that leaves them out, or rounds other values in their place, can miss the bound.
Values may be sent and summed in bfloat16 or wider, within the bound.
A program may use at most 320 MiB of HBM per device.

v0:
```python
from functools import partial
import math

import jax
import jax.numpy as jnp
from jax import lax
from jax.sharding import PartitionSpec as P

BLOCK = 64


precise = lax.Precision.HIGHEST
epsilon = 1e-06
o_floor = 0.001


def rms_norm(vector, gain_vec, floor_add=epsilon):
    return (
        vector * lax.rsqrt(jnp.mean(vector * vector, axis=-1, keepdims=True) + floor_add) * gain_vec
    )


def unit_norm(vector):
    return vector * lax.rsqrt(jnp.sum(vector * vector, axis=-1, keepdims=True) + epsilon)


def swiglu(gate_pre, up_pre):
    return jax.nn.silu(gate_pre) * up_pre


def short_conv(signal, kernel, seg_ids):
    tap_count = kernel.shape[0]
    length = signal.shape[0]
    summed = signal * kernel[tap_count - 1]
    for offset in range(1, tap_count):
        shifted = jnp.concatenate(
            [jnp.zeros((offset, signal.shape[1]), signal.dtype), signal[: length - offset]], axis=0
        )
        seg_shift = jnp.concatenate(
            [jnp.full((offset,), -1, jnp.int32), seg_ids[: length - offset]]
        )
        keep_mask = (seg_shift == seg_ids).astype(signal.dtype)
        summed = summed + shifted * kernel[tap_count - 1 - offset] * keep_mask[:, None]
    return summed


def span_step(carried_in, pieces):
    state_mat, last_seg = carried_in
    queries, keys_n, values, decays, beta_rate, seg_ids = pieces
    block_len = queries.shape[0]
    cumulative = jnp.cumsum(decays)
    places = jnp.arange(block_len)
    lower_tri = places[:, None] >= places[None, :]
    inside = jnp.logical_and(seg_ids[:, None] == seg_ids[None, :], lower_tri)
    log_gap = jnp.where(inside, cumulative[:, None] - cumulative[None, :], 0.0)
    within = jnp.exp(log_gap) * inside.astype(jnp.float32)
    strict = within * (places[:, None] > places[None, :]).astype(jnp.float32)
    carried = jnp.exp(cumulative) * (seg_ids == last_seg).astype(jnp.float32)
    key_gram = jnp.dot(keys_n, keys_n.T, precision=precise)
    system = jnp.eye(block_len, dtype=jnp.float32) + beta_rate[:, None] * strict * key_gram
    right_side = beta_rate[:, None] * (
        values - carried[:, None] * jnp.dot(keys_n, state_mat.T, precision=precise)
    )
    update = jax.scipy.linalg.solve_triangular(system, right_side, lower=True, unit_diagonal=True)
    scores = jnp.dot(queries, keys_n.T, precision=precise) * within
    output = carried[:, None] * jnp.dot(queries, state_mat.T, precision=precise) + jnp.dot(
        scores, update, precision=precise
    )
    tail_row = within[block_len - 1]
    new_state = carried[block_len - 1] * state_mat + jnp.dot(
        update.T, tail_row[:, None] * keys_n, precision=precise
    )
    return ((new_state, seg_ids[block_len - 1]), output)


def delta_rule(queries, keys_n, values, decays, beta_rate, seg_ids):
    length = queries.shape[0]
    count_blocks = length // BLOCK

    def blocks(array):
        return array.reshape((count_blocks, BLOCK) + array.shape[1:])

    initial = (jnp.zeros((values.shape[1], keys_n.shape[1]), jnp.float32), jnp.int32(-1))
    final_carry, outputs = lax.scan(
        jax.checkpoint(span_step),
        initial,
        (
            blocks(queries),
            blocks(keys_n),
            blocks(values),
            blocks(decays),
            blocks(beta_rate),
            blocks(seg_ids),
        ),
    )
    return outputs.reshape(length, values.shape[1])


def head_mixer(
    proj_query,
    proj_key,
    proj_value,
    proj_gate,
    proj_alpha,
    proj_beta,
    kernel_query,
    kernel_key,
    kernel_value,
    a_here,
    dt_here,
    o_gain,
    seg_ids,
    live_mask,
):
    queries = unit_norm(jax.nn.silu(short_conv(proj_query, kernel_query, seg_ids))) * (
        1.0 / math.sqrt(proj_query.shape[1])
    )
    keys_n = unit_norm(jax.nn.silu(short_conv(proj_key, kernel_key, seg_ids)))
    values = jax.nn.silu(short_conv(proj_value, kernel_value, seg_ids))
    decays = -jnp.exp(a_here) * jax.nn.softplus(proj_alpha + dt_here)
    beta_rate = jax.nn.sigmoid(proj_beta)
    recurrent = delta_rule(queries, keys_n, values, decays, beta_rate, seg_ids)
    return rms_norm(recurrent, o_gain, o_floor) * jax.nn.silu(proj_gate) * live_mask[:, None]


def local_mixer(
    proj_query,
    proj_key,
    proj_value,
    proj_gate,
    proj_alpha,
    proj_beta,
    kernel_query,
    kernel_key,
    kernel_value,
    a_here,
    dt_here,
    o_gain,
    seg_ids=None,
    live_mask=None,
):
    row_count = proj_query.shape[0]
    heads_here = proj_alpha.shape[1]

    def by_head(array):
        return jnp.moveaxis(array.reshape(row_count, heads_here, -1), 1, 0)

    def kernel_heads(kernel):
        return jnp.moveaxis(kernel.reshape(kernel.shape[0], heads_here, -1), 1, 0)

    per_head = jax.vmap(head_mixer, in_axes=(0,) * 11 + (None, None, None))
    mixed_heads = per_head(
        by_head(proj_query),
        by_head(proj_key),
        by_head(proj_value),
        by_head(proj_gate),
        proj_alpha.T,
        proj_beta.T,
        kernel_heads(kernel_query),
        kernel_heads(kernel_key),
        kernel_heads(kernel_value),
        a_here,
        dt_here,
        o_gain,
        seg_ids,
        live_mask,
    )
    return jnp.moveaxis(mixed_heads, 0, 1).reshape(row_count, -1)


def contract_rows(left, right):
    return lax.dot_general(
        left, right, (((0,), (0,)), ((), ())), preferred_element_type=jnp.float32
    )


def contract_cols(left, right):
    return lax.dot_general(
        left, right, (((1,), (1,)), ((), ())), preferred_element_type=jnp.float32
    )


def on_device(
    tokens,
    w_query,
    w_key,
    w_value,
    w_outgate,
    w_alpha,
    w_beta,
    conv_query,
    conv_key,
    conv_value,
    a_log,
    dt_bias,
    o_gain,
    w_out,
    gain_in,
    gain_ffn,
    w_gate,
    w_up,
    w_down,
    segments,
    valid_len,
    cotangent,
):
    residual = tokens[0].astype(jnp.float32)
    heads_here = w_alpha.shape[1]
    head_first = lax.axis_index("head") * heads_here
    norm_one, pull_one = jax.vjp(rms_norm, residual, gain_in)
    normed_one = norm_one.astype(jnp.bfloat16)
    gathered = (
        lax.all_gather(w_query.astype(jnp.bfloat16), "row", axis=0, tiled=True),
        lax.all_gather(w_key.astype(jnp.bfloat16), "row", axis=0, tiled=True),
        lax.all_gather(w_value.astype(jnp.bfloat16), "row", axis=0, tiled=True),
        lax.all_gather(w_outgate.astype(jnp.bfloat16), "row", axis=0, tiled=True),
        lax.all_gather(w_alpha.astype(jnp.bfloat16), "row", axis=0, tiled=True),
        lax.all_gather(w_beta.astype(jnp.bfloat16), "row", axis=0, tiled=True),
        lax.all_gather(conv_query.astype(jnp.bfloat16), "row", axis=1, tiled=True),
        lax.all_gather(conv_key.astype(jnp.bfloat16), "row", axis=1, tiled=True),
        lax.all_gather(conv_value.astype(jnp.bfloat16), "row", axis=1, tiled=True),
        lax.all_gather(w_out.astype(jnp.bfloat16), "row", axis=1, tiled=True),
    )
    w_inward = jnp.concatenate(
        [gathered[0], gathered[1], gathered[2], gathered[3], gathered[4], gathered[5]], axis=1
    )
    out_matrix = gathered[9]
    edges = [0]
    for member in gathered[:6]:
        edges.append(edges[-1] + member.shape[1])
    all_rows = lax.all_gather(normed_one, "head", axis=0, tiled=True)
    projected = jnp.dot(all_rows, w_inward, preferred_element_type=jnp.float32)
    proj_parts = [projected[:, edges[spot] : edges[spot + 1]] for spot in range(6)]
    seg_ids = segments[0]
    live_mask = (jnp.arange(seg_ids.shape[0]) < valid_len[0]).astype(jnp.float32)
    a_here = lax.dynamic_slice_in_dim(a_log, head_first, heads_here)
    dt_here = lax.dynamic_slice_in_dim(dt_bias, head_first, heads_here)
    mixer_fn = partial(local_mixer, seg_ids=seg_ids, live_mask=live_mask)
    mixed, pull_core = jax.vjp(
        mixer_fn,
        proj_parts[0],
        proj_parts[1],
        proj_parts[2],
        proj_parts[3],
        proj_parts[4],
        proj_parts[5],
        gathered[6].astype(jnp.float32),
        gathered[7].astype(jnp.float32),
        gathered[8].astype(jnp.float32),
        a_here,
        dt_here,
        o_gain,
    )
    mixed_half = mixed.astype(jnp.bfloat16)
    mixer_output = lax.psum_scatter(
        jnp.dot(mixed_half, out_matrix, preferred_element_type=jnp.float32),
        "head",
        scatter_dimension=0,
        tiled=True,
    )
    middle = residual + mixer_output
    norm_two, pull_two = jax.vjp(rms_norm, middle, gain_ffn)
    normed_two = norm_two.astype(jnp.bfloat16)
    ffn_mats = (
        lax.all_gather(w_gate.astype(jnp.bfloat16), "head", axis=0, tiled=True),
        lax.all_gather(w_up.astype(jnp.bfloat16), "head", axis=0, tiled=True),
        lax.all_gather(w_down.astype(jnp.bfloat16), "head", axis=1, tiled=True),
    )
    grad_out = cotangent[0]
    ffn_inputs, grad_out_rows = (
        lax.all_gather(normed_two, "row", axis=0, tiled=True),
        lax.all_gather(grad_out, "row", axis=0, tiled=True),
    )
    gate_pre = jnp.dot(ffn_inputs, ffn_mats[0], preferred_element_type=jnp.float32)
    up_pre = jnp.dot(ffn_inputs, ffn_mats[1], preferred_element_type=jnp.float32)
    hidden_val, pull_act = jax.vjp(swiglu, gate_pre, up_pre)
    hidden_half = hidden_val.astype(jnp.bfloat16)
    ffn_output = lax.psum_scatter(
        jnp.dot(hidden_half, ffn_mats[2], preferred_element_type=jnp.float32).astype(jnp.bfloat16),
        "row",
        scatter_dimension=0,
        tiled=True,
    ).astype(jnp.float32)
    final_out = (middle + ffn_output).astype(jnp.bfloat16)
    grad_hidden = contract_cols(grad_out_rows, ffn_mats[2])
    grad_down = contract_rows(hidden_half, grad_out_rows)
    grad_gate_f, grad_up_f = pull_act(grad_hidden)
    grad_gate = grad_gate_f.astype(jnp.bfloat16)
    grad_upper = grad_up_f.astype(jnp.bfloat16)
    grad_wgate = contract_rows(ffn_inputs, grad_gate)
    grad_wup = contract_rows(ffn_inputs, grad_upper)
    grad_norm_two = lax.psum_scatter(
        contract_cols(grad_gate, ffn_mats[0]) + contract_cols(grad_upper, ffn_mats[1]),
        "row",
        scatter_dimension=0,
        tiled=True,
    )
    grad_mid_part, grad_gain_ffn = pull_two(grad_norm_two)
    grad_middle = grad_out.astype(jnp.float32) + grad_mid_part
    ffn_grads = (
        lax.psum_scatter(
            grad_wgate.astype(jnp.bfloat16), "head", scatter_dimension=0, tiled=True
        ).astype(jnp.float32),
        lax.psum_scatter(
            grad_wup.astype(jnp.bfloat16), "head", scatter_dimension=0, tiled=True
        ).astype(jnp.float32),
        lax.psum_scatter(
            grad_down.astype(jnp.bfloat16), "head", scatter_dimension=1, tiled=True
        ).astype(jnp.float32),
    )
    grad_mid_half = grad_middle.astype(jnp.bfloat16)
    grad_mid_rows = lax.all_gather(grad_mid_half, "head", axis=0, tiled=True)
    grad_mixed = contract_cols(grad_mid_rows, out_matrix)
    grad_wout = contract_rows(mixed_half, grad_mid_rows)
    core_grads = pull_core(grad_mixed)
    grad_proj = jnp.concatenate(
        [core_grads[0], core_grads[1], core_grads[2], core_grads[3], core_grads[4], core_grads[5]],
        axis=1,
    ).astype(jnp.bfloat16)
    grad_inward = contract_rows(all_rows, grad_proj)
    grad_norm_one = lax.psum_scatter(
        contract_cols(grad_proj, w_inward).astype(jnp.bfloat16),
        "head",
        scatter_dimension=0,
        tiled=True,
    ).astype(jnp.float32)
    grad_in_part, grad_gain_in = pull_one(grad_norm_one)
    grad_input = grad_middle + grad_in_part
    inward_parts = [grad_inward[:, edges[spot] : edges[spot + 1]] for spot in range(6)]
    mixer_grads = (
        lax.psum_scatter(
            inward_parts[0].astype(jnp.bfloat16), "row", scatter_dimension=0, tiled=True
        ).astype(jnp.float32),
        lax.psum_scatter(
            inward_parts[1].astype(jnp.bfloat16), "row", scatter_dimension=0, tiled=True
        ).astype(jnp.float32),
        lax.psum_scatter(
            inward_parts[2].astype(jnp.bfloat16), "row", scatter_dimension=0, tiled=True
        ).astype(jnp.float32),
        lax.psum_scatter(
            inward_parts[3].astype(jnp.bfloat16), "row", scatter_dimension=0, tiled=True
        ).astype(jnp.float32),
        lax.psum_scatter(
            inward_parts[4].astype(jnp.bfloat16), "row", scatter_dimension=0, tiled=True
        ).astype(jnp.float32),
        lax.psum_scatter(
            inward_parts[5].astype(jnp.bfloat16), "row", scatter_dimension=0, tiled=True
        ).astype(jnp.float32),
        lax.psum_scatter(
            core_grads[6].astype(jnp.bfloat16), "row", scatter_dimension=1, tiled=True
        ).astype(jnp.float32),
        lax.psum_scatter(
            core_grads[7].astype(jnp.bfloat16), "row", scatter_dimension=1, tiled=True
        ).astype(jnp.float32),
        lax.psum_scatter(
            core_grads[8].astype(jnp.bfloat16), "row", scatter_dimension=1, tiled=True
        ).astype(jnp.float32),
        lax.psum_scatter(
            grad_wout.astype(jnp.bfloat16), "row", scatter_dimension=1, tiled=True
        ).astype(jnp.float32),
    )
    head_total = a_log.shape[0]
    grad_a_full = lax.dynamic_update_slice_in_dim(
        jnp.zeros((head_total,), jnp.float32), core_grads[9], head_first, 0
    )
    grad_dt_full = lax.dynamic_update_slice_in_dim(
        jnp.zeros((head_total,), jnp.float32), core_grads[10], head_first, 0
    )
    small_sums = lax.psum(
        (grad_gain_in, grad_gain_ffn, core_grads[11], grad_a_full, grad_dt_full), ("head", "row")
    )
    return (
        final_out[None],
        grad_input[None],
        mixer_grads[0],
        mixer_grads[1],
        mixer_grads[2],
        mixer_grads[3],
        mixer_grads[4],
        mixer_grads[5],
        mixer_grads[6],
        mixer_grads[7],
        mixer_grads[8],
        small_sums[3],
        small_sums[4],
        small_sums[2],
        mixer_grads[9],
        small_sums[0],
        small_sums[1],
        ffn_grads[0],
        ffn_grads[1],
        ffn_grads[2],
    )


def solution(mesh):
    return jax.shard_map(
        on_device,
        mesh=mesh,
        in_specs=(
            P("row", "head", None),
            P("row", "head"),
            P("row", "head"),
            P("row", "head"),
            P("row", "head"),
            P("row", "head"),
            P("row", "head"),
            P(None, ("head", "row")),
            P(None, ("head", "row")),
            P(None, ("head", "row")),
            P(),
            P(),
            P(),
            P("head", "row"),
            P(),
            P(),
            P("head", "row"),
            P("head", "row"),
            P("row", "head"),
            P("row", None),
            P("row"),
            P("row", "head", None),
        ),
        out_specs=(
            P("row", "head", None),
            P("row", "head", None),
            P("row", "head"),
            P("row", "head"),
            P("row", "head"),
            P("row", "head"),
            P("row", "head"),
            P("row", "head"),
            P(None, ("head", "row")),
            P(None, ("head", "row")),
            P(None, ("head", "row")),
            P(),
            P(),
            P(),
            P("head", "row"),
            P(),
            P(),
            P("head", "row"),
            P("head", "row"),
            P("row", "head"),
        ),
        check_vma=False,
    )
```

profile of v0, /device:TPU:0, one launch (start us, length us, event | category | flops | bytes accessed | tf_op | source)
XLA Modules:
  0.0 3496.9 jit_solution(107006303143153162)
XLA Ops:
  48.6 24.8 all-gather.22.cloned.1.call-done
  73.4 24.6 all-gather.24.cloned.1.call-done
  109.2 116.3 %all-gather.16.cloned.1.call-done = bf16[2048,2048]{1,0:T(8,128)(2,1)} async-done(((bf16[256,2048]{1,0:T(8,128)(2,1)}), bf16[2048,2048]{1,0:T(8,128)(2,1)}) %all-gather.16.cloned.1.call-update) | async-done | bytes 8388624 | tf_op jit(solution)/shard_map/all_gather | solution.py:231
  225.5 18.2 fusion.203
  290.7 647.6 %while.45 = (s32[]{:T(128)}, f32[2,256,128]{2,1,0:T(8,128)S(1)}, s32[]{:T(128)}, f32[32,2,64,256]{3,2,0,1:T(8,128)}, f32[32,2,256,128]{3,2,1,0:T(8,128)}, /*inde...) while((s32[]{:T(128)}, f32[2,256,128]{2,1,0:T(8,128)S(1)}, ...), condition=%wide.region_5.7_spmd.clone, body=%wide.region_3.6_spmd.clone.sunk | while | flops 227250368 | bytes 3611614 | solution.py:84
  968.3 278.7 %reduce-scatter.28.cloned.1.call-done = f32[256,2048]{1,0:T(8,128)} async-done(((f32[2048,2048]{1,0:T(8,128)}), f32[256,2048]{1,0:T(8,128)}) %reduce-scatter.28.cloned.1.call-update) | async-done | bytes 2097168 | tf_op jit(solution)/shard_map/reduce_scatter | solution.py:255
  1255.6 86.1 %all-gather.30.cloned.1.call-done = bf16[2048,1408]{1,0:T(8,128)(2,1)} async-done(((bf16[256,1408]{1,0:T(8,128)(2,1)}), bf16[2048,1408]{1,0:T(8,128)(2,1)}) %all-gather.30.cloned.1.call-update) | async-done | bytes 5767184 | tf_op jit(solution)/shard_map/all_gather | solution.py:265
  1341.7 34.9 all-gather.28.cloned.1.call-done
  1388.5 83.6 %all-gather.32.cloned.1.call-done = bf16[2048,1408]{1,0:T(8,128)(2,1)} async-done(((bf16[256,1408]{1,0:T(8,128)(2,1)}), bf16[2048,1408]{1,0:T(8,128)(2,1)}) %all-gather.32.cloned.1.call-update) | async-done | bytes 5767184 | tf_op jit(solution)/shard_map/all_gather | solution.py:266
  1483.8 22.7 all-gather.38.cloned.1.call-done
  1506.4 96.3 %all-gather.34.cloned.1.call-done = bf16[1408,2048]{1,0:T(8,128)(2,1)} async-done(((bf16[1408,256]{1,0:T(8,128)(2,1)}), bf16[1408,2048]{1,0:T(8,128)(2,1)}) %all-gather.34.cloned.1.call-update) | async-done | bytes 5767184 | tf_op jit(solution)/shard_map/all_gather | solution.py:267
  1602.7 15.6 multiply_convert_fusion
  1638.7 69.6 %reduce-scatter.32.cloned.1.call-done = f32[256,2048]{1,0:T(8,128)} async-done(((f32[1024,2048]{1,0:T(8,128)}), f32[256,2048]{1,0:T(8,128)}) %reduce-scatter.32.cloned.1.call-update) | async-done | bytes 2097168 | tf_op jit(solution)/shard_map/reduce_scatter | solution.py:292
  1749.5 88.6 %all-gather.36.cloned.1.call-done = bf16[2048,2048]{1,0:T(8,128)(2,1)} async-done(((bf16[256,2048]{1,0:T(8,128)(2,1)}), bf16[2048,2048]{1,0:T(8,128)(2,1)}) %all-gather.36.cloned.1.call-update) | async-done | bytes 8388624 | tf_op jit(solution)/shard_map/all_gather | solution.py:312
  1869.7 1093.1 %while.46 = (s32[]{:T(128)}, f32[2,256,128]{2,1,0:T(8,128)}, f32[32,2,64,128]{3,2,0,1:T(8,128)S(1)}, f32[32,2,64,128]{3,2,0,1:T(8,128)}, f32[32,2,64,256]{3,2,0,...) while((s32[]{:T(128)}, f32[2,256,128]{2,1,0:T(8,128)}, ...), condition=%wide.region_24.26_spmd.clone, body=%wide.region_13.25_spmd.clone.sunk | while | flops 612053184 | bytes 11012455 | solution.py:84
  3032.6 27.8 concatenate.69
  3060.4 17.2 convolution_convert_fusion.4
  3102.0 21.0 convolution_convert_fusion
  3156.7 26.0 reduce-scatter.38.cloned.1.call-done
  3184.6 32.3 reduce-scatter.40.cloned.1.call-done
  3219.1 32.2 reduce-scatter.42.cloned.1.call-done
  3253.5 31.7 reduce-scatter.44.cloned.1.call-done
  3287.4 150.5 %reduce-scatter.34.cloned.1.call-done = bf16[256,2048]{1,0:T(8,128)(2,1)} async-done(((bf16[2048,2048]{1,0:T(8,128)(2,1)}), bf16[256,2048]{1,0:T(8,128)(2,1)}) %reduce-scatter.34.cloned.1.call-update) | async-done | bytes 1048592 | tf_op jit(solution)/shard_map/reduce_scatter | solution.py:321
  3440.2 39.8 %all-reduce.34 = (f32[16]{0:T(128)}, f32[16]{0:T(128)}, f32[256]{0:T(256)}, f32[2048]{0:T(1024)}, f32[2048]{0:T(1024)}) all-reduce(f32[16]{0:T(128)S(1)} %multiply_dynamic-update-slice_fusion, f32[16]{0:T(128)S(1)} %dynamic_update_slice.72, f32[256]{0:T(256)S(1)} %copy-done.103, ...), channel_id=1, replica_groups=mesh['head'=8,'row'=4] {'head','row'}, use_global_device_ids=true, to_apply=%region_51.53 | all-reduce | flops 4384 | bytes 35072 | tf_op jit(solution)/shard_map/psum | solution.py:369
  (3315 shorter events, 2110.1 us)
Async XLA Ops:
  12.0 86.0 %all-gather.24.cloned.1.call-start = ((), (), s32[]{:S(2)}) async-start(), calls=%async_computation.21 | async-start | bytes 2621440 | tf_op jit(solution)/shard_map/all_gather | solution.py:216
  13.0 212.6 %all-gather.16.cloned.1.call-start = ((), (), s32[]{:S(2)}) async-start(), calls=%async_computation.17 | async-start | bytes 9437184 | tf_op jit(solution)/shard_map/all_gather | solution.py:231
  14.7 938.6 %all-gather.26.cloned.1.call-start = ((), (), s32[]{:S(2)}) async-start(), calls=%async_computation.22 | async-start | bytes 2621440 | tf_op jit(solution)/shard_map/all_gather | solution.py:222
  15.6 1231.3 %reduce-scatter.28.cloned.1.call-start = ((), (), s32[]{:S(2)}) async-start(), calls=%async_computation.23 | async-start | bytes 18874368 | tf_op jit(solution)/shard_map/reduce_scatter | solution.py:255
  966.0 375.7 %all-gather.30.cloned.1.call-start = ((), (), s32[]{:S(2)}) async-start(), calls=%async_computation.25 | async-start | bytes 6488064 | tf_op jit(solution)/shard_map/all_gather | solution.py:265
  968.3 408.3 %all-gather.28.cloned.1.call-start = ((), (), s32[]{:S(2)}) async-start(), calls=%async_computation.24 | async-start | bytes 5242880 | tf_op jit(solution)/shard_map/all_gather | solution.py:271
  1252.2 219.9 %all-gather.32.cloned.1.call-start = ((), (), s32[]{:S(2)}) async-start(), calls=%async_computation.26 | async-start | bytes 6488064 | tf_op jit(solution)/shard_map/all_gather | solution.py:266
  1253.2 253.2 %all-gather.38.cloned.1.call-start = ((), (), s32[]{:S(2)}) async-start(), calls=%async_computation.40 | async-start | bytes 5242880 | tf_op jit(solution)/shard_map/all_gather | solution.py:272
  1254.0 348.8 %all-gather.34.cloned.1.call-start = ((), (), s32[]{:S(2)}) async-start(), calls=%async_computation.27 | async-start | bytes 6488064 | tf_op jit(solution)/shard_map/all_gather | solution.py:267
  1255.5 452.8 %reduce-scatter.32.cloned.1.call-start = ((), (), s32[]{:S(2)}) async-start(), calls=%async_computation.29 | async-start | bytes 10485760 | tf_op jit(solution)/shard_map/reduce_scatter | solution.py:292
  1638.2 199.8 %all-gather.36.cloned.1.call-start = ((), (), s32[]{:S(2)}) async-start(), calls=%async_computation.30 | async-start | bytes 9437184 | tf_op jit(solution)/shard_map/all_gather | solution.py:312
  1712.9 1423.1 %reduce-scatter.46.cloned.1.call-start = ((), (), s32[]{:S(2)}) async-start(), calls=%async_computation.37 | async-start | bytes 6488064 | tf_op jit(solution)/shard_map/reduce_scatter | solution.py:301
  1724.0 1414.4 %reduce-scatter.48.cloned.1.call-start = ((), (), s32[]{:S(2)}) async-start(), calls=%async_computation.38 | async-start | bytes 6488064 | tf_op jit(solution)/shard_map/reduce_scatter | solution.py:304
  1736.7 1404.0 %reduce-scatter.50.cloned.1.call-start = ((), (), s32[]{:S(2)}) async-start(), calls=%async_computation.39 | async-start | bytes 6488064 | tf_op jit(solution)/shard_map/reduce_scatter | solution.py:307
  1749.2 1394.1 %reduce-scatter.58.cloned.1.call-start = ((), (), s32[]{:S(2)}) async-start(), calls=%async_computation.44 | async-start | bytes 81920
  3009.6 135.2 %reduce-scatter.56.cloned.1.call-start = ((), (), s32[]{:S(2)}) async-start(), calls=%async_computation.43 | async-start | bytes 81920
  3015.4 130.8 %reduce-scatter.60.cloned.1.call-start = ((), (), s32[]{:S(2)}) async-start(), calls=%async_computation.45 | async-start | bytes 163840
  3032.5 115.1 %reduce-scatter.52.cloned.1.call-start = ((), (), s32[]{:S(2)}) async-start(), calls=%async_computation.41 | async-start | bytes 655360
  3085.7 97.0 %reduce-scatter.38.cloned.1.call-start = ((), (), s32[]{:S(2)}) async-start(), calls=%async_computation.33 | async-start | bytes 1310720 | tf_op jit(solution)/shard_map/reduce_scatter | solution.py:334
  3086.3 130.6 %reduce-scatter.40.cloned.1.call-start = ((), (), s32[]{:S(2)}) async-start(), calls=%async_computation.34 | async-start | bytes 2621440 | tf_op jit(solution)/shard_map/reduce_scatter | solution.py:337
  3091.3 160.0 %reduce-scatter.42.cloned.1.call-start = ((), (), s32[]{:S(2)}) async-start(), calls=%async_computation.35 | async-start | bytes 2621440 | tf_op jit(solution)/shard_map/reduce_scatter | solution.py:340
  3091.9 193.4 %reduce-scatter.44.cloned.1.call-start = ((), (), s32[]{:S(2)}) async-start(), calls=%async_computation.36 | async-start | bytes 2621440 | tf_op jit(solution)/shard_map/reduce_scatter | solution.py:358
  3101.9 336.0 %reduce-scatter.34.cloned.1.call-start = ((), (), s32[]{:S(2)}) async-start(), calls=%async_computation.31 | async-start | bytes 9437184 | tf_op jit(solution)/shard_map/reduce_scatter | solution.py:321
  3123.0 361.8 %reduce-scatter.30.cloned.1.call-start = ((), (), s32[]{:S(2)}) async-start(), calls=%async_computation.28 | async-start | bytes 5242880 | tf_op jit(solution)/shard_map/reduce_scatter | solution.py:278
  (441 other events, 9584.2 us)
Sparse Core Ops, SparseCore 0:
  50.7 22.6 all-gather.21
  75.4 22.5 all-gather.23
  100.6 124.9 all-gather.15
  227.5 20.7 all-gather.25
  966.1 280.8 reduce-scatter.27
  1250.0 91.6 all-gather.29
  1343.9 32.6 all-gather.27
  1379.4 92.6 all-gather.31
  1473.7 32.6 all-gather.37
  1509.1 93.5 all-gather.33
  1638.3 69.9 reduce-scatter.31
  1713.0 124.9 all-gather.35
  1841.5 108.1 reduce-scatter.45
  1953.2 109.7 reduce-scatter.47
  2066.5 110.2 reduce-scatter.49
  3081.5 20.2 reduce-scatter.51
  3104.9 21.6 reduce-scatter.53
  3129.9 24.8 reduce-scatter.35
  3157.8 24.8 reduce-scatter.37
  3185.4 31.4 reduce-scatter.39
  3219.8 31.4 reduce-scatter.41
  3253.8 31.3 reduce-scatter.43
  3288.9 148.9 reduce-scatter.33
  3440.6 44.1 reduce-scatter.29
  (5 shorter events, 93.0 us)
where the time goes:
time: 3520 us; the launch traced here: 3500 us
  waiting for transfers between devices  1210 us (34%)
  other arithmetic  997 us (28%)
  matrix products  794 us (23%)
  local copies, waits for them, and re-layouts  376 us (11%)
  blocking collectives  67.1 us (2%)
    another operation x224, other arithmetic, span_step(): jax.scipy.linalg.solve_triangular(system, right_side, lower=True, unit_di...  680 us
    reduce_scatter x1, waiting for transfers between devices, on_device(): lax.psum_scatter(jnp.dot(mixed_half, out_matrix, preferred_element_type=j...  279 us
    squeeze x224, local copies, waits for them, and re-layouts, delta_rule(): lax.scan(jax.checkpoint(span_step), initial, (blocks(queries), blocks(key...  163 us
    reduce_scatter x1, waiting for transfers between devices, on_device(): lax.psum_scatter(contract_cols(grad_proj, w_inward).astype(jnp.bfloat16),...  151 us
    dot_general x128, matrix products, span_step(): jnp.dot(keys_n, state_mat.T, precision=precise)  130 us
    all_gather x1, waiting for transfers between devices, on_device(): all_rows = lax.all_gather(normed_one, 'head', axis=0, tiled=True)  116 us
    all_gather x1, waiting for transfers between devices, on_device(): lax.all_gather(w_down.astype(jnp.bfloat16), 'head', axis=1, tiled=True)  96.3 us
    dot_general x96, matrix products, span_step(): jnp.dot(update.T, tail_row[:, None] * keys_n, precision=precise)  91.6 us
  transfers between devices with their start and end apart: 29, of which 19 were waited for; matrix products, arithmetic and copies ran while one was open for 60% of the time, Pallas kernels for 0%

commit v1 on v0

v1 whole, which is shorter than its diff:
```python
from functools import partial
import math

import jax
import jax.numpy as jnp
from jax import lax
from jax.sharding import PartitionSpec as P
from jax.experimental import pallas as pl
from jax.experimental.pallas import tpu as pltpu

BLOCK = 64


precise = lax.Precision.HIGHEST
epsilon = 1e-06
o_floor = 0.001


def rms_norm(vector, gain_vec, floor_add=epsilon):
    return (
        vector * lax.rsqrt(jnp.mean(vector * vector, axis=-1, keepdims=True) + floor_add) * gain_vec
    )


def unit_norm(vector):
    return vector * lax.rsqrt(jnp.sum(vector * vector, axis=-1, keepdims=True) + epsilon)


def swiglu(gate_pre, up_pre):
    return jax.nn.silu(gate_pre) * up_pre


def short_conv(signal, kernel, seg_ids):
    tap_count = kernel.shape[0]
    length = signal.shape[0]
    summed = signal * kernel[tap_count - 1]
    for offset in range(1, tap_count):
        shifted = jnp.concatenate(
            [jnp.zeros((offset, signal.shape[1]), signal.dtype), signal[: length - offset]], axis=0
        )
        seg_shift = jnp.concatenate(
            [jnp.full((offset,), -1, jnp.int32), seg_ids[: length - offset]]
        )
        keep_mask = (seg_shift == seg_ids).astype(signal.dtype)
        summed = summed + shifted * kernel[tap_count - 1 - offset] * keep_mask[:, None]
    return summed


def _recur_fwd_kernel(nb, u0_ref, w_ref, kt_ref, c_ref, s_out, u_out, s_scr):
    @pl.when(pl.program_id(1) == 0)
    def _():
        s_scr[...] = jnp.zeros_like(s_scr)

    def step(j, carry):
        state = s_scr[...]
        s_out[0, j] = state
        update = u0_ref[0, j] - lax.dot_general(
            w_ref[0, j], state, (((1,), (1,)), ((), ())),
            precision=precise, preferred_element_type=jnp.float32,
        )
        u_out[0, j] = update
        s_scr[...] = c_ref[0, j] * state + lax.dot_general(
            update, kt_ref[0, j], (((0,), (0,)), ((), ())),
            precision=precise, preferred_element_type=jnp.float32,
        )
        return carry

    lax.fori_loop(0, nb, step, 0)


def _recur_bwd_kernel(
    nb, s_ref, u_ref, w_ref, kt_ref, c_ref, ds_ref, du_ref,
    du0_out, dw_out, dkt_out, dc_out, g_scr,
):
    @pl.when(pl.program_id(1) == 0)
    def _():
        g_scr[...] = jnp.zeros_like(g_scr)

    def step(i, carry):
        j = nb - 1 - i
        grad_state = g_scr[...]
        state = s_ref[0, j]
        grad_update = du_ref[0, j] + lax.dot_general(
            kt_ref[0, j], grad_state, (((1,), (1,)), ((), ())),
            precision=precise, preferred_element_type=jnp.float32,
        )
        dkt_out[0, j] = jnp.dot(
            u_ref[0, j], grad_state, precision=precise, preferred_element_type=jnp.float32
        )
        dc_out[0, j] = jnp.sum(grad_state * state, axis=0, keepdims=True)
        du0_out[0, j] = grad_update
        dw_out[0, j] = -jnp.dot(
            grad_update, state, precision=precise, preferred_element_type=jnp.float32
        )
        g_scr[...] = (
            c_ref[0, j] * grad_state
            - lax.dot_general(
                grad_update, w_ref[0, j], (((0,), (0,)), ((), ())),
                precision=precise, preferred_element_type=jnp.float32,
            )
            + ds_ref[0, j]
        )
        return carry

    lax.fori_loop(0, nb, step, 0)


def _chunk_spec(nb, tail, reverse, count):
    if reverse:
        return pl.BlockSpec((1, nb) + tail, lambda h, b: (h, count - 1 - b, 0, 0))
    return pl.BlockSpec((1, nb) + tail, lambda h, b: (h, b, 0, 0))


def _recur_forward(u0, w, kt, c):
    heads, count, chunk, dv = u0.shape
    dk = w.shape[-1]
    nb = min(8, count)
    blocks = count // nb
    flops = 4 * heads * count * chunk * dk * dv * 6
    moved = 4 * heads * count * (2 * chunk * dv + 2 * chunk * dk + dv * dk)
    return pl.pallas_call(
        partial(_recur_fwd_kernel, nb),
        grid=(heads, blocks),
        in_specs=[
            _chunk_spec(nb, (chunk, dv), False, blocks),
            _chunk_spec(nb, (chunk, dk), False, blocks),
            _chunk_spec(nb, (chunk, dk), False, blocks),
            _chunk_spec(nb, (1, dk), False, blocks),
        ],
        out_specs=[
            _chunk_spec(nb, (dv, dk), False, blocks),
            _chunk_spec(nb, (chunk, dv), False, blocks),
        ],
        out_shape=[
            jax.ShapeDtypeStruct((heads, count, dv, dk), jnp.float32),
            jax.ShapeDtypeStruct((heads, count, chunk, dv), jnp.float32),
        ],
        scratch_shapes=[pltpu.VMEM((dv, dk), jnp.float32)],
        compiler_params=pltpu.CompilerParams(dimension_semantics=("arbitrary", "arbitrary")),
        cost_estimate=pl.CostEstimate(flops=flops, transcendentals=0, bytes_accessed=moved),
        name="delta_state_forward",
    )(u0, w, kt, c)


def _recur_backward(states, updates, w, kt, c, d_states, d_updates):
    heads, count, chunk, dv = updates.shape
    dk = w.shape[-1]
    nb = min(8, count)
    blocks = count // nb
    flops = 8 * heads * count * chunk * dk * dv * 6
    moved = 4 * heads * count * (4 * chunk * dv + 4 * chunk * dk + 2 * dv * dk)
    return pl.pallas_call(
        partial(_recur_bwd_kernel, nb),
        grid=(heads, blocks),
        in_specs=[
            _chunk_spec(nb, (dv, dk), True, blocks),
            _chunk_spec(nb, (chunk, dv), True, blocks),
            _chunk_spec(nb, (chunk, dk), True, blocks),
            _chunk_spec(nb, (chunk, dk), True, blocks),
            _chunk_spec(nb, (1, dk), True, blocks),
            _chunk_spec(nb, (dv, dk), True, blocks),
            _chunk_spec(nb, (chunk, dv), True, blocks),
        ],
        out_specs=[
            _chunk_spec(nb, (chunk, dv), True, blocks),
            _chunk_spec(nb, (chunk, dk), True, blocks),
            _chunk_spec(nb, (chunk, dk), True, blocks),
            _chunk_spec(nb, (1, dk), True, blocks),
        ],
        out_shape=[
            jax.ShapeDtypeStruct((heads, count, chunk, dv), jnp.float32),
            jax.ShapeDtypeStruct((heads, count, chunk, dk), jnp.float32),
            jax.ShapeDtypeStruct((heads, count, chunk, dk), jnp.float32),
            jax.ShapeDtypeStruct((heads, count, 1, dk), jnp.float32),
        ],
        scratch_shapes=[pltpu.VMEM((dv, dk), jnp.float32)],
        compiler_params=pltpu.CompilerParams(dimension_semantics=("arbitrary", "arbitrary")),
        cost_estimate=pl.CostEstimate(flops=flops, transcendentals=0, bytes_accessed=moved),
        name="delta_state_backward",
    )(states, updates, w, kt, c, d_states, d_updates)


@jax.custom_vjp
def state_recurrence(u0, w, kt, c):
    return _recur_forward(u0, w, kt, c)


def _recurrence_fwd(u0, w, kt, c):
    states, updates = _recur_forward(u0, w, kt, c)
    return (states, updates), (states, updates, w, kt, c)


def _recurrence_bwd(saved, grads):
    states, updates, w, kt, c = saved
    d_states, d_updates = grads
    du0, dw, dkt, dc_lanes = _recur_backward(states, updates, w, kt, c, d_states, d_updates)
    return du0, dw, dkt, dc_lanes


state_recurrence.defvjp(_recurrence_fwd, _recurrence_bwd)


def chunk_prepare(queries, keys_n, values, decays, beta_rate, seg_ids):
    length, dk = keys_n.shape
    count = length // BLOCK
    q = queries.reshape(count, BLOCK, dk)
    k = keys_n.reshape(count, BLOCK, dk)
    v = values.reshape(count, BLOCK, values.shape[1])
    beta = beta_rate.reshape(count, BLOCK)
    seg = seg_ids.reshape(count, BLOCK)
    cumulative = jnp.cumsum(decays.reshape(count, BLOCK), axis=1)
    places = jnp.arange(BLOCK)
    lower_tri = places[:, None] >= places[None, :]
    inside = jnp.logical_and(seg[:, :, None] == seg[:, None, :], lower_tri)
    log_gap = jnp.where(inside, cumulative[:, :, None] - cumulative[:, None, :], 0.0)
    within = jnp.exp(log_gap) * inside.astype(jnp.float32)
    strict = within * (places[:, None] > places[None, :]).astype(jnp.float32)
    last_seg = jnp.concatenate([jnp.full((1,), -1, seg.dtype), seg[:-1, BLOCK - 1]])
    carried = jnp.exp(cumulative) * (seg == last_seg[:, None]).astype(jnp.float32)
    key_gram = jnp.einsum("nid,njd->nij", k, k, precision=precise)
    system = jnp.eye(BLOCK, dtype=jnp.float32) + beta[:, :, None] * strict * key_gram
    right_side = jnp.concatenate([beta[:, :, None] * v, (beta * carried)[:, :, None] * k], axis=2)
    solved = lax.linalg.triangular_solve(
        system, right_side, left_side=True, lower=True, unit_diagonal=True
    )
    dv = v.shape[2]
    kt = within[:, BLOCK - 1, :, None] * k
    scores = jnp.einsum("nid,njd->nij", q, k, precision=precise) * within
    return solved[:, :, :dv], solved[:, :, dv:], kt, carried[:, BLOCK - 1], carried, scores


def chunk_finish(queries, carried, scores, states, updates):
    count = states.shape[0]
    q = queries.reshape(count, BLOCK, queries.shape[1])
    output = carried[:, :, None] * jnp.einsum(
        "nid,nvd->niv", q, states, precision=precise
    ) + jnp.einsum("nij,njv->niv", scores, updates, precision=precise)
    return output.reshape(count * BLOCK, states.shape[1])


def delta_rule(queries, keys_n, values, decays, beta_rate, seg_ids):
    u0, w, kt, tail, carried, scores = jax.vmap(chunk_prepare, in_axes=(0, 0, 0, 0, 0, None))(
        queries, keys_n, values, decays, beta_rate, seg_ids
    )
    c = jnp.broadcast_to(tail[:, :, None, None], tail.shape + (1, w.shape[-1]))
    states, updates = state_recurrence(u0, w, kt, c)
    return jax.vmap(chunk_finish)(queries, carried, scores, states, updates)


def head_inputs(proj_query, proj_key, proj_value, proj_alpha, proj_beta,
                kernel_query, kernel_key, kernel_value, a_here, dt_here, seg_ids):
    queries = unit_norm(jax.nn.silu(short_conv(proj_query, kernel_query, seg_ids))) * (
        1.0 / math.sqrt(proj_query.shape[1])
    )
    keys_n = unit_norm(jax.nn.silu(short_conv(proj_key, kernel_key, seg_ids)))
    values = jax.nn.silu(short_conv(proj_value, kernel_value, seg_ids))
    decays = -jnp.exp(a_here) * jax.nn.softplus(proj_alpha + dt_here)
    beta_rate = jax.nn.sigmoid(proj_beta)
    return queries, keys_n, values, decays, beta_rate


def head_output(recurrent, proj_gate, o_gain, live_mask):
    return rms_norm(recurrent, o_gain, o_floor) * jax.nn.silu(proj_gate) * live_mask[:, None]


def local_mixer(
    proj_query,
    proj_key,
    proj_value,
    proj_gate,
    proj_alpha,
    proj_beta,
    kernel_query,
    kernel_key,
    kernel_value,
    a_here,
    dt_here,
    o_gain,
    seg_ids=None,
    live_mask=None,
):
    row_count = proj_query.shape[0]
    heads_here = proj_alpha.shape[1]

    def by_head(array):
        return jnp.moveaxis(array.reshape(row_count, heads_here, -1), 1, 0)

    def kernel_heads(kernel):
        return jnp.moveaxis(kernel.reshape(kernel.shape[0], heads_here, -1), 1, 0)

    queries, keys_n, values, decays, beta_rate = jax.vmap(
        head_inputs, in_axes=(0,) * 10 + (None,)
    )(
        by_head(proj_query),
        by_head(proj_key),
        by_head(proj_value),
        proj_alpha.T,
        proj_beta.T,
        kernel_heads(kernel_query),
        kernel_heads(kernel_key),
        kernel_heads(kernel_value),
        a_here,
        dt_here,
        seg_ids,
    )
    recurrent = delta_rule(queries, keys_n, values, decays, beta_rate, seg_ids)
    mixed_heads = jax.vmap(head_output, in_axes=(0, 0, None, None))(
        recurrent, by_head(proj_gate), o_gain, live_mask
    )
    return jnp.moveaxis(mixed_heads, 0, 1).reshape(row_count, -1)


def contract_rows(left, right):
    return lax.dot_general(
        left, right, (((0,), (0,)), ((), ())), preferred_element_type=jnp.float32
    )


def contract_cols(left, right):
    return lax.dot_general(
        left, right, (((1,), (1,)), ((), ())), preferred_element_type=jnp.float32
    )


def on_device(
    tokens,
    w_query,
    w_key,
    w_value,
    w_outgate,
    w_alpha,
    w_beta,
    conv_query,
    conv_key,
    conv_value,
    a_log,
    dt_bias,
    o_gain,
    w_out,
    gain_in,
    gain_ffn,
    w_gate,
    w_up,
    w_down,
    segments,
    valid_len,
    cotangent,
):
    residual = tokens[0].astype(jnp.float32)
    heads_here = w_alpha.shape[1]
    head_first = lax.axis_index("head") * heads_here
    norm_one, pull_one = jax.vjp(rms_norm, residual, gain_in)
    normed_one = norm_one.astype(jnp.bfloat16)
    row_count = lax.psum(1, "row")
    w_local = jnp.concatenate(
        [w_query, w_key, w_value, w_outgate, w_alpha, w_beta], axis=1
    ).astype(jnp.bfloat16)
    edges = [0]
    for member in (w_query, w_key, w_value, w_outgate, w_alpha, w_beta):
        edges.append(edges[-1] + member.shape[1])
    w_inward = lax.all_gather(w_local, "row", axis=0, tiled=True)
    conv_local = jnp.concatenate([conv_query, conv_key, conv_value], axis=1).astype(jnp.bfloat16)
    conv_edges = [0, conv_query.shape[1], conv_query.shape[1] + conv_key.shape[1], conv_local.shape[1]]
    conv_all = lax.all_gather(conv_local, "row", axis=1, tiled=True).reshape(
        conv_local.shape[0], row_count, conv_local.shape[1]
    )
    conv_parts = [
        conv_all[:, :, conv_edges[i] : conv_edges[i + 1]].reshape(conv_local.shape[0], -1)
        for i in range(3)
    ]
    out_matrix = lax.all_gather(w_out.astype(jnp.bfloat16), "row", axis=1, tiled=True)
    ff_width = w_gate.shape[1]
    ffn_local = jnp.concatenate([w_gate, w_up, w_down.T], axis=1).astype(jnp.bfloat16)
    ffn_all = lax.all_gather(ffn_local, "head", axis=0, tiled=True)
    grad_out = cotangent[0]
    grad_out_rows = lax.all_gather(grad_out, "row", axis=0, tiled=True)
    all_rows = lax.all_gather(normed_one, "head", axis=0, tiled=True)
    projected = jnp.dot(all_rows, w_inward, preferred_element_type=jnp.float32)
    proj_parts = [projected[:, edges[spot] : edges[spot + 1]] for spot in range(6)]
    seg_ids = segments[0]
    live_mask = (jnp.arange(seg_ids.shape[0]) < valid_len[0]).astype(jnp.float32)
    a_here = lax.dynamic_slice_in_dim(a_log, head_first, heads_here)
    dt_here = lax.dynamic_slice_in_dim(dt_bias, head_first, heads_here)
    mixer_fn = partial(local_mixer, seg_ids=seg_ids, live_mask=live_mask)
    mixed, pull_core = jax.vjp(
        mixer_fn,
        proj_parts[0],
        proj_parts[1],
        proj_parts[2],
        proj_parts[3],
        proj_parts[4],
        proj_parts[5],
        conv_parts[0].astype(jnp.float32),
        conv_parts[1].astype(jnp.float32),
        conv_parts[2].astype(jnp.float32),
        a_here,
        dt_here,
        o_gain,
    )
    mixed, ffn_all, grad_out_rows = lax.optimization_barrier((mixed, ffn_all, grad_out_rows))
    w_gate_all = ffn_all[:, :ff_width]
    w_up_all = ffn_all[:, ff_width : 2 * ff_width]
    w_down_t = ffn_all[:, 2 * ff_width :]
    mixed_half = mixed.astype(jnp.bfloat16)
    mixer_output = lax.psum_scatter(
        jnp.dot(mixed_half, out_matrix, preferred_element_type=jnp.float32).astype(jnp.bfloat16),
        "head",
        scatter_dimension=0,
        tiled=True,
    ).astype(jnp.float32)
    middle = residual + mixer_output
    norm_two, pull_two = jax.vjp(rms_norm, middle, gain_ffn)
    normed_two = norm_two.astype(jnp.bfloat16)
    ffn_inputs = lax.all_gather(normed_two, "row", axis=0, tiled=True)
    gate_pre = jnp.dot(ffn_inputs, w_gate_all, preferred_element_type=jnp.float32)
    up_pre = jnp.dot(ffn_inputs, w_up_all, preferred_element_type=jnp.float32)
    hidden_val, pull_act = jax.vjp(swiglu, gate_pre, up_pre)
    hidden_half = hidden_val.astype(jnp.bfloat16)
    ffn_partial = contract_cols(hidden_half, w_down_t).astype(jnp.bfloat16)
    grad_hidden = jnp.dot(grad_out_rows, w_down_t, preferred_element_type=jnp.float32)
    grad_down_t = contract_rows(grad_out_rows, hidden_half)
    grad_gate_f, grad_up_f = pull_act(grad_hidden)
    grad_gate = grad_gate_f.astype(jnp.bfloat16)
    grad_upper = grad_up_f.astype(jnp.bfloat16)
    grad_wgate = contract_rows(ffn_inputs, grad_gate)
    grad_wup = contract_rows(ffn_inputs, grad_upper)
    grad_norm_two = lax.psum_scatter(
        (contract_cols(grad_gate, w_gate_all) + contract_cols(grad_upper, w_up_all)).astype(
            jnp.bfloat16
        ),
        "row",
        scatter_dimension=0,
        tiled=True,
    ).astype(jnp.float32)
    grad_mid_part, grad_gain_ffn = pull_two(grad_norm_two)
    grad_middle = grad_out.astype(jnp.float32) + grad_mid_part
    ffn_grad_cat = jnp.concatenate([grad_wgate, grad_wup, grad_down_t], axis=1).astype(
        jnp.bfloat16
    )
    grad_mid_half = grad_middle.astype(jnp.bfloat16)
    grad_mid_rows = lax.all_gather(grad_mid_half, "head", axis=0, tiled=True)
    grad_mid_rows, ffn_partial, ffn_grad_cat = lax.optimization_barrier(
        (grad_mid_rows, ffn_partial, ffn_grad_cat)
    )
    ffn_output = lax.psum_scatter(ffn_partial, "row", scatter_dimension=0, tiled=True)
    ffn_grad_all = lax.psum_scatter(ffn_grad_cat, "head", scatter_dimension=0, tiled=True)
    grad_mixed = contract_cols(grad_mid_rows, out_matrix)
    grad_wout = contract_rows(mixed_half, grad_mid_rows)
    wout_grad = lax.psum_scatter(
        grad_wout.astype(jnp.bfloat16), "row", scatter_dimension=1, tiled=True
    )
    core_grads = pull_core(grad_mixed)
    core_grads, ffn_output, ffn_grad_all, wout_grad = lax.optimization_barrier(
        (core_grads, ffn_output, ffn_grad_all, wout_grad)
    )
    final_out = (middle + ffn_output.astype(jnp.float32)).astype(jnp.bfloat16)
    ffn_grad_all = ffn_grad_all.astype(jnp.float32)
    ffn_grads = (
        ffn_grad_all[:, :ff_width],
        ffn_grad_all[:, ff_width : 2 * ff_width],
        ffn_grad_all[:, 2 * ff_width :].T,
    )
    grad_proj = jnp.concatenate(
        [core_grads[0], core_grads[1], core_grads[2], core_grads[3], core_grads[4], core_grads[5]],
        axis=1,
    ).astype(jnp.bfloat16)
    grad_inward = contract_rows(all_rows, grad_proj).astype(jnp.bfloat16)
    grad_norm_one = lax.psum_scatter(
        contract_cols(grad_proj, w_inward).astype(jnp.bfloat16),
        "head",
        scatter_dimension=0,
        tiled=True,
    )
    grad_norm_one, grad_inward = lax.optimization_barrier((grad_norm_one, grad_inward))
    grad_norm_one = grad_norm_one.astype(jnp.float32)
    grad_in_part, grad_gain_in = pull_one(grad_norm_one)
    grad_input = grad_middle + grad_in_part
    inward_all = lax.psum_scatter(
        grad_inward, "row", scatter_dimension=0, tiled=True
    ).astype(jnp.float32)
    conv_grad_local = jnp.concatenate(
        [
            core_grads[6 + i].reshape(conv_local.shape[0], row_count, -1)
            for i in range(3)
        ],
        axis=2,
    ).reshape(conv_local.shape[0], -1)
    conv_grad = lax.psum_scatter(
        conv_grad_local.astype(jnp.bfloat16), "row", scatter_dimension=1, tiled=True
    ).astype(jnp.float32)
    mixer_grads = tuple(inward_all[:, edges[spot] : edges[spot + 1]] for spot in range(6)) + tuple(
        conv_grad[:, conv_edges[i] : conv_edges[i + 1]] for i in range(3)
    ) + (wout_grad.astype(jnp.float32),)
    head_total = a_log.shape[0]
    grad_a_full = lax.dynamic_update_slice_in_dim(
        jnp.zeros((head_total,), jnp.float32), core_grads[9], head_first, 0
    )
    grad_dt_full = lax.dynamic_update_slice_in_dim(
        jnp.zeros((head_total,), jnp.float32), core_grads[10], head_first, 0
    )
    small_sums = lax.psum(
        (grad_gain_in, grad_gain_ffn, core_grads[11], grad_a_full, grad_dt_full), ("head", "row")
    )
    return (
        final_out[None],
        grad_input[None],
        mixer_grads[0],
        mixer_grads[1],
        mixer_grads[2],
        mixer_grads[3],
        mixer_grads[4],
        mixer_grads[5],
        mixer_grads[6],
        mixer_grads[7],
        mixer_grads[8],
        small_sums[3],
        small_sums[4],
        small_sums[2],
        mixer_grads[9],
        small_sums[0],
        small_sums[1],
        ffn_grads[0],
        ffn_grads[1],
        ffn_grads[2],
    )


def solution(mesh):
    return jax.shard_map(
        on_device,
        mesh=mesh,
        in_specs=(
            P("row", "head", None),
            P("row", "head"),
            P("row", "head"),
            P("row", "head"),
            P("row", "head"),
            P("row", "head"),
            P("row", "head"),
            P(None, ("head", "row")),
            P(None, ("head", "row")),
            P(None, ("head", "row")),
            P(),
            P(),
            P(),
            P("head", "row"),
            P(),
            P(),
            P("head", "row"),
            P("head", "row"),
            P("row", "head"),
            P("row", None),
            P("row"),
            P("row", "head", None),
        ),
        out_specs=(
            P("row", "head", None),
            P("row", "head", None),
            P("row", "head"),
            P("row", "head"),
            P("row", "head"),
            P("row", "head"),
            P("row", "head"),
            P("row", "head"),
            P(None, ("head", "row")),
            P(None, ("head", "row")),
            P(None, ("head", "row")),
            P(),
            P(),
            P(),
            P("head", "row"),
            P(),
            P(),
            P("head", "row"),
            P("head", "row"),
            P("row", "head"),
        ),
        check_vma=False,
    )
```

time: 3520 us -> 1690 us (0.48)
  other arithmetic: 997 us -> 294 us
  matrix products: 794 us -> 294 us
  waiting for transfers between devices: 1210 us -> 776 us
  local copies, waits for them, and re-layouts: 376 us -> 157 us
  Pallas kernels: 0 us -> 95.6 us
    another operation x384 -> x15, other arithmetic: 742 us -> 140 us  [the longest x4 135 us: chunk_prepare(): lax.linalg.triangular_solve(system, right_side, left_side=True, lower=Tru...]
    dot_general x739 -> x16, matrix products: 577 us -> 137 us  [the longest x3 38.3 us: chunk_finish(): jnp.einsum('nid,nvd->niv', q, states, precision=precise)]
    all_gather x9 -> x4, waiting for transfers between devices: 375 us -> 76.7 us  [the longest x1 27.6 us: on_device(): w_inward = lax.all_gather(w_local, 'row', axis=0, tiled=True)]
    squeeze x224 -> x1, local copies, waits for them, and re-layouts: 163 us -> 0.01 us  [chunk_prepare(): seg[:-1, BLOCK - 1]]
    reduce_scatter x1, waiting for transfers between devices: 279 us -> 149 us  [on_device(): lax.psum_scatter(jnp.dot(mixed_half, out_matrix, preferred_element_type=j...]
    pallas_call x0 -> x2, Pallas kernels: none -> 95.6 us  [the longest x1 49.5 us: _recur_forward(): pl.pallas_call(partial(_recur_fwd_kernel, nb), grid=(heads, blocks), in_s...]
    convert_element_type x88 -> x6, other arithmetic: 66.4 us -> 4.2 us  [the longest x1 2.39 us: on_device(): ffn_grad_all = ffn_grad_all.astype(jnp.float32)]
    another operation x128 -> x3, matrix products: 61.8 us -> 19.3 us  [chunk_prepare(): lax.linalg.triangular_solve(system, right_side, left_side=True, lower=Tru...]
  transfers between devices with their start and end apart: 29 -> 15, of which waited for: 19 -> 12; matrix products, arithmetic and copies ran while one was open for 60% -> 35% of each run, Pallas kernels for 0% -> 6%
where the time goes in v1:
time: 1690 us; the launch traced here: 1680 us
  waiting for transfers between devices  776 us (46%)
  other arithmetic  294 us (17%)
  matrix products  294 us (17%)
  local copies, waits for them, and re-layouts  157 us (9%)
  Pallas kernels  95.6 us (6%)
  blocking collectives  46.4 us (3%)
  between operations  16.9 us (1%)
    reduce_scatter x1, waiting for transfers between devices, on_device(): lax.psum_scatter(jnp.dot(mixed_half, out_matrix, preferred_element_type=j...  149 us
    another operation x4, other arithmetic, chunk_prepare(): lax.linalg.triangular_solve(system, right_side, left_side=True, lower=Tru...  135 us
    all_gather x1, waiting for transfers between devices, on_device(): all_rows = lax.all_gather(normed_one, 'head', axis=0, tiled=True)  128 us
    reduce_scatter x1, waiting for transfers between devices, on_device(): lax.psum_scatter(contract_cols(grad_proj, w_inward).astype(jnp.bfloat16),...  128 us
    reduce_scatter x1, waiting for transfers between devices, on_device(): lax.psum_scatter(ffn_grad_cat, 'head', scatter_dimension=0, tiled=True)  119 us
    all_gather x1, waiting for transfers between devices, on_device(): grad_mid_rows = lax.all_gather(grad_mid_half, 'head', axis=0, tiled=True)  84 us
    dot_general x5, matrix products, contract_cols(): lax.dot_general(left, right, (((1,), (1,)), ((), ())), preferred_element_...  60.4 us
    dot_general x5, matrix products, contract_rows(): lax.dot_general(left, right, (((0,), (0,)), ((), ())), preferred_element_...  50.9 us
  transfers between devices with their start and end apart: 15, of which 12 were waited for; matrix products, arithmetic and copies ran while one was open for 35% of the time, Pallas kernels for 6%

profile of v1, /device:TPU:0, one launch (start us, length us, event | category | flops | bytes accessed | tf_op | source)
XLA Modules:
  0.0 1681.1 jit_solution(17279676055298017043)
XLA Ops:
  38.0 27.6 %all-gather.11.cloned.1.call-done = bf16[2048,1540]{1,0:T(8,128)(2,1)} async-done(((bf16[512,1540]{1,0:T(8,128)(2,1)}), bf16[2048,1540]{1,0:T(8,128)(2,1)}) %all-gather.11.cloned.1.call-update) | async-done | bytes 6307856 | tf_op jit(solution)/shard_map/all_gather | solution.py:361
  65.5 127.7 %all-gather.9.cloned.1.call-done = bf16[2048,2048]{1,0:T(8,128)(2,1)} async-done(((bf16[256,2048]{1,0:T(8,128)(2,1)}), bf16[2048,2048]{1,0:T(8,128)(2,1)}) %all-gather.9.cloned.1.call-update) | async-done | bytes 8388624 | tf_op jit(solution)/shard_map/all_gather | solution.py:377
  193.2 18.2 %fusion.107 = f32[2048,1540]{0,1:T(8,128)S(1)} fusion(bf16[2048,2048]{1,0:T(8,128)(2,1)} %all-gather.9.cloned.1.call-done, bf16[2048,1540]{1,0:T(8,128)(2,1)} %all-gather.11.cloned.1.call-done), kind=kOutput, calls=%fused_computation.271 | convolution fusion | flops 12918456320 | bytes 27312128 | tf_op jit(solution)/shard_map/dot_general | solution.py:378
  297.7 134.0 %custom-call.7 = f32[2,32,1,64,64]{1,3,4,2,0:T(8,128)} custom-call(f32[2,32,1,64,64]{1,4,3,2,0:T(8,128)} %get-tuple-element.227), custom_call_target="InvertDiagBlocksLowerTriangular" | custom-call | tf_op jit(solution)/shard_map/jvp(vmap())/triangular_solve | solution.py:223
  456.5 49.5 %jvp_delta_state_forward_.1 = (f32[2,32,256,128]{3,2,1,0:T(8,128)}, f32[2,32,64,256]{3,2,1,0:T(8,128)}) custom-call(f32[2,32,64,256]{3,2,1,0:T(8,128)} %slice.269.u0_ref, f32[2,32,64,128]{3,2,1,0:T(8,128)} %slice.270.w_ref, f32[2,32,64,128]{3,2,1,0:T(8,128)} %get-tuple-element.199.kt_ref, f32[2,32,1,128]{3,2,1,0:T(1,128)} %broadcast_in_dim.34.c_ref), custom_call_target="tpu_custom_call" | custom-call | flops 3221225472 | bytes 20971520 | tf_op jit(solution)/shard_map/jvp(delta_state_forward)/pallas_call | solution.py:121
  535.9 27.2 %all-gather.13.cloned.1.call-done = bf16[2048,4224]{0,1:T(8,128)(2,1)} async-done(((bf16[256,4224]{0,1:T(8,128)(2,1)}), bf16[2048,4224]{0,1:T(8,128)(2,1)}) %all-gather.13.cloned.1.call-update) | async-done | bytes 17301520 | tf_op jit(solution)/shard_map/all_gather | solution.py:374
  563.1 24.7 %all-gather.15.cloned.1.call-done = bf16[512,2048]{1,0:T(8,128)(2,1)} async-done(((bf16[512,512]{1,0:T(8,128)(2,1)}), bf16[512,2048]{1,0:T(8,128)(2,1)}) %all-gather.15.cloned.1.call-update) | async-done | bytes 2097168 | tf_op jit(solution)/shard_map/all_gather | solution.py:371
  596.3 149.1 %reduce-scatter.11.cloned.1.call-done = bf16[256,2048]{1,0:T(8,128)(2,1)} async-done(((bf16[2048,2048]{1,0:T(8,128)(2,1)}), bf16[256,2048]{1,0:T(8,128)(2,1)}) %reduce-scatter.11.cloned.1.call-update) | async-done | bytes 1048592 | tf_op jit(solution)/shard_map/reduce_scatter | solution.py:405
  749.7 11.8 fusion.20
  761.5 21.8 %all-gather.17.cloned.1.call-done = bf16[1024,2048]{1,0:T(8,128)(2,1)} async-done(((bf16[256,2048]{1,0:T(8,128)(2,1)}), bf16[1024,2048]{1,0:T(8,128)(2,1)}) %all-gather.17.cloned.1.call-update) | async-done | bytes 4194320 | tf_op jit(solution)/shard_map/all_gather | solution.py:414
  783.3 11.9 fusion.12
  795.2 14.4 multiply_convert_fusion
  830.7 44.6 %reduce-scatter.13.cloned.1.call-done = bf16[256,2048]{1,0:T(8,128)(2,1)} async-done(((bf16[1024,2048]{1,0:T(8,128)(2,1)}), bf16[256,2048]{1,0:T(8,128)(2,1)}) %reduce-scatter.13.cloned.1.call-update) | async-done | bytes 1048592 | tf_op jit(solution)/shard_map/reduce_scatter | solution.py:427
  921.8 84.0 %all-gather.19.cloned.1.call-done = bf16[2048,2048]{1,0:T(8,128)(2,1)} async-done(((bf16[256,2048]{1,0:T(8,128)(2,1)}), bf16[2048,2048]{1,0:T(8,128)(2,1)}) %all-gather.19.cloned.1.call-update) | async-done | bytes 8388624 | tf_op jit(solution)/shard_map/all_gather | solution.py:441
  1048.8 17.5 %fusion.29.ds_ref = f32[2,32,256,128]{3,2,1,0:T(8,128)} fusion(f32[2,32,64,128]{3,2,1,0:T(8,128)S(1)} %bitcast.292, f32[2,32,64,256]{3,2,1,0:T(8,128)S(1)} %bitcast.287, f32[2,32,64]{2,1,0:T(8,128)S(1)} %copy-done.58), kind=kOutput, calls=%fused_computation.76 | convolution fusion | flops 1611661312 | bytes 14696448 | tf_op jit(solution)/shard_map/transpose(jvp(vmap(nid,nvd->niv)))/dot_general | solution.py:235
  1066.3 46.2 %transpose_jvp_delta_state_backward__.1 = (f32[2,32,64,256]{3,2,1,0:T(8,128)}, f32[2,32,64,128]{3,2,1,0:T(8,128)}, f32[2,32,64,128]{3,2,1,0:T(8,128)}, f32[2,32,1,128]{3,2,1,0:T(1,128)}) custom-call(f32[2,32,256,128]{3,2,1,0:T(8,128)} %get-tuple-element.49.s_ref, f32[2,32,64,256]{3,2,1,0:T(8,128)} %get-tuple-element.50.u_ref, ...), custom_call_target="tpu_custom_call" | custom-call | flops 6442450944 | bytes 41943040 | tf_op jit(solution)/shard_map/transpose(jvp(delta_state_backward))/pallas_call | solution.py:246
  1154.9 12.3 multiply_reduce_fusion.5
  1270.3 118.6 %reduce-scatter.17.cloned.1.call-done = bf16[256,4224]{0,1:T(8,128)(2,1)} async-done(((bf16[2048,4224]{0,1:T(8,128)(2,1)}), bf16[256,4224]{0,1:T(8,128)(2,1)}) %reduce-scatter.17.cloned.1.call-update) | async-done | bytes 2162704 | tf_op jit(solution)/shard_map/reduce_scatter | solution.py:446
  1388.9 23.4 %concatenate.97 = bf16[2048,1540]{0,1:T(8,128)(2,1)} concatenate(bf16[2048,256]{0,1:T(8,128)(2,1)S(1)} %bitcast.304, bf16[2048,256]{0,1:T(8,128)(2,1)} %bitcast.305, bf16[2048,512]{0,1:T(8,128)(2,1)S(1)} %bitcast.300, bf16[2048,512]{0,1:T(8,128)(2,1)} %bitcast.303, bf16[2048,2]{0,1:T(2,128)(2,1)S(1)} %bitcast.315, bf16[2048,2]{0,1:T(2,128)(2,1)S(1)} %fusion.72), dimensions={1} | concatenate | bytes 12615680 | tf_op jit(solution)/shard_map/concatenate | solution.py:463
  1412.3 21.0 %convolution_convert_fusion = bf16[2048,2048]{1,0:T(8,128)(2,1)} fusion(bf16[2048,1540]{0,1:T(8,128)(2,1)} %concatenate.97, bf16[2048,1540]{1,0:T(8,128)(2,1)} %all-gather.11.cloned.1.call-done), kind=kOutput, calls=%fused_computation.3 | convolution fusion | flops 12922650624 | bytes 21004288 | tf_op jit(solution)/shard_map/dot_general | solution.py:320
  1434.7 19.4 %convolution_convert_fusion.5 = bf16[2048,1540]{0,1:T(8,128)(2,1)} fusion(bf16[2048,2048]{1,0:T(8,128)(2,1)} %all-gather.9.cloned.1.call-done, bf16[2048,1540]{0,1:T(8,128)(2,1)} %concatenate.97), kind=kOutput, calls=%fused_computation.8 | convolution fusion | flops 12921610240 | bytes 21004288 | tf_op jit(solution)/shard_map/dot_general | solution.py:314
  1454.1 127.5 %reduce-scatter.21.cloned.1.call-done = bf16[256,2048]{1,0:T(8,128)(2,1)} async-done(((bf16[2048,2048]{1,0:T(8,128)(2,1)}), bf16[256,2048]{1,0:T(8,128)(2,1)}) %reduce-scatter.21.cloned.1.call-update) | async-done | bytes 1048592 | tf_op jit(solution)/shard_map/reduce_scatter | solution.py:468
  1608.1 40.0 %all-reduce.36 = (f32[16]{0:T(128)}, f32[16]{0:T(128)}, f32[256]{0:T(256)}, f32[2048]{0:T(1024)}, f32[2048]{0:T(1024)}) all-reduce(f32[16]{0:T(128)S(1)} %dynamic_update_slice.6, f32[16]{0:T(128)S(1)} %dynamic_update_slice.7, f32[256]{0:T(256)S(1)} %copy-done.132, ...), channel_id=1, replica_groups=mesh['head'=8,'row'=4] {'head','row'}, use_global_device_ids=true, to_apply=%region_43.44 | all-reduce | flops 4384 | bytes 35072 | tf_op jit(solution)/shard_map/psum | solution.py:501
  1653.3 12.2 reduce-scatter.23.cloned.1.call-done
  (544 shorter events, 479.5 us)
Async XLA Ops:
  7.2 58.3 %all-gather.11.cloned.1.call-start = ((), (), s32[]{:S(2)}) async-start(), calls=%async_computation.9 | async-start | bytes 8519680 | tf_op jit(solution)/shard_map/all_gather | solution.py:361
  13.3 179.9 %all-gather.9.cloned.1.call-start = ((), (), s32[]{:S(2)}) async-start(), calls=%async_computation.8 | async-start | bytes 9437184 | tf_op jit(solution)/shard_map/all_gather | solution.py:377
  15.0 520.9 %all-gather.21.cloned.1.call-start = ((), (), s32[]{:S(2)}) async-start(), calls=%async_computation.21 | async-start | bytes 5242880 | tf_op jit(solution)/shard_map/all_gather | solution.py:376
  15.7 547.4 %all-gather.13.cloned.1.call-start = ((), (), s32[]{:S(2)}) async-start(), calls=%async_computation.10 | async-start | bytes 19464192 | tf_op jit(solution)/shard_map/all_gather | solution.py:374
  22.1 565.8 %all-gather.15.cloned.1.call-start = ((), (), s32[]{:S(2)}) async-start(), calls=%async_computation.11 | async-start | bytes 2621440 | tf_op jit(solution)/shard_map/all_gather | solution.py:371
  24.2 721.2 %reduce-scatter.11.cloned.1.call-start = ((), (), s32[]{:S(2)}) async-start(), calls=%async_computation.12 | async-start | bytes 9437184 | tf_op jit(solution)/shard_map/reduce_scatter | solution.py:405
  24.3 261.5 %copy-start.70 = (f32[64,64]{1,0:T(8,128)}, f32[64,64]{1,0:T(8,128)S(1)}, u32[]{:S(2)}) copy-start(f32[64,64]{1,0:T(8,128)S(1)} %fusion.69) | copy-start | bytes 49156
  26.0 238.6 %copy-start.87 = (f32[32,64]{1,0:T(8,128)}, f32[32,64]{1,0:T(8,128)S(1)}, u32[]{:S(2)}) copy-start(f32[32,64]{1,0:T(8,128)S(1)} %compare_convert_fusion) | copy-start | bytes 24580
  32.7 198.6 %copy-start.118 = (f32[2,128]{1,0:T(2,128)}, f32[2,128]{1,0:T(2,128)S(1)}, u32[]{:S(2)}) copy-start(f32[2,128]{1,0:T(2,128)S(1)} %get-tuple-element.274) | copy-start | bytes 3076
  32.7 198.6 %copy-start.120 = (f32[2,128]{1,0:T(2,128)}, f32[2,128]{1,0:T(2,128)S(1)}, u32[]{:S(2)}) copy-start(f32[2,128]{1,0:T(2,128)S(1)} %get-tuple-element.275) | copy-start | bytes 3076
  37.3 493.0 %copy-start.89 = (f32[2048]{0:T(1024)}, f32[2048]{0:T(1024)S(1)}, u32[]{:S(2)}) copy-start(f32[2048]{0:T(1024)S(1)} %fusion.83) | copy-start | bytes 24580
  37.9 227.3 %copy-start.72 = (f32[2048]{0:T(1024)}, f32[2048]{0:T(1024)S(1)}, u32[]{:S(2)}) copy-start(f32[2048]{0:T(1024)S(1)} %get-tuple-element.260) | copy-start | bytes 24580
  37.9 227.3 %copy-start.74 = (f32[2048]{0:T(1024)}, f32[2048]{0:T(1024)S(1)}, u32[]{:S(2)}) copy-start(f32[2048]{0:T(1024)S(1)} %get-tuple-element.261) | copy-start | bytes 24580
  38.0 227.3 %copy-start.76 = (f32[2048]{0:T(1024)}, f32[2048]{0:T(1024)S(1)}, u32[]{:S(2)}) copy-start(f32[2048]{0:T(1024)S(1)} %get-tuple-element.262) | copy-start | bytes 24580
  265.3 252.5 %copy-start.57 = (f32[2,32,64]{2,1,0:T(8,128)}, f32[2,32,64]{2,1,0:T(8,128)S(1)}, u32[]{:S(2)}) copy-start(f32[2,32,64]{2,1,0:T(8,128)S(1)} %get-tuple-element.204) | copy-start | bytes 49156
  596.3 187.1 %all-gather.17.cloned.1.call-start = ((), (), s32[]{:S(2)}) async-start(), calls=%async_computation.13 | async-start | bytes 5242880 | tf_op jit(solution)/shard_map/all_gather | solution.py:414
  749.7 125.6 %reduce-scatter.13.cloned.1.call-start = ((), (), s32[]{:S(2)}) async-start(), calls=%async_computation.14 | async-start | bytes 5242880 | tf_op jit(solution)/shard_map/reduce_scatter | solution.py:427
  830.6 175.1 %all-gather.19.cloned.1.call-start = ((), (), s32[]{:S(2)}) async-start(), calls=%async_computation.15 | async-start | bytes 9437184 | tf_op jit(solution)/shard_map/all_gather | solution.py:441
  880.7 389.6 %reduce-scatter.19.cloned.1.call-start = ((), (), s32[]{:S(2)}) async-start(), calls=%async_computation.18 | async-start | bytes 2621440 | tf_op jit(solution)/shard_map/reduce_scatter | solution.py:449
  1015.0 255.3 %reduce-scatter.15.cloned.1.call-start = ((), (), s32[]{:S(2)}) async-start(), calls=%async_computation.16 | async-start | bytes 5242880 | tf_op jit(solution)/shard_map/reduce_scatter | solution.py:445
  1015.8 373.2 %reduce-scatter.17.cloned.1.call-start = ((), (), s32[]{:S(2)}) async-start(), calls=%async_computation.17 | async-start | bytes 19464192 | tf_op jit(solution)/shard_map/reduce_scatter | solution.py:446
  1016.4 565.3 %reduce-scatter.21.cloned.1.call-start = ((), (), s32[]{:S(2)}) async-start(), calls=%async_computation.19 | async-start | bytes 9437184 | tf_op jit(solution)/shard_map/reduce_scatter | solution.py:468
  1433.4 170.2 %reduce-scatter.25.cloned.1.call-start = ((), (), s32[]{:S(2)}) async-start(), calls=%async_computation.22 | async-start | bytes 327680
  1434.6 230.9 %reduce-scatter.23.cloned.1.call-start = ((), (), s32[]{:S(2)}) async-start(), calls=%async_computation.20 | async-start | bytes 7905280 | tf_op jit(solution)/shard_map/reduce_scatter | solution.py:478
  (143 other events, 2790.4 us)
Sparse Core Ops, SparseCore 0:
  13.4 52.0 all-gather.10
  68.2 124.9 all-gather.8
  194.8 32.6 all-gather.20
  228.8 334.3 all-gather.12
  565.1 22.6 all-gather.14
  596.4 148.9 reduce-scatter.10
  749.8 33.4 all-gather.16
  830.8 44.4 reduce-scatter.12
  880.8 124.9 all-gather.18
  1015.2 29.6 reduce-scatter.18
  1047.5 44.5 reduce-scatter.14
  1095.8 293.0 reduce-scatter.16
  1433.5 148.0 reduce-scatter.20
  1584.5 19.0 reduce-scatter.24
  1606.2 59.2 reduce-scatter.22

commit v2 on v1

--- a/solution.py
+++ b/solution.py
@@ -310,6 +310,177 @@
     return jnp.moveaxis(mixed_heads, 0, 1).reshape(row_count, -1)
 
 
+MESH_ID = pl.DeviceIdType.MESH
+
+
+def _ring_position(h, major, minor):
+    a = h // minor
+    b = h % minor
+    return b * major + a + (b % 2) * (major - 1 - 2 * a)
+
+
+def _ring_member(q, major, minor):
+    count = major * minor
+    q = (q + count) % count
+    b = q // major
+    r = q % major
+    return (r + (b % 2) * (major - 1 - 2 * r)) * minor + b
+
+
+def _ring_sides(major, minor):
+    p = _ring_position(lax.axis_index("head"), major, minor)
+    return p, _ring_member(p + 1, major, minor), _ring_member(p - 1, major, minor)
+
+
+def _greet(nxt, prv, row):
+    barrier = pltpu.get_barrier_semaphore()
+    pl.semaphore_signal(barrier, 1, device_id=(prv, row), device_id_type=MESH_ID)
+    pl.semaphore_signal(barrier, 1, device_id=(nxt, row), device_id_type=MESH_ID)
+    pl.semaphore_wait(barrier, 2)
+
+
+def _ring_gather_kernel(major, minor, x_ref, out_ref, send_sem, recv_sem):
+    count = major * minor
+    blk = x_ref.shape[0]
+    half = blk // 2
+    row = lax.axis_index("row")
+    p, nxt, prv = _ring_sides(major, minor)
+    out_ref[pl.ds(pl.multiple_of(lax.axis_index("head") * blk, blk), blk), :] = x_ref[...]
+    _greet(nxt, prv, row)
+
+    def piece(pos, off):
+        return out_ref.at[pl.ds(pl.multiple_of(_ring_member(pos, major, minor) * blk + off, half), half)]
+
+    def outgoing(d, s):
+        pos = p - s if d == 0 else p + s
+        target = nxt if d == 0 else prv
+        ref = piece(pos, d * half)
+        return pltpu.make_async_remote_copy(
+            ref, ref, send_sem.at[d, s], recv_sem.at[d, s], device_id=(target, row),
+            device_id_type=MESH_ID,
+        )
+
+    def incoming(d, s):
+        pos = p - 1 - s if d == 0 else p + 1 + s
+        source = prv if d == 0 else nxt
+        ref = piece(pos, d * half)
+        return pltpu.make_async_remote_copy(
+            ref, ref, send_sem.at[d, s], recv_sem.at[d, s], device_id=(source, row),
+            device_id_type=MESH_ID,
+        )
+
+    for s in range(count - 1):
+        for d in (0, 1):
+            if s > 0:
+                incoming(d, s - 1).wait_recv()
+            outgoing(d, s).start()
+    for d in (0, 1):
+        incoming(d, count - 2).wait_recv()
+    for s in range(count - 1):
+        for d in (0, 1):
+            outgoing(d, s).wait_send()
+
+
+def _ring_scatter_kernel(major, minor, y_ref, out_ref, buf, send_sem, recv_sem):
+    count = major * minor
+    blk = out_ref.shape[0]
+    half = blk // 2
+    row = lax.axis_index("row")
+    p, nxt, prv = _ring_sides(major, minor)
+    _greet(nxt, prv, row)
+
+    def piece(pos, off):
+        return y_ref.at[pl.ds(pl.multiple_of(_ring_member(pos, major, minor) * blk + off, half), half)]
+
+    def outgoing(d, s):
+        pos = p - s - 1 if d == 0 else p + s + 1
+        target = nxt if d == 0 else prv
+        source = piece(pos, d * half) if s == 0 else buf.at[d, s - 1]
+        return pltpu.make_async_remote_copy(
+            source, buf.at[d, s], send_sem.at[d, s], recv_sem.at[d, s],
+            device_id=(target, row), device_id_type=MESH_ID,
+        )
+
+    def incoming(d, s):
+        source = prv if d == 0 else nxt
+        return pltpu.make_async_remote_copy(
+            buf.at[d, s], buf.at[d, s], send_sem.at[d, s], recv_sem.at[d, s],
+            device_id=(source, row), device_id_type=MESH_ID,
+        )
+
+    for s in range(count - 1):
+        for d in (0, 1):
+            if s > 0:
+                incoming(d, s - 1).wait_recv()
+                pos = p - s - 1 if d == 0 else p + s + 1
+                buf[d, s - 1] = (
+                    buf[d, s - 1].astype(jnp.float32)
+                    + piece(pos, d * half)[...].astype(jnp.float32)
+                ).astype(buf.dtype)
+            outgoing(d, s).start()
+    for d in (0, 1):
+        incoming(d, count - 2).wait_recv()
+        out_ref[pl.ds(d * half, half), :] = piece(p, d * half)[...].astype(
+            jnp.float32
+        ) + buf[d, count - 2].astype(jnp.float32)
+    for s in range(count - 1):
+        for d in (0, 1):
+            outgoing(d, s).wait_send()
+
+
+def ring_gather(x, ring, collective):
+    major, minor = ring
+    count = major * minor
+    blk, width = x.shape
+    return pl.pallas_call(
+        partial(_ring_gather_kernel, major, minor),
+        out_shape=jax.ShapeDtypeStruct((count * blk, width), x.dtype),
+        in_specs=[pl.BlockSpec(memory_space=pltpu.VMEM)],
+        out_specs=pl.BlockSpec(memory_space=pltpu.VMEM),
+        scratch_shapes=[
+            pltpu.SemaphoreType.DMA((2, count - 1)),
+            pltpu.SemaphoreType.DMA((2, count - 1)),
+        ],
+        compiler_params=pltpu.CompilerParams(collective_id=collective, has_side_effects=True),
+        name="ring_gather_head",
+    )(x)
+
+
+def ring_scatter(y, ring, collective):
+    major, minor = ring
+    count = major * minor
+    rows, width = y.shape
+    blk = rows // count
+    return pl.pallas_call(
+        partial(_ring_scatter_kernel, major, minor),
+        out_shape=jax.ShapeDtypeStruct((blk, width), jnp.float32),
+        in_specs=[pl.BlockSpec(memory_space=pltpu.VMEM)],
+        out_specs=pl.BlockSpec(memory_space=pltpu.VMEM),
+        scratch_shapes=[
+            pltpu.VMEM((2, count - 1, blk // 2, width), y.dtype),
+            pltpu.SemaphoreType.DMA((2, count - 1)),
+            pltpu.SemaphoreType.DMA((2, count - 1)),
+        ],
+        compiler_params=pltpu.CompilerParams(collective_id=collective, has_side_effects=True),
+        name="ring_scatter_head",
+    )(y)
+
+
+def head_ring(mesh):
+    count = mesh.shape["head"]
+    try:
+        spots = [tuple(device.coords) for device in mesh.devices[:, 0]]
+    except (AttributeError, TypeError):
+        return (count, 1)
+    moving = [axis for axis in range(len(spots[0])) if spots[0][axis] != spots[1][axis]]
+    if len(moving) != 1:
+        return (count, 1)
+    minor = len({spot[moving[0]] for spot in spots})
+    if count % minor or minor % 2:
+        return (count, 1)
+    return (count // minor, minor)
+
+
 def contract_rows(left, right):
     return lax.dot_general(
         left, right, (((0,), (0,)), ((), ())), preferred_element_type=jnp.float32
@@ -323,6 +494,7 @@
 
 
 def on_device(
+    ring,
     tokens,
     w_query,
     w_key,
@@ -374,7 +546,7 @@
     ffn_all = lax.all_gather(ffn_local, "head", axis=0, tiled=True)
     grad_out = cotangent[0]
     grad_out_rows = lax.all_gather(grad_out, "row", axis=0, tiled=True)
-    all_rows = lax.all_gather(normed_one, "head", axis=0, tiled=True)
+    all_rows = ring_gather(normed_one, ring, 0)
     projected = jnp.dot(all_rows, w_inward, preferred_element_type=jnp.float32)
     proj_parts = [projected[:, edges[spot] : edges[spot + 1]] for spot in range(6)]
     seg_ids = segments[0]
@@ -402,12 +574,11 @@
     w_up_all = ffn_all[:, ff_width : 2 * ff_width]
     w_down_t = ffn_all[:, 2 * ff_width :]
     mixed_half = mixed.astype(jnp.bfloat16)
-    mixer_output = lax.psum_scatter(
+    mixer_output = ring_scatter(
         jnp.dot(mixed_half, out_matrix, preferred_element_type=jnp.float32).astype(jnp.bfloat16),
-        "head",
-        scatter_dimension=0,
-        tiled=True,
-    ).astype(jnp.float32)
+        ring,
+        1,
+    )
     middle = residual + mixer_output
     norm_two, pull_two = jax.vjp(rms_norm, middle, gain_ffn)
     normed_two = norm_two.astype(jnp.bfloat16)
@@ -438,7 +609,7 @@
         jnp.bfloat16
     )
     grad_mid_half = grad_middle.astype(jnp.bfloat16)
-    grad_mid_rows = lax.all_gather(grad_mid_half, "head", axis=0, tiled=True)
+    grad_mid_rows = ring_gather(grad_mid_half, ring, 2)
     grad_mid_rows, ffn_partial, ffn_grad_cat = lax.optimization_barrier(
         (grad_mid_rows, ffn_partial, ffn_grad_cat)
     )
@@ -465,14 +636,7 @@
         axis=1,
     ).astype(jnp.bfloat16)
     grad_inward = contract_rows(all_rows, grad_proj).astype(jnp.bfloat16)
-    grad_norm_one = lax.psum_scatter(
-        contract_cols(grad_proj, w_inward).astype(jnp.bfloat16),
-        "head",
-        scatter_dimension=0,
-        tiled=True,
-    )
-    grad_norm_one, grad_inward = lax.optimization_barrier((grad_norm_one, grad_inward))
-    grad_norm_one = grad_norm_one.astype(jnp.float32)
+    grad_norm_one = ring_scatter(contract_cols(grad_proj, w_inward).astype(jnp.bfloat16), ring, 3)
     grad_in_part, grad_gain_in = pull_one(grad_norm_one)
     grad_input = grad_middle + grad_in_part
     inward_all = lax.psum_scatter(
@@ -527,7 +691,7 @@
 
 def solution(mesh):
     return jax.shard_map(
-        on_device,
+        partial(on_device, head_ring(mesh)),
         mesh=mesh,
         in_specs=(
             P("row", "head", None),

time: 1690 us -> 1440 us (0.85)
  waiting for transfers between devices: 776 us -> 145 us
  Pallas kernels: 95.6 us -> 487 us
    pallas_call x0 -> x4, Pallas kernels: none -> 392 us  [the longest x2 215 us: ring_gather(): pl.pallas_call(partial(_ring_gather_kernel, major, minor), out_shape=jax....]
    reduce_scatter x2 -> x0, waiting for transfers between devices: 277 us -> none  [the longest x1 149 us: on_device(): lax.psum_scatter(jnp.dot(mixed_half, out_matrix, preferred_element_type=j...]
    all_gather x2 -> x0, waiting for transfers between devices: 212 us -> none  [the longest x1 128 us: on_device(): all_rows = lax.all_gather(normed_one, 'head', axis=0, tiled=True)]
    reduce_scatter x1, waiting for transfers between devices: 44.6 us -> 3.09 us  [on_device(): lax.psum_scatter((contract_cols(grad_gate, w_gate_all) + contract_cols(gr...]
    all_gather x1, waiting for transfers between devices: 27.6 us -> 0.01 us  [on_device(): w_inward = lax.all_gather(w_local, 'row', axis=0, tiled=True)]
    all_gather x1, waiting for transfers between devices: 27.2 us -> 0.02 us  [on_device(): ffn_all = lax.all_gather(ffn_local, 'head', axis=0, tiled=True)]
    all_gather x1, waiting for transfers between devices: 24.7 us -> 0.02 us  [on_device(): lax.all_gather(w_out.astype(jnp.bfloat16), 'row', axis=1, tiled=True)]
  transfers between devices with their start and end apart: 15 -> 11, of which waited for: 12 -> 3; matrix products, arithmetic and copies ran while one was open for 35% -> 44% of each run, Pallas kernels for 6% -> 22%
where the time goes in v2:
time: 1440 us
  Pallas kernels  487 us (34%)
  matrix products  295 us (20%)
  other arithmetic  293 us (20%)
  local copies, waits for them, and re-layouts  155 us (11%)
  waiting for transfers between devices  145 us (10%)
  blocking collectives  45.9 us (3%)
  between operations  16.9 us (1%)
    pallas_call x2, Pallas kernels, ring_gather(): pl.pallas_call(partial(_ring_gather_kernel, major, minor), out_shape=jax....  215 us
    pallas_call x2, Pallas kernels, ring_scatter(): pl.pallas_call(partial(_ring_scatter_kernel, major, minor), out_shape=jax...  177 us
    another operation x4, other arithmetic, chunk_prepare(): lax.linalg.triangular_solve(system, right_side, left_side=True, lower=Tru...  135 us
    reduce_scatter x1, waiting for transfers between devices, on_device(): lax.psum_scatter(ffn_grad_cat, 'head', scatter_dimension=0, tiled=True)  119 us
    dot_general x5, matrix products, contract_cols(): lax.dot_general(left, right, (((1,), (1,)), ((), ())), preferred_element_...  60.2 us
    dot_general x5, matrix products, contract_rows(): lax.dot_general(left, right, (((0,), (0,)), ((), ())), preferred_element_...  50.6 us
    pallas_call x1, Pallas kernels, _recur_forward(): pl.pallas_call(partial(_recur_fwd_kernel, nb), grid=(heads, blocks), in_s...  49.5 us
    pallas_call x1, Pallas kernels, delta_rule(): states, updates = state_recurrence(u0, w, kt, c)  46.1 us
  transfers between devices with their start and end apart: 11, of which 3 were waited for; matrix products, arithmetic and copies ran while one was open for 44% of the time, Pallas kernels for 22%

profile of v2, /device:TPU:0, one launch (start us, length us, event | category | flops | bytes accessed | tf_op | source)
XLA Modules:
  0.0 1438.2 jit_solution(8110877356405654454)
XLA Ops:
  29.6 125.8 %ring_gather_head.2 = bf16[2048,2048]{1,0:T(8,128)(2,1)} custom-call(bf16[256,2048]{1,0:T(8,128)(2,1)} %fusion.45.x_ref), custom_call_target="tpu_custom_call" | custom-call | tf_op jit(solution)/shard_map/ring_gather_head/pallas_call | solution.py:435
  161.0 18.2 %fusion.107 = f32[2048,1540]{0,1:T(8,128)S(1)} fusion(bf16[2048,2048]{1,0:T(8,128)(2,1)} %ring_gather_head.2, bf16[2048,1540]{1,0:T(8,128)(2,1)} %all-gather.7.cloned.1.call-done), kind=kOutput, calls=%fused_computation.269 | convolution fusion | flops 12918456320 | bytes 27312128 | tf_op jit(solution)/shard_map/dot_general | solution.py:550
  232.1 10.6 fusion.27
  264.3 134.0 %custom-call.7 = f32[2,32,1,64,64]{1,3,4,2,0:T(8,128)} custom-call(f32[2,32,1,64,64]{1,4,3,2,0:T(8,128)} %get-tuple-element.225), custom_call_target="InvertDiagBlocksLowerTriangular" | custom-call | tf_op jit(solution)/shard_map/jvp(vmap())/triangular_solve | solution.py:223
  423.2 49.5 %jvp_delta_state_forward_.1 = (f32[2,32,256,128]{3,2,1,0:T(8,128)}, f32[2,32,64,256]{3,2,1,0:T(8,128)}) custom-call(f32[2,32,64,256]{3,2,1,0:T(8,128)} %slice.269.u0_ref, f32[2,32,64,128]{3,2,1,0:T(8,128)} %slice.270.w_ref, f32[2,32,64,128]{3,2,1,0:T(8,128)} %get-tuple-element.195.kt_ref, f32[2,32,1,128]{3,2,1,0:T(1,128)} %broadcast_in_dim.34.c_ref), custom_call_target="tpu_custom_call" | custom-call | flops 3221225472 | bytes 20971520 | tf_op jit(solution)/shard_map/jvp(delta_state_forward)/pallas_call | solution.py:121
  472.7 11.7 fusion.109
  511.4 87.1 %ring_scatter_head.2 = f32[256,2048]{1,0:T(8,128)} custom-call(bf16[2048,2048]{1,0:T(8,128)(2,1)} %convolution_convert_fusion.4.y_ref), custom_call_target="tpu_custom_call" | custom-call | tf_op jit(solution)/shard_map/ring_scatter_head/pallas_call | solution.py:454
  602.0 12.2 fusion.20
  614.2 20.3 %all-gather.13.cloned.1.call-done = bf16[1024,2048]{1,0:T(8,128)(2,1)} async-done(((bf16[256,2048]{1,0:T(8,128)(2,1)}), bf16[1024,2048]{1,0:T(8,128)(2,1)}) %all-gather.13.cloned.1.call-update) | async-done | bytes 4194320 | tf_op jit(solution)/shard_map/all_gather | solution.py:585
  634.5 11.9 fusion.12
  646.4 14.8 %multiply_convert_fusion = (bf16[1024,1408]{1,0:T(8,128)(2,1)}, bf16[1024,1408]{1,0:T(8,128)(2,1)S(1)}, bf16[1024,1408]{1,0:T(8,128)(2,1)}) fusion(f32[1024,1408]{1,0:T(8,128)} %fusion.12, f32[1024,1408]{1,0:T(8,128)} %fusion.20, bf16[1024,2048]{1,0:T(8,128)(2,1)S(1)} %copy-done.145, bf16[2048,4224]{0,1:T(8,128)(2,1)} %all-gather.9.cloned.1.call-done), kind=kOutput, calls=%fused_computation.20 | convolution fusion | flops 5928648704 | bytes 30146560 | tf_op jit(solution)/shard_map/dot_general | solution.py:587
  671.1 10.9 add_convert_fusion
  712.3 11.3 fusion.33
  731.5 88.9 %ring_gather_head.3 = bf16[2048,2048]{1,0:T(8,128)(2,1)} custom-call(bf16[256,2048]{1,0:T(8,128)(2,1)} %fusion.91.x_ref), custom_call_target="tpu_custom_call" | custom-call | tf_op jit(solution)/shard_map/ring_gather_head/pallas_call | solution.py:435
  863.5 17.6 %fusion.29.ds_ref = f32[2,32,256,128]{3,2,1,0:T(8,128)} fusion(f32[2,32,64,128]{3,2,1,0:T(8,128)S(1)} %bitcast.284, f32[2,32,64,256]{3,2,1,0:T(8,128)S(1)} %bitcast.279, f32[2,32,64]{2,1,0:T(8,128)S(1)} %copy-done.59), kind=kOutput, calls=%fused_computation.76 | convolution fusion | flops 1611661312 | bytes 14696448 | tf_op jit(solution)/shard_map/transpose(jvp(vmap(nid,nvd->niv)))/dot_general | solution.py:235
  881.1 46.1 %transpose_jvp_delta_state_backward__.1 = (f32[2,32,64,256]{3,2,1,0:T(8,128)}, f32[2,32,64,128]{3,2,1,0:T(8,128)}, f32[2,32,64,128]{3,2,1,0:T(8,128)}, f32[2,32,1,128]{3,2,1,0:T(1,128)}) custom-call(f32[2,32,256,128]{3,2,1,0:T(8,128)} %get-tuple-element.47.s_ref, f32[2,32,64,256]{3,2,1,0:T(8,128)} %get-tuple-element.48.u_ref, ...), custom_call_target="tpu_custom_call" | custom-call | flops 6442450944 | bytes 41943040 | tf_op jit(solution)/shard_map/transpose(jvp(delta_state_backward))/pallas_call | solution.py:246
  927.2 11.2 fusion.8
  969.6 12.3 multiply_reduce_fusion.5
  1085.0 119.1 %reduce-scatter.13.cloned.1.call-done = bf16[256,4224]{0,1:T(8,128)(2,1)} async-done(((bf16[2048,4224]{0,1:T(8,128)(2,1)}), bf16[256,4224]{0,1:T(8,128)(2,1)}) %reduce-scatter.13.cloned.1.call-update) | async-done | bytes 2162704 | tf_op jit(solution)/shard_map/reduce_scatter | solution.py:617
  1205.4 23.7 %concatenate.97 = bf16[2048,1540]{0,1:T(8,128)(2,1)} concatenate(bf16[2048,256]{0,1:T(8,128)(2,1)S(1)} %bitcast.296, bf16[2048,256]{0,1:T(8,128)(2,1)} %bitcast.297, bf16[2048,512]{0,1:T(8,128)(2,1)S(1)} %bitcast.292, bf16[2048,512]{0,1:T(8,128)(2,1)} %bitcast.295, bf16[2048,2]{0,1:T(2,128)(2,1)S(1)} %bitcast.307, bf16[2048,2]{0,1:T(2,128)(2,1)S(1)} %fusion.72), dimensions={1} | concatenate | bytes 12615680 | tf_op jit(solution)/shard_map/concatenate | solution.py:634
  1229.1 19.2 %convolution_convert_fusion.5 = bf16[2048,1540]{0,1:T(8,128)(2,1)} fusion(bf16[2048,2048]{1,0:T(8,128)(2,1)} %ring_gather_head.2, bf16[2048,1540]{0,1:T(8,128)(2,1)} %concatenate.97), kind=kOutput, calls=%fused_computation.8 | convolution fusion | flops 12921610240 | bytes 21004288 | tf_op jit(solution)/shard_map/dot_general | solution.py:485
  1248.2 21.0 %convolution_convert_fusion.y_ref = bf16[2048,2048]{1,0:T(8,128)(2,1)} fusion(bf16[2048,1540]{0,1:T(8,128)(2,1)} %concatenate.97, bf16[2048,1540]{1,0:T(8,128)(2,1)} %all-gather.7.cloned.1.call-done), kind=kOutput, calls=%fused_computation.3 | convolution fusion | flops 12922650624 | bytes 21004288 | tf_op jit(solution)/shard_map/dot_general | solution.py:491
  1269.2 90.0 %ring_scatter_head.3 = f32[256,2048]{1,0:T(8,128)} custom-call(bf16[2048,2048]{1,0:T(8,128)(2,1)} %convolution_convert_fusion.y_ref), custom_call_target="tpu_custom_call" | custom-call | tf_op jit(solution)/shard_map/ring_scatter_head/pallas_call | solution.py:454
  1362.0 39.8 %all-reduce.36 = (f32[16]{0:T(128)}, f32[16]{0:T(128)}, f32[256]{0:T(256)}, f32[2048]{0:T(1024)}, f32[2048]{0:T(1024)}) all-reduce(f32[16]{0:T(128)S(1)} %dynamic_update_slice.6, f32[16]{0:T(128)S(1)} %dynamic_update_slice.7, f32[256]{0:T(256)S(1)} %copy-done.133, ...), channel_id=1, replica_groups=mesh['head'=8,'row'=4] {'head','row'}, use_global_device_ids=true, to_apply=%region_41.42 | all-reduce | flops 4384 | bytes 35072 | tf_op jit(solution)/shard_map/psum | solution.py:665
  (538 shorter events, 414.2 us)
Async XLA Ops:
  7.2 153.8 %all-gather.7.cloned.1.call-start = ((), (), s32[]{:S(2)}) async-start(), calls=%async_computation.6 | async-start | bytes 8519680 | tf_op jit(solution)/shard_map/all_gather | solution.py:533
  13.3 489.0 %all-gather.15.cloned.1.call-start = ((), (), s32[]{:S(2)}) async-start(), calls=%async_computation.15 | async-start | bytes 5242880 | tf_op jit(solution)/shard_map/all_gather | solution.py:548
  14.0 488.3 %all-gather.9.cloned.1.call-start = ((), (), s32[]{:S(2)}) async-start(), calls=%async_computation.7 | async-start | bytes 19464192 | tf_op jit(solution)/shard_map/all_gather | solution.py:546
  17.8 484.5 %all-gather.11.cloned.1.call-start = ((), (), s32[]{:S(2)}) async-start(), calls=%async_computation.8 | async-start | bytes 2621440 | tf_op jit(solution)/shard_map/all_gather | solution.py:543
  19.9 614.6 %all-gather.13.cloned.1.call-start = ((), (), s32[]{:S(2)}) async-start(), calls=%async_computation.9 | async-start | bytes 5242880 | tf_op jit(solution)/shard_map/all_gather | solution.py:585
  19.9 232.5 %copy-start.71 = (f32[64,64]{1,0:T(8,128)}, f32[64,64]{1,0:T(8,128)S(1)}, u32[]{:S(2)}) copy-start(f32[64,64]{1,0:T(8,128)S(1)} %fusion.69) | copy-start | bytes 49156
  21.6 209.8 %copy-start.88 = (f32[32,64]{1,0:T(8,128)}, f32[32,64]{1,0:T(8,128)S(1)}, u32[]{:S(2)}) copy-start(f32[32,64]{1,0:T(8,128)S(1)} %compare_convert_fusion) | copy-start | bytes 24580
  29.6 128.7 %copy-start.143 = (f32[16]{0:T(128)S(1)}, f32[16]{0:T(128)}, u32[]{:S(2)}) copy-start(f32[16]{0:T(128)} %param.32) | copy-start | bytes 196
  29.6 128.8 %copy-start.148 = (f32[16]{0:T(128)S(1)}, f32[16]{0:T(128)}, u32[]{:S(2)}) copy-start(f32[16]{0:T(128)} %param.33) | copy-start | bytes 196
  160.4 336.3 %copy-start.90 = (f32[2048]{0:T(1024)}, f32[2048]{0:T(1024)S(1)}, u32[]{:S(2)}) copy-start(f32[2048]{0:T(1024)S(1)} %fusion.83) | copy-start | bytes 24580
  161.0 71.1 %copy-start.77 = (f32[2048]{0:T(1024)}, f32[2048]{0:T(1024)S(1)}, u32[]{:S(2)}) copy-start(f32[2048]{0:T(1024)S(1)} %get-tuple-element.260) | copy-start | bytes 24580
  232.1 252.3 %copy-start.58 = (f32[2,32,64]{2,1,0:T(8,128)}, f32[2,32,64]{2,1,0:T(8,128)S(1)}, u32[]{:S(2)}) copy-start(f32[2,32,64]{2,1,0:T(8,128)S(1)} %get-tuple-element.200) | copy-start | bytes 49156
  600.4 128.8 %copy-start.17 = (f32[256,2048]{1,0:T(8,128)}, f32[256,2048]{1,0:T(8,128)S(1)}, u32[]{:S(2)}) copy-start(f32[256,2048]{1,0:T(8,128)S(1)} %get-tuple-element.194) | copy-start | bytes 6291460
  600.4 128.8 %copy-start.103 = (f32[256]{0:T(256)}, f32[256]{0:T(256)S(1)}, u32[]{:S(2)}) copy-start(f32[256]{0:T(256)S(1)} %fusion.86) | copy-start | bytes 3076
  601.9 124.7 %reduce-scatter.9.cloned.1.call-start = ((), (), s32[]{:S(2)}) async-start(), calls=%async_computation.10 | async-start | bytes 5242880 | tf_op jit(solution)/shard_map/reduce_scatter | solution.py:598
  682.0 403.0 %reduce-scatter.15.cloned.1.call-start = ((), (), s32[]{:S(2)}) async-start(), calls=%async_computation.13 | async-start | bytes 2621440 | tf_op jit(solution)/shard_map/reduce_scatter | solution.py:620
  731.5 88.9 %copy-start.51 = (bf16[2,2048,256]{1,2,0:T(8,128)(2,1)S(1)}, bf16[2,2048,256]{1,2,0:T(8,128)(2,1)}, u32[]{:S(2)}) copy-start(bf16[2,2048,256]{1,2,0:T(8,128)(2,1)} %copy-done.50) | copy-start | bytes 6291460
  829.6 255.4 %reduce-scatter.11.cloned.1.call-start = ((), (), s32[]{:S(2)}) async-start(), calls=%async_computation.11 | async-start | bytes 5242880 | tf_op jit(solution)/shard_map/reduce_scatter | solution.py:616
  830.3 373.8 %reduce-scatter.13.cloned.1.call-start = ((), (), s32[]{:S(2)}) async-start(), calls=%async_computation.12 | async-start | bytes 19464192 | tf_op jit(solution)/shard_map/reduce_scatter | solution.py:617
  831.1 589.3 %reduce-scatter.19.cloned.1.call-start = ((), (), s32[]{:S(2)}) async-start(), calls=%async_computation.16 | async-start | bytes 327680
  1205.3 217.3 %reduce-scatter.17.cloned.1.call-start = ((), (), s32[]{:S(2)}) async-start(), calls=%async_computation.14 | async-start | bytes 7905280 | tf_op jit(solution)/shard_map/reduce_scatter | solution.py:642
  1269.2 90.5 %copy-start.28 = (bf16[1,256,2048]{2,1,0:T(8,128)(2,1)S(1)}, bf16[1,256,2048]{2,1,0:T(8,128)(2,1)}, u32[]{:S(2)}) copy-start(bf16[1,256,2048]{2,1,0:T(8,128)(2,1)} %param.22) | copy-start | bytes 3145732
  1269.2 90.5 %copy-start.96 = (f32[2048]{0:T(1024)S(1)}, f32[2048]{0:T(1024)}, u32[]{:S(2)}) copy-start(f32[2048]{0:T(1024)} %param.36) | copy-start | bytes 24580
  1269.2 90.5 %copy-start.112 = (f32[256]{0:T(256)S(1)}, f32[256]{0:T(256)}, u32[]{:S(2)}) copy-start(f32[256]{0:T(256)} %copy-done.111) | copy-start | bytes 3076
  (140 other events, 1269.9 us)
Sparse Core Ops, SparseCore 0:
  13.4 52.0 all-gather.6
  67.0 34.5 all-gather.14
  103.1 345.3 all-gather.8
  450.4 22.3 all-gather.10
  602.0 32.3 all-gather.12
  682.1 44.4 reduce-scatter.8
  829.7 29.5 reduce-scatter.14
  861.8 44.5 reduce-scatter.10
  910.8 293.2 reduce-scatter.12
  1207.0 19.0 reduce-scatter.18
  1248.4 57.5 reduce-scatter.16

commit v3 on v2

--- a/solution.py
+++ b/solution.py
@@ -543,10 +543,11 @@
     out_matrix = lax.all_gather(w_out.astype(jnp.bfloat16), "row", axis=1, tiled=True)
     ff_width = w_gate.shape[1]
     ffn_local = jnp.concatenate([w_gate, w_up, w_down.T], axis=1).astype(jnp.bfloat16)
-    ffn_all = lax.all_gather(ffn_local, "head", axis=0, tiled=True)
     grad_out = cotangent[0]
     grad_out_rows = lax.all_gather(grad_out, "row", axis=0, tiled=True)
     all_rows = ring_gather(normed_one, ring, 0)
+    all_rows, out_matrix, ffn_local = lax.optimization_barrier((all_rows, out_matrix, ffn_local))
+    ffn_all = lax.all_gather(ffn_local, "head", axis=0, tiled=True)
     projected = jnp.dot(all_rows, w_inward, preferred_element_type=jnp.float32)
     proj_parts = [projected[:, edges[spot] : edges[spot + 1]] for spot in range(6)]
     seg_ids = segments[0]
@@ -610,19 +611,14 @@
     )
     grad_mid_half = grad_middle.astype(jnp.bfloat16)
     grad_mid_rows = ring_gather(grad_mid_half, ring, 2)
-    grad_mid_rows, ffn_partial, ffn_grad_cat = lax.optimization_barrier(
-        (grad_mid_rows, ffn_partial, ffn_grad_cat)
-    )
+    ffn_grad_all = lax.psum_scatter(ffn_grad_cat, "head", scatter_dimension=0, tiled=True)
     ffn_output = lax.psum_scatter(ffn_partial, "row", scatter_dimension=0, tiled=True)
-    ffn_grad_all = lax.psum_scatter(ffn_grad_cat, "head", scatter_dimension=0, tiled=True)
     grad_mixed = contract_cols(grad_mid_rows, out_matrix)
-    grad_wout = contract_rows(mixed_half, grad_mid_rows)
-    wout_grad = lax.psum_scatter(
-        grad_wout.astype(jnp.bfloat16), "row", scatter_dimension=1, tiled=True
-    )
+    grad_wout = contract_rows(mixed_half, grad_mid_rows).astype(jnp.bfloat16)
+    wout_grad = lax.psum_scatter(grad_wout, "row", scatter_dimension=1, tiled=True)
     core_grads = pull_core(grad_mixed)
-    core_grads, ffn_output, ffn_grad_all, wout_grad = lax.optimization_barrier(
-        (core_grads, ffn_output, ffn_grad_all, wout_grad)
+    core_grads, ffn_output, ffn_grad_all = lax.optimization_barrier(
+        (core_grads, ffn_output, ffn_grad_all)
     )
     final_out = (middle + ffn_output.astype(jnp.float32)).astype(jnp.bfloat16)
     ffn_grad_all = ffn_grad_all.astype(jnp.float32)
@@ -637,6 +633,7 @@
     ).astype(jnp.bfloat16)
     grad_inward = contract_rows(all_rows, grad_proj).astype(jnp.bfloat16)
     grad_norm_one = ring_scatter(contract_cols(grad_proj, w_inward).astype(jnp.bfloat16), ring, 3)
+    grad_norm_one, wout_grad = lax.optimization_barrier((grad_norm_one, wout_grad))
     grad_in_part, grad_gain_in = pull_one(grad_norm_one)
     grad_input = grad_middle + grad_in_part
     inward_all = lax.psum_scatter(

time: 1440 us -> 1360 us (0.944)
  waiting for transfers between devices: 145 us -> 22.7 us
  Pallas kernels: 487 us -> 520 us
    reduce_scatter x1, waiting for transfers between devices: 119 us -> 0.01 us  [on_device(): lax.psum_scatter(ffn_grad_cat, 'head', scatter_dimension=0, tiled=True)]
    pallas_call x2, Pallas kernels: 215 us -> 246 us  [ring_gather(): pl.pallas_call(partial(_ring_gather_kernel, major, minor), out_shape=jax....]
    unnamed x320 -> x340, local copies, waits for them, and re-layouts: 31.3 us -> 37.8 us
  transfers between devices with their start and end apart: 11 -> 11, of which waited for: 3 -> 1; matrix products, arithmetic and copies ran while one was open for 44% -> 49% of each run, Pallas kernels for 22% -> 32%
where the time goes in v3:
time: 1360 us
  Pallas kernels  520 us (38%)
  other arithmetic  295 us (22%)
  matrix products  292 us (21%)
  local copies, waits for them, and re-layouts  167 us (12%)
  blocking collectives  44.7 us (3%)
  waiting for transfers between devices  22.7 us (2%)
  between operations  16.9 us (1%)
    pallas_call x2, Pallas kernels, ring_gather(): pl.pallas_call(partial(_ring_gather_kernel, major, minor), out_shape=jax....  246 us
    pallas_call x2, Pallas kernels, ring_scatter(): pl.pallas_call(partial(_ring_scatter_kernel, major, minor), out_shape=jax...  178 us
    another operation x4, other arithmetic, chunk_prepare(): lax.linalg.triangular_solve(system, right_side, left_side=True, lower=Tru...  134 us
    dot_general x5, matrix products, contract_cols(): lax.dot_general(left, right, (((1,), (1,)), ((), ())), preferred_element_...  61.4 us
    pallas_call x1, Pallas kernels, _recur_forward(): pl.pallas_call(partial(_recur_fwd_kernel, nb), grid=(heads, blocks), in_s...  49.5 us
    dot_general x5, matrix products, contract_rows(): lax.dot_general(left, right, (((0,), (0,)), ((), ())), preferred_element_...  47.3 us
    pallas_call x1, Pallas kernels, delta_rule(): states, updates = state_recurrence(u0, w, kt, c)  46.5 us
    psum x1, blocking collectives, on_device(): lax.psum((grad_gain_in, grad_gain_ffn, core_grads[11], grad_a_full, grad_...  39.5 us
  transfers between devices with their start and end apart: 11, of which 1 were waited for; matrix products, arithmetic and copies ran while one was open for 49% of the time, Pallas kernels for 32%

profile of v3, /device:TPU:0, one launch (start us, length us, event | category | flops | bytes accessed | tf_op | source)
XLA Modules:
  0.0 1359.6 jit_solution(18243367831798299926)
XLA Ops:
  20.4 90.6 %ring_gather_head.2 = bf16[2048,2048]{1,0:T(8,128)(2,1)} custom-call(bf16[256,2048]{1,0:T(8,128)(2,1)} %fusion.45.x_ref), custom_call_target="tpu_custom_call" | custom-call | tf_op jit(solution)/shard_map/ring_gather_head/pallas_call | solution.py:435
  125.8 18.9 %fusion.107 = f32[2048,1540]{0,1:T(8,128)S(1)} fusion(bf16[2048,2048]{1,0:T(8,128)(2,1)} %ring_gather_head.2, bf16[2048,1540]{1,0:T(8,128)(2,1)} %all-gather.9.cloned.1.call-done), kind=kOutput, calls=%fused_computation.269 | convolution fusion | flops 12918456320 | bytes 27312128 | tf_op jit(solution)/shard_map/dot_general | solution.py:551
  195.5 10.4 fusion.38
  205.9 134.0 %custom-call.7 = f32[2,32,1,64,64]{1,3,4,2,0:T(8,128)} custom-call(f32[2,32,1,64,64]{1,4,3,2,0:T(8,128)} %get-tuple-element.227), custom_call_target="InvertDiagBlocksLowerTriangular" | custom-call | tf_op jit(solution)/shard_map/jvp(vmap())/triangular_solve | solution.py:223
  387.9 49.5 %jvp_delta_state_forward_.1 = (f32[2,32,256,128]{3,2,1,0:T(8,128)}, f32[2,32,64,256]{3,2,1,0:T(8,128)}) custom-call(f32[2,32,64,256]{3,2,1,0:T(8,128)} %slice.269.u0_ref, f32[2,32,64,128]{3,2,1,0:T(8,128)} %slice.270.w_ref, f32[2,32,64,128]{3,2,1,0:T(8,128)} %get-tuple-element.197.kt_ref, f32[2,32,1,128]{3,2,1,0:T(1,128)} %broadcast_in_dim.34.c_ref), custom_call_target="tpu_custom_call" | custom-call | flops 3221225472 | bytes 20971520 | tf_op jit(solution)/shard_map/jvp(delta_state_forward)/pallas_call | solution.py:121
  437.4 11.7 fusion.109
  475.7 89.3 %ring_scatter_head.2 = f32[256,2048]{1,0:T(8,128)} custom-call(bf16[2048,2048]{1,0:T(8,128)(2,1)} %convolution_convert_fusion.4.y_ref), custom_call_target="tpu_custom_call" | custom-call | tf_op jit(solution)/shard_map/ring_scatter_head/pallas_call | solution.py:454
  568.4 12.0 fusion.20
  580.4 21.8 %all-gather.13.cloned.1.call-done = bf16[1024,2048]{1,0:T(8,128)(2,1)} async-done(((bf16[256,2048]{1,0:T(8,128)(2,1)}), bf16[1024,2048]{1,0:T(8,128)(2,1)}) %all-gather.13.cloned.1.call-update) | async-done | bytes 4194320 | tf_op jit(solution)/shard_map/all_gather | solution.py:586
  602.2 11.9 fusion.12
  614.1 14.6 %multiply_convert_fusion = (bf16[1024,1408]{1,0:T(8,128)(2,1)}, bf16[1024,1408]{1,0:T(8,128)(2,1)S(1)}, bf16[1024,1408]{1,0:T(8,128)(2,1)}) fusion(f32[1024,1408]{1,0:T(8,128)} %fusion.12, f32[1024,1408]{1,0:T(8,128)} %fusion.20, bf16[1024,2048]{1,0:T(8,128)(2,1)S(1)} %copy-done.153, bf16[2048,4224]{0,1:T(8,128)(2,1)} %all-gather.11.cloned.1.call-done), kind=kOutput, calls=%fused_computation.20 | convolution fusion | flops 5928648704 | bytes 30146560 | tf_op jit(solution)/shard_map/dot_general | solution.py:588
  628.8 9.8 fusion.10
  638.6 11.3 add_convert_fusion
  650.0 11.0 fusion.33
  699.9 155.6 %ring_gather_head.3 = bf16[2048,2048]{1,0:T(8,128)(2,1)} custom-call(bf16[256,2048]{1,0:T(8,128)(2,1)} %fusion.91.x_ref), custom_call_target="tpu_custom_call" | custom-call | tf_op jit(solution)/shard_map/ring_gather_head/pallas_call | solution.py:435
  896.3 17.4 %fusion.29.ds_ref = f32[2,32,256,128]{3,2,1,0:T(8,128)} fusion(f32[2,32,64,128]{3,2,1,0:T(8,128)S(1)} %bitcast.285, f32[2,32,64,256]{3,2,1,0:T(8,128)S(1)} %bitcast.279, f32[2,32,64]{2,1,0:T(8,128)S(1)} %copy-done.70), kind=kOutput, calls=%fused_computation.76 | convolution fusion | flops 1611661312 | bytes 14696448 | tf_op jit(solution)/shard_map/transpose(jvp(vmap(nid,nvd->niv)))/dot_general | solution.py:235
  913.7 46.5 %transpose_jvp_delta_state_backward__.1 = (f32[2,32,64,256]{3,2,1,0:T(8,128)}, f32[2,32,64,128]{3,2,1,0:T(8,128)}, f32[2,32,64,128]{3,2,1,0:T(8,128)}, f32[2,32,1,128]{3,2,1,0:T(1,128)}) custom-call(f32[2,32,256,128]{3,2,1,0:T(8,128)} %get-tuple-element.49.s_ref, f32[2,32,64,256]{3,2,1,0:T(8,128)} %get-tuple-element.50.u_ref, ...), custom_call_target="tpu_custom_call" | custom-call | flops 6442450944 | bytes 41943040 | tf_op jit(solution)/shard_map/transpose(jvp(delta_state_backward))/pallas_call | solution.py:246
  961.4 10.9 fusion.8
  1003.2 11.4 multiply_reduce_fusion.5
  1126.8 23.6 %concatenate.97 = bf16[2048,1540]{0,1:T(8,128)(2,1)} concatenate(bf16[2048,256]{0,1:T(8,128)(2,1)S(1)} %bitcast.298, bf16[2048,256]{0,1:T(8,128)(2,1)} %bitcast.299, bf16[2048,512]{0,1:T(8,128)(2,1)S(1)} %bitcast.294, bf16[2048,512]{0,1:T(8,128)(2,1)} %bitcast.297, bf16[2048,2]{0,1:T(2,128)(2,1)S(1)} %bitcast.309, bf16[2048,2]{0,1:T(2,128)(2,1)S(1)} %fusion.72), dimensions={1} | concatenate | bytes 12615680 | tf_op jit(solution)/shard_map/concatenate | solution.py:630
  1150.4 19.2 %convolution_convert_fusion.5 = bf16[2048,1540]{0,1:T(8,128)(2,1)} fusion(bf16[2048,2048]{1,0:T(8,128)(2,1)} %ring_gather_head.2, bf16[2048,1540]{0,1:T(8,128)(2,1)} %concatenate.97), kind=kOutput, calls=%fused_computation.8 | convolution fusion | flops 12921610240 | bytes 21004288 | tf_op jit(solution)/shard_map/dot_general | solution.py:485
  1169.6 22.2 %convolution_convert_fusion.y_ref = bf16[2048,2048]{1,0:T(8,128)(2,1)} fusion(bf16[2048,1540]{0,1:T(8,128)(2,1)} %concatenate.97, bf16[2048,1540]{1,0:T(8,128)(2,1)} %all-gather.9.cloned.1.call-done), kind=kOutput, calls=%fused_computation.3 | convolution fusion | flops 12922650624 | bytes 21004288 | tf_op jit(solution)/shard_map/dot_general | solution.py:491
  1191.8 88.3 %ring_scatter_head.3 = f32[256,2048]{1,0:T(8,128)} custom-call(bf16[2048,2048]{1,0:T(8,128)(2,1)} %convolution_convert_fusion.y_ref), custom_call_target="tpu_custom_call" | custom-call | tf_op jit(solution)/shard_map/ring_scatter_head/pallas_call | solution.py:454
  1283.1 39.5 %all-reduce.36 = (f32[16]{0:T(128)}, f32[16]{0:T(128)}, f32[256]{0:T(256)}, f32[2048]{0:T(1024)}, f32[2048]{0:T(1024)}) all-reduce(f32[16]{0:T(128)S(1)} %dynamic_update_slice.6, f32[16]{0:T(128)S(1)} %dynamic_update_slice.7, f32[256]{0:T(256)S(1)} %copy-done.141, ...), channel_id=1, replica_groups=mesh['head'=8,'row'=4] {'head','row'}, use_global_device_ids=true, to_apply=%region_41.42 | all-reduce | flops 4384 | bytes 35072 | tf_op jit(solution)/shard_map/psum | solution.py:662
  (559 shorter events, 411.3 us)
Async XLA Ops:
  7.2 106.8 %all-gather.7.cloned.1.call-start = ((), (), s32[]{:S(2)}) async-start(), calls=%async_computation.6 | async-start | bytes 2621440 | tf_op jit(solution)/shard_map/all_gather | solution.py:543
  9.5 116.3 %all-gather.9.cloned.1.call-start = ((), (), s32[]{:S(2)}) async-start(), calls=%async_computation.7 | async-start | bytes 8519680 | tf_op jit(solution)/shard_map/all_gather | solution.py:533
  14.7 451.9 %all-gather.15.cloned.1.call-start = ((), (), s32[]{:S(2)}) async-start(), calls=%async_computation.15 | async-start | bytes 5242880 | tf_op jit(solution)/shard_map/all_gather | solution.py:547
  15.5 451.2 %all-gather.11.cloned.1.call-start = ((), (), s32[]{:S(2)}) async-start(), calls=%async_computation.8 | async-start | bytes 19464192 | tf_op jit(solution)/shard_map/all_gather | solution.py:550
  114.1 488.1 %all-gather.13.cloned.1.call-start = ((), (), s32[]{:S(2)}) async-start(), calls=%async_computation.9 | async-start | bytes 5242880 | tf_op jit(solution)/shard_map/all_gather | solution.py:586
  122.2 338.9 %copy-start.101 = (f32[2048]{0:T(1024)}, f32[2048]{0:T(1024)S(1)}, u32[]{:S(2)}) copy-start(f32[2048]{0:T(1024)S(1)} %fusion.83) | copy-start | bytes 24580
  123.5 228.2 %copy-start.115 = (f32[2,256]{1,0:T(2,128)}, f32[2,256]{1,0:T(2,128)S(1)}, u32[]{:S(2)}) copy-start(f32[2,256]{1,0:T(2,128)S(1)} %get-tuple-element.266) | copy-start | bytes 6148
  123.5 228.2 %copy-start.117 = (f32[2,256]{1,0:T(2,128)}, f32[2,256]{1,0:T(2,128)S(1)}, u32[]{:S(2)}) copy-start(f32[2,256]{1,0:T(2,128)S(1)} %get-tuple-element.269) | copy-start | bytes 6148
  123.5 228.1 %copy-start.119 = (f32[2,256]{1,0:T(2,128)}, f32[2,256]{1,0:T(2,128)S(1)}, u32[]{:S(2)}) copy-start(f32[2,256]{1,0:T(2,128)S(1)} %get-tuple-element.268) | copy-start | bytes 6148
  123.6 228.1 %copy-start.121 = (f32[2,256]{1,0:T(2,128)}, f32[2,256]{1,0:T(2,128)S(1)}, u32[]{:S(2)}) copy-start(f32[2,256]{1,0:T(2,128)S(1)} %get-tuple-element.267) | copy-start | bytes 6148
  123.6 243.0 %copy-start.99 = (f32[32,64]{1,0:T(8,128)}, f32[32,64]{1,0:T(8,128)S(1)}, u32[]{:S(2)}) copy-start(f32[32,64]{1,0:T(8,128)S(1)} %compare_convert_fusion) | copy-start | bytes 24580
  124.2 227.5 %copy-start.84 = (f32[2048]{0:T(1024)}, f32[2048]{0:T(1024)S(1)}, u32[]{:S(2)}) copy-start(f32[2048]{0:T(1024)S(1)} %get-tuple-element.260) | copy-start | bytes 24580
  124.3 227.5 %copy-start.86 = (f32[2048]{0:T(1024)}, f32[2048]{0:T(1024)S(1)}, u32[]{:S(2)}) copy-start(f32[2048]{0:T(1024)S(1)} %get-tuple-element.261) | copy-start | bytes 24580
  124.3 227.5 %copy-start.88 = (f32[2048]{0:T(1024)}, f32[2048]{0:T(1024)S(1)}, u32[]{:S(2)}) copy-start(f32[2048]{0:T(1024)S(1)} %get-tuple-element.262) | copy-start | bytes 24580
  149.5 218.4 %copy-start.65 = (f32[2,32,64]{2,1,0:T(8,128)}, f32[2,32,64]{2,1,0:T(8,128)S(1)}, u32[]{:S(2)}) copy-start(f32[2,32,64]{2,1,0:T(8,128)S(1)} %mul.969) | copy-start | bytes 49156
  151.6 215.0 %copy-start.74 = (f32[2,32,64]{2,1,0:T(8,128)}, f32[2,32,64]{2,1,0:T(8,128)S(1)}, u32[]{:S(2)}) copy-start(f32[2,32,64]{2,1,0:T(8,128)S(1)} %reduce_window_sum.22) | copy-start | bytes 49156
  174.2 193.1 %copy-start.5 = (f32[2,2048,128]{2,1,0:T(8,128)}, f32[2,2048,128]{2,1,0:T(8,128)S(1)}, u32[]{:S(2)}) copy-start(f32[2,2048,128]{2,1,0:T(8,128)S(1)} %get-tuple-element.198) | copy-start | bytes 6291460
  568.4 127.1 %reduce-scatter.9.cloned.1.call-start = ((), (), s32[]{:S(2)}) async-start(), calls=%async_computation.10 | async-start | bytes 5242880 | tf_op jit(solution)/shard_map/reduce_scatter | solution.py:599
  649.9 475.6 %reduce-scatter.11.cloned.1.call-start = ((), (), s32[]{:S(2)}) async-start(), calls=%async_computation.11 | async-start | bytes 5242880 | tf_op jit(solution)/shard_map/reduce_scatter | solution.py:615
  661.0 464.6 %reduce-scatter.13.cloned.1.call-start = ((), (), s32[]{:S(2)}) async-start(), calls=%async_computation.12 | async-start | bytes 19464192 | tf_op jit(solution)/shard_map/reduce_scatter | solution.py:614
  691.0 589.1 %reduce-scatter.15.cloned.1.call-start = ((), (), s32[]{:S(2)}) async-start(), calls=%async_computation.13 | async-start | bytes 2621440 | tf_op jit(solution)/shard_map/reduce_scatter | solution.py:618
  699.9 155.6 %copy-start.155 = (bf16[512,2048]{1,0:T(8,128)(2,1)S(1)}, bf16[512,2048]{1,0:T(8,128)(2,1)}, u32[]{:S(2)}) copy-start(bf16[512,2048]{1,0:T(8,128)(2,1)} %all-gather.7.cloned.1.call-done) | copy-start | bytes 6291460
  1097.1 244.7 %reduce-scatter.19.cloned.1.call-start = ((), (), s32[]{:S(2)}) async-start(), calls=%async_computation.16 | async-start | bytes 327680
  1126.7 217.2 %reduce-scatter.17.cloned.1.call-start = ((), (), s32[]{:S(2)}) async-start(), calls=%async_computation.14 | async-start | bytes 7905280 | tf_op jit(solution)/shard_map/reduce_scatter | solution.py:639
  (150 other events, 2099.2 us)
Sparse Core Ops, SparseCore 0:
  10.2 25.2 all-gather.6
  37.6 49.3 all-gather.8
  88.6 34.5 all-gather.14
  124.5 334.2 all-gather.10
  568.5 33.6 all-gather.12
  650.0 44.4 reduce-scatter.8
  697.3 44.5 reduce-scatter.10
  745.7 319.7 reduce-scatter.12
  1097.2 28.2 reduce-scatter.14
  1128.4 20.0 reduce-scatter.18
  1169.7 54.5 reduce-scatter.16

commit v4 on v3

--- a/solution.py
+++ b/solution.py
@@ -611,8 +611,9 @@
     )
     grad_mid_half = grad_middle.astype(jnp.bfloat16)
     grad_mid_rows = ring_gather(grad_mid_half, ring, 2)
+    ffn_output = lax.psum_scatter(ffn_partial, "row", scatter_dimension=0, tiled=True)
+    grad_mid_rows, ffn_grad_cat = lax.optimization_barrier((grad_mid_rows, ffn_grad_cat))
     ffn_grad_all = lax.psum_scatter(ffn_grad_cat, "head", scatter_dimension=0, tiled=True)
-    ffn_output = lax.psum_scatter(ffn_partial, "row", scatter_dimension=0, tiled=True)
     grad_mixed = contract_cols(grad_mid_rows, out_matrix)
     grad_wout = contract_rows(mixed_half, grad_mid_rows).astype(jnp.bfloat16)
     wout_grad = lax.psum_scatter(grad_wout, "row", scatter_dimension=1, tiled=True)

time: 1360 us -> 1320 us (0.971)
  Pallas kernels: 520 us -> 455 us
  waiting for transfers between devices: 22.7 us -> 42.3 us
    pallas_call x2, Pallas kernels: 246 us -> 179 us  [ring_gather(): pl.pallas_call(partial(_ring_gather_kernel, major, minor), out_shape=jax....]
    reduce_scatter x1, waiting for transfers between devices: 0.01 us -> 16.5 us  [on_device(): lax.psum_scatter(ffn_grad_cat, 'head', scatter_dimension=0, tiled=True)]
  transfers between devices with their start and end apart: 11 -> 11, of which waited for: 1 -> 3; matrix products, arithmetic and copies ran while one was open for 49% -> 51% of each run, Pallas kernels for 32% -> 28%
where the time goes in v4:
time: 1320 us
  Pallas kernels  455 us (34%)
  other arithmetic  295 us (22%)
  matrix products  293 us (22%)
  local copies, waits for them, and re-layouts  168 us (13%)
  blocking collectives  45 us (3%)
  waiting for transfers between devices  42.3 us (3%)
  between operations  16.9 us (1%)
    pallas_call x2, Pallas kernels, ring_scatter(): pl.pallas_call(partial(_ring_scatter_kernel, major, minor), out_shape=jax...  180 us
    pallas_call x2, Pallas kernels, ring_gather(): pl.pallas_call(partial(_ring_gather_kernel, major, minor), out_shape=jax....  179 us
    another operation x4, other arithmetic, chunk_prepare(): lax.linalg.triangular_solve(system, right_side, left_side=True, lower=Tru...  134 us
    dot_general x5, matrix products, contract_cols(): lax.dot_general(left, right, (((1,), (1,)), ((), ())), preferred_element_...  60.3 us
    pallas_call x1, Pallas kernels, _recur_forward(): pl.pallas_call(partial(_recur_fwd_kernel, nb), grid=(heads, blocks), in_s...  49.5 us
    dot_general x5, matrix products, contract_rows(): lax.dot_general(left, right, (((0,), (0,)), ((), ())), preferred_element_...  47.8 us
    pallas_call x1, Pallas kernels, delta_rule(): states, updates = state_recurrence(u0, w, kt, c)  46.1 us
    psum x1, blocking collectives, on_device(): lax.psum((grad_gain_in, grad_gain_ffn, core_grads[11], grad_a_full, grad_...  39.8 us
  transfers between devices with their start and end apart: 11, of which 3 were waited for; matrix products, arithmetic and copies ran while one was open for 51% of the time, Pallas kernels for 28%

profile of v4, /device:TPU:0, one launch (start us, length us, event | category | flops | bytes accessed | tf_op | source)
XLA Modules:
  0.0 1315.6 jit_solution(12842785592517403198)
XLA Ops:
  20.4 90.6 %ring_gather_head.2 = bf16[2048,2048]{1,0:T(8,128)(2,1)} custom-call(bf16[256,2048]{1,0:T(8,128)(2,1)} %fusion.45.x_ref), custom_call_target="tpu_custom_call" | custom-call | tf_op jit(solution)/shard_map/ring_gather_head/pallas_call | solution.py:435
  125.9 18.9 %fusion.107 = f32[2048,1540]{0,1:T(8,128)S(1)} fusion(bf16[2048,2048]{1,0:T(8,128)(2,1)} %ring_gather_head.2, bf16[2048,1540]{1,0:T(8,128)(2,1)} %all-gather.9.cloned.1.call-done), kind=kOutput, calls=%fused_computation.269 | convolution fusion | flops 12918456320 | bytes 27312128 | tf_op jit(solution)/shard_map/dot_general | solution.py:551
  195.9 10.4 fusion.38
  206.3 134.0 %custom-call.7 = f32[2,32,1,64,64]{1,3,4,2,0:T(8,128)} custom-call(f32[2,32,1,64,64]{1,4,3,2,0:T(8,128)} %get-tuple-element.231), custom_call_target="InvertDiagBlocksLowerTriangular" | custom-call | tf_op jit(solution)/shard_map/jvp(vmap())/triangular_solve | solution.py:223
  388.4 49.5 %jvp_delta_state_forward_.1 = (f32[2,32,256,128]{3,2,1,0:T(8,128)}, f32[2,32,64,256]{3,2,1,0:T(8,128)}) custom-call(f32[2,32,64,256]{3,2,1,0:T(8,128)} %slice.269.u0_ref, f32[2,32,64,128]{3,2,1,0:T(8,128)} %slice.270.w_ref, f32[2,32,64,128]{3,2,1,0:T(8,128)} %get-tuple-element.201.kt_ref, f32[2,32,1,128]{3,2,1,0:T(1,128)} %broadcast_in_dim.34.c_ref), custom_call_target="tpu_custom_call" | custom-call | flops 3221225472 | bytes 20971520 | tf_op jit(solution)/shard_map/jvp(delta_state_forward)/pallas_call | solution.py:121
  437.9 11.7 fusion.109
  476.4 89.3 %ring_scatter_head.2 = f32[256,2048]{1,0:T(8,128)} custom-call(bf16[2048,2048]{1,0:T(8,128)(2,1)} %convolution_convert_fusion.4.y_ref), custom_call_target="tpu_custom_call" | custom-call | tf_op jit(solution)/shard_map/ring_scatter_head/pallas_call | solution.py:454
  569.1 11.9 fusion.20
  581.1 21.8 %all-gather.13.cloned.1.call-done = bf16[1024,2048]{1,0:T(8,128)(2,1)} async-done(((bf16[256,2048]{1,0:T(8,128)(2,1)}), bf16[1024,2048]{1,0:T(8,128)(2,1)}) %all-gather.13.cloned.1.call-update) | async-done | bytes 4194320 | tf_op jit(solution)/shard_map/all_gather | solution.py:586
  602.8 11.9 fusion.12
  614.8 14.6 %multiply_convert_fusion = (bf16[1024,1408]{1,0:T(8,128)(2,1)}, bf16[1024,1408]{1,0:T(8,128)(2,1)S(1)}, bf16[1024,1408]{1,0:T(8,128)(2,1)}) fusion(f32[1024,1408]{1,0:T(8,128)} %fusion.12, f32[1024,1408]{1,0:T(8,128)} %fusion.20, bf16[1024,2048]{1,0:T(8,128)(2,1)S(1)} %copy-done.153, bf16[2048,4224]{0,1:T(8,128)(2,1)} %all-gather.11.cloned.1.call-done), kind=kOutput, calls=%fused_computation.20 | convolution fusion | flops 5928648704 | bytes 30146560 | tf_op jit(solution)/shard_map/dot_general | solution.py:588
  639.2 10.8 add_convert_fusion
  650.1 11.0 fusion.33
  699.7 88.9 %ring_gather_head.3 = bf16[2048,2048]{1,0:T(8,128)(2,1)} custom-call(bf16[256,2048]{1,0:T(8,128)(2,1)} %fusion.91.x_ref), custom_call_target="tpu_custom_call" | custom-call | tf_op jit(solution)/shard_map/ring_gather_head/pallas_call | solution.py:435
  834.7 17.4 %fusion.29.ds_ref = f32[2,32,256,128]{3,2,1,0:T(8,128)} fusion(f32[2,32,64,128]{3,2,1,0:T(8,128)S(1)} %bitcast.285, f32[2,32,64,256]{3,2,1,0:T(8,128)S(1)} %bitcast.279, f32[2,32,64]{2,1,0:T(8,128)S(1)} %copy-done.70), kind=kOutput, calls=%fused_computation.76 | convolution fusion | flops 1611661312 | bytes 14696448 | tf_op jit(solution)/shard_map/transpose(jvp(vmap(nid,nvd->niv)))/dot_general | solution.py:235
  852.1 46.1 %transpose_jvp_delta_state_backward__.1 = (f32[2,32,64,256]{3,2,1,0:T(8,128)}, f32[2,32,64,128]{3,2,1,0:T(8,128)}, f32[2,32,64,128]{3,2,1,0:T(8,128)}, f32[2,32,1,128]{3,2,1,0:T(1,128)}) custom-call(f32[2,32,256,128]{3,2,1,0:T(8,128)} %get-tuple-element.51.s_ref, f32[2,32,64,256]{3,2,1,0:T(8,128)} %get-tuple-element.52.u_ref, ...), custom_call_target="tpu_custom_call" | custom-call | flops 6442450944 | bytes 41943040 | tf_op jit(solution)/shard_map/transpose(jvp(delta_state_backward))/pallas_call | solution.py:246
  899.4 11.6 fusion.8
  941.9 11.5 multiply_reduce_fusion.5
  1063.7 16.5 %reduce-scatter.13.cloned.1.call-done = bf16[256,4224]{0,1:T(8,128)(2,1)} async-done(((bf16[2048,4224]{0,1:T(8,128)(2,1)}), bf16[256,4224]{0,1:T(8,128)(2,1)}) %reduce-scatter.13.cloned.1.call-update) | async-done | bytes 2162704 | tf_op jit(solution)/shard_map/reduce_scatter | solution.py:616
  1081.4 23.6 %concatenate.97 = bf16[2048,1540]{0,1:T(8,128)(2,1)} concatenate(bf16[2048,256]{0,1:T(8,128)(2,1)S(1)} %bitcast.298, bf16[2048,256]{0,1:T(8,128)(2,1)} %bitcast.299, bf16[2048,512]{0,1:T(8,128)(2,1)S(1)} %bitcast.294, bf16[2048,512]{0,1:T(8,128)(2,1)} %bitcast.297, bf16[2048,2]{0,1:T(2,128)(2,1)S(1)} %bitcast.309, bf16[2048,2]{0,1:T(2,128)(2,1)S(1)} %fusion.72), dimensions={1} | concatenate | bytes 12615680 | tf_op jit(solution)/shard_map/concatenate | solution.py:631
  1105.1 19.2 %convolution_convert_fusion.5 = bf16[2048,1540]{0,1:T(8,128)(2,1)} fusion(bf16[2048,2048]{1,0:T(8,128)(2,1)} %ring_gather_head.2, bf16[2048,1540]{0,1:T(8,128)(2,1)} %concatenate.97), kind=kOutput, calls=%fused_computation.8 | convolution fusion | flops 12921610240 | bytes 21004288 | tf_op jit(solution)/shard_map/dot_general | solution.py:485
  1124.3 21.0 %convolution_convert_fusion.y_ref = bf16[2048,2048]{1,0:T(8,128)(2,1)} fusion(bf16[2048,1540]{0,1:T(8,128)(2,1)} %concatenate.97, bf16[2048,1540]{1,0:T(8,128)(2,1)} %all-gather.9.cloned.1.call-done), kind=kOutput, calls=%fused_computation.3 | convolution fusion | flops 12922650624 | bytes 21004288 | tf_op jit(solution)/shard_map/dot_general | solution.py:491
  1145.4 90.5 %ring_scatter_head.3 = f32[256,2048]{1,0:T(8,128)} custom-call(bf16[2048,2048]{1,0:T(8,128)(2,1)} %convolution_convert_fusion.y_ref), custom_call_target="tpu_custom_call" | custom-call | tf_op jit(solution)/shard_map/ring_scatter_head/pallas_call | solution.py:454
  1238.8 39.8 %all-reduce.36 = (f32[16]{0:T(128)}, f32[16]{0:T(128)}, f32[256]{0:T(256)}, f32[2048]{0:T(1024)}, f32[2048]{0:T(1024)}) all-reduce(f32[16]{0:T(128)S(1)} %dynamic_update_slice.6, f32[16]{0:T(128)S(1)} %dynamic_update_slice.7, f32[256]{0:T(256)S(1)} %copy-done.141, ...), channel_id=1, replica_groups=mesh['head'=8,'row'=4] {'head','row'}, use_global_device_ids=true, to_apply=%region_41.42 | all-reduce | flops 4384 | bytes 35072 | tf_op jit(solution)/shard_map/psum | solution.py:663
  (559 shorter events, 426.1 us)
Async XLA Ops:
  7.2 106.8 %all-gather.7.cloned.1.call-start = ((), (), s32[]{:S(2)}) async-start(), calls=%async_computation.6 | async-start | bytes 2621440 | tf_op jit(solution)/shard_map/all_gather | solution.py:543
  9.5 116.5 %all-gather.9.cloned.1.call-start = ((), (), s32[]{:S(2)}) async-start(), calls=%async_computation.7 | async-start | bytes 8519680 | tf_op jit(solution)/shard_map/all_gather | solution.py:533
  14.7 452.6 %all-gather.15.cloned.1.call-start = ((), (), s32[]{:S(2)}) async-start(), calls=%async_computation.15 | async-start | bytes 5242880 | tf_op jit(solution)/shard_map/all_gather | solution.py:547
  15.5 451.8 %all-gather.11.cloned.1.call-start = ((), (), s32[]{:S(2)}) async-start(), calls=%async_computation.8 | async-start | bytes 19464192 | tf_op jit(solution)/shard_map/all_gather | solution.py:550
  114.1 488.8 %all-gather.13.cloned.1.call-start = ((), (), s32[]{:S(2)}) async-start(), calls=%async_computation.9 | async-start | bytes 5242880 | tf_op jit(solution)/shard_map/all_gather | solution.py:586
  122.2 339.6 %copy-start.101 = (f32[2048]{0:T(1024)}, f32[2048]{0:T(1024)S(1)}, u32[]{:S(2)}) copy-start(f32[2048]{0:T(1024)S(1)} %fusion.83) | copy-start | bytes 24580
  123.5 228.6 %copy-start.115 = (f32[2,256]{1,0:T(2,128)}, f32[2,256]{1,0:T(2,128)S(1)}, u32[]{:S(2)}) copy-start(f32[2,256]{1,0:T(2,128)S(1)} %get-tuple-element.270) | copy-start | bytes 6148
  123.5 228.6 %copy-start.117 = (f32[2,256]{1,0:T(2,128)}, f32[2,256]{1,0:T(2,128)S(1)}, u32[]{:S(2)}) copy-start(f32[2,256]{1,0:T(2,128)S(1)} %get-tuple-element.273) | copy-start | bytes 6148
  123.5 228.6 %copy-start.119 = (f32[2,256]{1,0:T(2,128)}, f32[2,256]{1,0:T(2,128)S(1)}, u32[]{:S(2)}) copy-start(f32[2,256]{1,0:T(2,128)S(1)} %get-tuple-element.272) | copy-start | bytes 6148
  123.5 228.6 %copy-start.121 = (f32[2,256]{1,0:T(2,128)}, f32[2,256]{1,0:T(2,128)S(1)}, u32[]{:S(2)}) copy-start(f32[2,256]{1,0:T(2,128)S(1)} %get-tuple-element.271) | copy-start | bytes 6148
  123.6 243.4 %copy-start.99 = (f32[32,64]{1,0:T(8,128)}, f32[32,64]{1,0:T(8,128)S(1)}, u32[]{:S(2)}) copy-start(f32[32,64]{1,0:T(8,128)S(1)} %compare_convert_fusion) | copy-start | bytes 24580
  124.2 227.9 %copy-start.84 = (f32[2048]{0:T(1024)}, f32[2048]{0:T(1024)S(1)}, u32[]{:S(2)}) copy-start(f32[2048]{0:T(1024)S(1)} %get-tuple-element.264) | copy-start | bytes 24580
  124.2 227.9 %copy-start.86 = (f32[2048]{0:T(1024)}, f32[2048]{0:T(1024)S(1)}, u32[]{:S(2)}) copy-start(f32[2048]{0:T(1024)S(1)} %get-tuple-element.265) | copy-start | bytes 24580
  124.2 227.9 %copy-start.88 = (f32[2048]{0:T(1024)}, f32[2048]{0:T(1024)S(1)}, u32[]{:S(2)}) copy-start(f32[2048]{0:T(1024)S(1)} %get-tuple-element.266) | copy-start | bytes 24580
  149.6 218.7 %copy-start.65 = (f32[2,32,64]{2,1,0:T(8,128)}, f32[2,32,64]{2,1,0:T(8,128)S(1)}, u32[]{:S(2)}) copy-start(f32[2,32,64]{2,1,0:T(8,128)S(1)} %mul.969) | copy-start | bytes 49156
  151.7 215.4 %copy-start.74 = (f32[2,32,64]{2,1,0:T(8,128)}, f32[2,32,64]{2,1,0:T(8,128)S(1)}, u32[]{:S(2)}) copy-start(f32[2,32,64]{2,1,0:T(8,128)S(1)} %reduce_window_sum.22) | copy-start | bytes 49156
  174.3 193.4 %copy-start.5 = (f32[2,2048,128]{2,1,0:T(8,128)}, f32[2,2048,128]{2,1,0:T(8,128)S(1)}, u32[]{:S(2)}) copy-start(f32[2,2048,128]{2,1,0:T(8,128)S(1)} %get-tuple-element.202) | copy-start | bytes 6291460
  567.6 129.8 %copy-start.17 = (f32[256,2048]{1,0:T(8,128)}, f32[256,2048]{1,0:T(8,128)S(1)}, u32[]{:S(2)}) copy-start(f32[256,2048]{1,0:T(8,128)S(1)} %get-tuple-element.200) | copy-start | bytes 6291460
  569.1 125.7 %reduce-scatter.9.cloned.1.call-start = ((), (), s32[]{:S(2)}) async-start(), calls=%async_computation.10 | async-start | bytes 5242880 | tf_op jit(solution)/shard_map/reduce_scatter | solution.py:599
  650.1 413.6 %reduce-scatter.11.cloned.1.call-start = ((), (), s32[]{:S(2)}) async-start(), calls=%async_computation.11 | async-start | bytes 5242880 | tf_op jit(solution)/shard_map/reduce_scatter | solution.py:614
  661.1 419.1 %reduce-scatter.13.cloned.1.call-start = ((), (), s32[]{:S(2)}) async-start(), calls=%async_computation.12 | async-start | bytes 19464192 | tf_op jit(solution)/shard_map/reduce_scatter | solution.py:616
  788.6 447.3 %reduce-scatter.15.cloned.1.call-start = ((), (), s32[]{:S(2)}) async-start(), calls=%async_computation.13 | async-start | bytes 2621440 | tf_op jit(solution)/shard_map/reduce_scatter | solution.py:619
  1035.9 261.9 %reduce-scatter.19.cloned.1.call-start = ((), (), s32[]{:S(2)}) async-start(), calls=%async_computation.16 | async-start | bytes 327680
  1081.4 218.6 %reduce-scatter.17.cloned.1.call-start = ((), (), s32[]{:S(2)}) async-start(), calls=%async_computation.14 | async-start | bytes 7905280 | tf_op jit(solution)/shard_map/reduce_scatter | solution.py:640
  (150 other events, 1991.8 us)
Sparse Core Ops, SparseCore 0:
  10.2 25.2 all-gather.6
  37.6 49.3 all-gather.8
  88.6 34.5 all-gather.14
  124.5 334.3 all-gather.10
  569.2 33.6 all-gather.12
  650.2 44.5 reduce-scatter.8
  697.5 44.5 reduce-scatter.10
  788.7 291.4 reduce-scatter.12
  1082.9 30.4 reduce-scatter.14
  1116.2 20.0 reduce-scatter.18
  1139.0 58.5 reduce-scatter.16

commit v5 on v4

--- a/solution.py
+++ b/solution.py
@@ -327,26 +327,31 @@
     return (r + (b % 2) * (major - 1 - 2 * r)) * minor + b
 
 
-def _ring_sides(major, minor):
-    p = _ring_position(lax.axis_index("head"), major, minor)
+def _ring_sides(axis, major, minor):
+    p = _ring_position(lax.axis_index(axis), major, minor)
     return p, _ring_member(p + 1, major, minor), _ring_member(p - 1, major, minor)
 
 
-def _greet(nxt, prv, row):
+def _peer(axis, target):
+    if axis == "head":
+        return (target, lax.axis_index("row"))
+    return (lax.axis_index("head"), target)
+
+
+def _greet(axis, nxt, prv):
     barrier = pltpu.get_barrier_semaphore()
-    pl.semaphore_signal(barrier, 1, device_id=(prv, row), device_id_type=MESH_ID)
-    pl.semaphore_signal(barrier, 1, device_id=(nxt, row), device_id_type=MESH_ID)
+    pl.semaphore_signal(barrier, 1, device_id=_peer(axis, prv), device_id_type=MESH_ID)
+    pl.semaphore_signal(barrier, 1, device_id=_peer(axis, nxt), device_id_type=MESH_ID)
     pl.semaphore_wait(barrier, 2)
 
 
-def _ring_gather_kernel(major, minor, x_ref, out_ref, send_sem, recv_sem):
+def _ring_gather_kernel(axis, major, minor, x_ref, out_ref, send_sem, recv_sem):
     count = major * minor
     blk = x_ref.shape[0]
     half = blk // 2
-    row = lax.axis_index("row")
-    p, nxt, prv = _ring_sides(major, minor)
-    out_ref[pl.ds(pl.multiple_of(lax.axis_index("head") * blk, blk), blk), :] = x_ref[...]
-    _greet(nxt, prv, row)
+    p, nxt, prv = _ring_sides(axis, major, minor)
+    out_ref[pl.ds(pl.multiple_of(lax.axis_index(axis) * blk, blk), blk), :] = x_ref[...]
+    _greet(axis, nxt, prv)
 
     def piece(pos, off):
         return out_ref.at[pl.ds(pl.multiple_of(_ring_member(pos, major, minor) * blk + off, half), half)]
@@ -356,7 +361,7 @@
         target = nxt if d == 0 else prv
         ref = piece(pos, d * half)
         return pltpu.make_async_remote_copy(
-            ref, ref, send_sem.at[d, s], recv_sem.at[d, s], device_id=(target, row),
+            ref, ref, send_sem.at[d, s], recv_sem.at[d, s], device_id=_peer(axis, target),
             device_id_type=MESH_ID,
         )
 
@@ -365,7 +370,7 @@
         source = prv if d == 0 else nxt
         ref = piece(pos, d * half)
         return pltpu.make_async_remote_copy(
-            ref, ref, send_sem.at[d, s], recv_sem.at[d, s], device_id=(source, row),
+            ref, ref, send_sem.at[d, s], recv_sem.at[d, s], device_id=_peer(axis, source),
             device_id_type=MESH_ID,
         )
 
@@ -381,13 +386,12 @@
             outgoing(d, s).wait_send()
 
 
-def _ring_scatter_kernel(major, minor, y_ref, out_ref, buf, send_sem, recv_sem):
+def _ring_scatter_kernel(axis, major, minor, y_ref, out_ref, buf, send_sem, recv_sem):
     count = major * minor
     blk = out_ref.shape[0]
     half = blk // 2
-    row = lax.axis_index("row")
-    p, nxt, prv = _ring_sides(major, minor)
-    _greet(nxt, prv, row)
+    p, nxt, prv = _ring_sides(axis, major, minor)
+    _greet(axis, nxt, prv)
 
     def piece(pos, off):
         return y_ref.at[pl.ds(pl.multiple_of(_ring_member(pos, major, minor) * blk + off, half), half)]
@@ -398,14 +402,14 @@
         source = piece(pos, d * half) if s == 0 else buf.at[d, s - 1]
         return pltpu.make_async_remote_copy(
             source, buf.at[d, s], send_sem.at[d, s], recv_sem.at[d, s],
-            device_id=(target, row), device_id_type=MESH_ID,
+            device_id=_peer(axis, target), device_id_type=MESH_ID,
         )
 
     def incoming(d, s):
         source = prv if d == 0 else nxt
         return pltpu.make_async_remote_copy(
             buf.at[d, s], buf.at[d, s], send_sem.at[d, s], recv_sem.at[d, s],
-            device_id=(source, row), device_id_type=MESH_ID,
+            device_id=_peer(axis, source), device_id_type=MESH_ID,
         )
 
     for s in range(count - 1):
@@ -429,11 +433,11 @@
 
 
 def ring_gather(x, ring, collective):
-    major, minor = ring
+    axis, major, minor = ring
     count = major * minor
     blk, width = x.shape
     return pl.pallas_call(
-        partial(_ring_gather_kernel, major, minor),
+        partial(_ring_gather_kernel, axis, major, minor),
         out_shape=jax.ShapeDtypeStruct((count * blk, width), x.dtype),
         in_specs=[pl.BlockSpec(memory_space=pltpu.VMEM)],
         out_specs=pl.BlockSpec(memory_space=pltpu.VMEM),
@@ -442,17 +446,17 @@
             pltpu.SemaphoreType.DMA((2, count - 1)),
         ],
         compiler_params=pltpu.CompilerParams(collective_id=collective, has_side_effects=True),
-        name="ring_gather_head",
+        name="ring_gather_" + axis,
     )(x)
 
 
 def ring_scatter(y, ring, collective):
-    major, minor = ring
+    axis, major, minor = ring
     count = major * minor
     rows, width = y.shape
     blk = rows // count
     return pl.pallas_call(
-        partial(_ring_scatter_kernel, major, minor),
+        partial(_ring_scatter_kernel, axis, major, minor),
         out_shape=jax.ShapeDtypeStruct((blk, width), jnp.float32),
         in_specs=[pl.BlockSpec(memory_space=pltpu.VMEM)],
         out_specs=pl.BlockSpec(memory_space=pltpu.VMEM),
@@ -462,23 +466,24 @@
             pltpu.SemaphoreType.DMA((2, count - 1)),
         ],
         compiler_params=pltpu.CompilerParams(collective_id=collective, has_side_effects=True),
-        name="ring_scatter_head",
+        name="ring_scatter_" + axis,
     )(y)
 
 
-def head_ring(mesh):
-    count = mesh.shape["head"]
+def axis_ring(mesh, axis):
+    count = mesh.shape[axis]
+    members = mesh.devices[:, 0] if axis == "head" else mesh.devices[0, :]
     try:
-        spots = [tuple(device.coords) for device in mesh.devices[:, 0]]
+        spots = [tuple(device.coords) + (device.core_on_chip,) for device in members]
     except (AttributeError, TypeError):
-        return (count, 1)
-    moving = [axis for axis in range(len(spots[0])) if spots[0][axis] != spots[1][axis]]
+        return (axis, count, 1)
+    moving = [spot for spot in range(len(spots[0])) if spots[0][spot] != spots[1][spot]]
     if len(moving) != 1:
-        return (count, 1)
+        return (axis, count, 1)
     minor = len({spot[moving[0]] for spot in spots})
     if count % minor or minor % 2:
-        return (count, 1)
-    return (count // minor, minor)
+        return (axis, count, 1)
+    return (axis, count // minor, minor)
 
 
 def contract_rows(left, right):
@@ -495,6 +500,7 @@
 
 def on_device(
     ring,
+    row_ring,
     tokens,
     w_query,
     w_key,
@@ -583,7 +589,7 @@
     middle = residual + mixer_output
     norm_two, pull_two = jax.vjp(rms_norm, middle, gain_ffn)
     normed_two = norm_two.astype(jnp.bfloat16)
-    ffn_inputs = lax.all_gather(normed_two, "row", axis=0, tiled=True)
+    ffn_inputs = ring_gather(normed_two, row_ring, 4)
     gate_pre = jnp.dot(ffn_inputs, w_gate_all, preferred_element_type=jnp.float32)
     up_pre = jnp.dot(ffn_inputs, w_up_all, preferred_element_type=jnp.float32)
     hidden_val, pull_act = jax.vjp(swiglu, gate_pre, up_pre)
@@ -596,14 +602,13 @@
     grad_upper = grad_up_f.astype(jnp.bfloat16)
     grad_wgate = contract_rows(ffn_inputs, grad_gate)
     grad_wup = contract_rows(ffn_inputs, grad_upper)
-    grad_norm_two = lax.psum_scatter(
+    grad_norm_two = ring_scatter(
         (contract_cols(grad_gate, w_gate_all) + contract_cols(grad_upper, w_up_all)).astype(
             jnp.bfloat16
         ),
-        "row",
-        scatter_dimension=0,
-        tiled=True,
-    ).astype(jnp.float32)
+        row_ring,
+        5,
+    )
     grad_mid_part, grad_gain_ffn = pull_two(grad_norm_two)
     grad_middle = grad_out.astype(jnp.float32) + grad_mid_part
     ffn_grad_cat = jnp.concatenate([grad_wgate, grad_wup, grad_down_t], axis=1).astype(
@@ -689,7 +694,7 @@
 
 def solution(mesh):
     return jax.shard_map(
-        partial(on_device, head_ring(mesh)),
+        partial(on_device, axis_ring(mesh, "head"), axis_ring(mesh, "row")),
         mesh=mesh,
         in_specs=(
             P("row", "head", None),

time: 1320 us -> 1400 us (1.061)
  Pallas kernels: 455 us -> 549 us
  waiting for transfers between devices: 42.3 us -> 23.1 us
    pallas_call x4 -> x6, Pallas kernels: 359 us -> 454 us  [the longest x3 235 us: ring_scatter(): pl.pallas_call(partial(_ring_scatter_kernel, axis, major, minor), out_sha...]
    all_gather x1 -> x0, waiting for transfers between devices: 21.8 us -> none  [on_device(): ffn_inputs = lax.all_gather(normed_two, 'row', axis=0, tiled=True)]
    unnamed x340 -> x338, local copies, waits for them, and re-layouts: 38.3 us -> 38.9 us
  transfers between devices with their start and end apart: 11 -> 9, of which waited for: 3 -> 1; matrix products, arithmetic and copies ran while one was open for 51% -> 48% of each run, Pallas kernels for 28% -> 30%
where the time goes in v5:
time: 1400 us; the launch traced here: 1390 us
  Pallas kernels  549 us (39%)
  other arithmetic  296 us (21%)
  matrix products  290 us (21%)
  local copies, waits for them, and re-layouts  169 us (12%)
  blocking collectives  44.8 us (3%)
  waiting for transfers between devices  23.1 us (2%)
  between operations  16.9 us (1%)
    pallas_call x3, Pallas kernels, ring_scatter(): pl.pallas_call(partial(_ring_scatter_kernel, axis, major, minor), out_sha...  235 us
    pallas_call x3, Pallas kernels, ring_gather(): pl.pallas_call(partial(_ring_gather_kernel, axis, major, minor), out_shap...  219 us
    another operation x4, other arithmetic, chunk_prepare(): lax.linalg.triangular_solve(system, right_side, left_side=True, lower=Tru...  134 us
    dot_general x5, matrix products, contract_cols(): lax.dot_general(left, right, (((1,), (1,)), ((), ())), preferred_element_...  60.1 us
    pallas_call x1, Pallas kernels, _recur_forward(): pl.pallas_call(partial(_recur_fwd_kernel, nb), grid=(heads, blocks), in_s...  49.4 us
    dot_general x5, matrix products, contract_rows(): lax.dot_general(left, right, (((0,), (0,)), ((), ())), preferred_element_...  47.5 us
    pallas_call x1, Pallas kernels, delta_rule(): states, updates = state_recurrence(u0, w, kt, c)  46.1 us
    psum x1, blocking collectives, on_device(): lax.psum((grad_gain_in, grad_gain_ffn, core_grads[11], grad_a_full, grad_...  39.7 us
  transfers between devices with their start and end apart: 9, of which 1 were waited for; matrix products, arithmetic and copies ran while one was open for 48% of the time, Pallas kernels for 30%

profile of v5, /device:TPU:0, one launch (start us, length us, event | category | flops | bytes accessed | tf_op | source)
XLA Modules:
  0.0 1389.4 jit_solution(13765855990809350566)
XLA Ops:
  20.4 90.6 %ring_gather_head.2 = bf16[2048,2048]{1,0:T(8,128)(2,1)} custom-call(bf16[256,2048]{1,0:T(8,128)(2,1)} %fusion.43.x_ref), custom_call_target="tpu_custom_call" | custom-call | tf_op jit(solution)/shard_map/ring_gather_head/pallas_call | solution.py:439
  125.8 18.9 %fusion.103 = f32[2048,1540]{0,1:T(8,128)S(1)} fusion(bf16[2048,2048]{1,0:T(8,128)(2,1)} %ring_gather_head.2, bf16[2048,1540]{1,0:T(8,128)(2,1)} %all-gather.8.cloned.1.call-done), kind=kOutput, calls=%fused_computation.265 | convolution fusion | flops 12918456320 | bytes 27312128 | tf_op jit(solution)/shard_map/dot_general | solution.py:557
  195.7 10.5 fusion.38
  206.2 134.0 %custom-call.7 = f32[2,32,1,64,64]{1,3,4,2,0:T(8,128)} custom-call(f32[2,32,1,64,64]{1,4,3,2,0:T(8,128)} %get-tuple-element.231), custom_call_target="InvertDiagBlocksLowerTriangular" | custom-call | tf_op jit(solution)/shard_map/jvp(vmap())/triangular_solve | solution.py:223
  388.2 49.4 %jvp_delta_state_forward_.1 = (f32[2,32,256,128]{3,2,1,0:T(8,128)}, f32[2,32,64,256]{3,2,1,0:T(8,128)}) custom-call(f32[2,32,64,256]{3,2,1,0:T(8,128)} %slice.269.u0_ref, f32[2,32,64,128]{3,2,1,0:T(8,128)} %slice.270.w_ref, f32[2,32,64,128]{3,2,1,0:T(8,128)} %get-tuple-element.201.kt_ref, f32[2,32,1,128]{3,2,1,0:T(1,128)} %broadcast_in_dim.34.c_ref), custom_call_target="tpu_custom_call" | custom-call | flops 3221225472 | bytes 20971520 | tf_op jit(solution)/shard_map/jvp(delta_state_forward)/pallas_call | solution.py:121
  437.6 11.7 fusion.105
  475.9 89.3 %ring_scatter_head.2 = f32[256,2048]{1,0:T(8,128)} custom-call(bf16[2048,2048]{1,0:T(8,128)(2,1)} %convolution_convert_fusion.4.y_ref), custom_call_target="tpu_custom_call" | custom-call | tf_op jit(solution)/shard_map/ring_scatter_head/pallas_call | solution.py:458
  568.5 40.1 %ring_gather_row.1 = bf16[1024,2048]{1,0:T(8,128)(2,1)} custom-call(bf16[256,2048]{1,0:T(8,128)(2,1)} %multiply_convert_fusion.2.x_ref), custom_call_target="tpu_custom_call" | custom-call | tf_op jit(solution)/shard_map/ring_gather_row/pallas_call | solution.py:439
  608.6 12.1 fusion.20
  631.1 14.7 %multiply_convert_fusion = (bf16[1024,1408]{1,0:T(8,128)(2,1)S(1)}, bf16[1024,1408]{1,0:T(8,128)(2,1)}, bf16[1024,1408]{1,0:T(8,128)(2,1)}) fusion(f32[1024,1408]{1,0:T(8,128)} %fusion.12, f32[1024,1408]{1,0:T(8,128)} %fusion.20, bf16[1024,2048]{1,0:T(8,128)(2,1)S(1)} %copy-done.59, bf16[2048,4224]{0,1:T(8,128)(2,1)} %all-gather.10.cloned.1.call-done), kind=kOutput, calls=%fused_computation.20 | convolution fusion | flops 5928648704 | bytes 30146560 | tf_op jit(solution)/shard_map/dot_general | solution.py:594
  647.4 11.0 fusion.33
  668.7 10.8 add_convert_fusion.y_ref
  679.5 55.6 %ring_scatter_row.1 = f32[256,2048]{1,0:T(8,128)} custom-call(bf16[1024,2048]{1,0:T(8,128)(2,1)} %add_convert_fusion.y_ref), custom_call_target="tpu_custom_call" | custom-call | tf_op jit(solution)/shard_map/ring_scatter_row/pallas_call | solution.py:458
  739.7 87.9 %ring_gather_head.3 = bf16[2048,2048]{1,0:T(8,128)(2,1)} custom-call(bf16[256,2048]{1,0:T(8,128)(2,1)} %fusion.88.x_ref), custom_call_target="tpu_custom_call" | custom-call | tf_op jit(solution)/shard_map/ring_gather_head/pallas_call | solution.py:439
  903.3 17.4 %fusion.29.ds_ref = f32[2,32,256,128]{3,2,1,0:T(8,128)} fusion(f32[2,32,64,128]{3,2,1,0:T(8,128)S(1)} %bitcast.285, f32[2,32,64,256]{3,2,1,0:T(8,128)S(1)} %bitcast.279, f32[2,32,64]{2,1,0:T(8,128)S(1)} %copy-done.71), kind=kOutput, calls=%fused_computation.76 | convolution fusion | flops 1611661312 | bytes 14696448 | tf_op jit(solution)/shard_map/transpose(jvp(vmap(nid,nvd->niv)))/dot_general | solution.py:235
  920.7 46.1 %transpose_jvp_delta_state_backward__.1 = (f32[2,32,64,256]{3,2,1,0:T(8,128)}, f32[2,32,64,128]{3,2,1,0:T(8,128)}, f32[2,32,64,128]{3,2,1,0:T(8,128)}, f32[2,32,1,128]{3,2,1,0:T(1,128)}) custom-call(f32[2,32,256,128]{3,2,1,0:T(8,128)} %get-tuple-element.51.s_ref, f32[2,32,64,256]{3,2,1,0:T(8,128)} %get-tuple-element.52.u_ref, ...), custom_call_target="tpu_custom_call" | custom-call | flops 6442450944 | bytes 41943040 | tf_op jit(solution)/shard_map/transpose(jvp(delta_state_backward))/pallas_call | solution.py:246
  967.9 11.1 fusion.8
  1009.7 11.4 multiply_reduce_fusion.5
  1131.5 22.3 %reduce-scatter.10.cloned.1.call-done = bf16[256,4224]{0,1:T(8,128)(2,1)} async-done(((bf16[2048,4224]{0,1:T(8,128)(2,1)}), bf16[256,4224]{0,1:T(8,128)(2,1)}) %reduce-scatter.10.cloned.1.call-update) | async-done | bytes 2162704 | tf_op jit(solution)/shard_map/reduce_scatter | solution.py:621
  1154.9 23.9 %concatenate.97 = bf16[2048,1540]{0,1:T(8,128)(2,1)} concatenate(bf16[2048,256]{0,1:T(8,128)(2,1)S(1)} %bitcast.298, bf16[2048,256]{0,1:T(8,128)(2,1)} %bitcast.299, bf16[2048,512]{0,1:T(8,128)(2,1)S(1)} %bitcast.294, bf16[2048,512]{0,1:T(8,128)(2,1)} %bitcast.297, bf16[2048,2]{0,1:T(2,128)(2,1)S(1)} %bitcast.309, bf16[2048,2]{0,1:T(2,128)(2,1)S(1)} %fusion.68), dimensions={1} | concatenate | bytes 12615680 | tf_op jit(solution)/shard_map/concatenate | solution.py:636
  1178.8 19.2 %convolution_convert_fusion.5 = bf16[2048,1540]{0,1:T(8,128)(2,1)} fusion(bf16[2048,2048]{1,0:T(8,128)(2,1)} %ring_gather_head.2, bf16[2048,1540]{0,1:T(8,128)(2,1)} %concatenate.97), kind=kOutput, calls=%fused_computation.8 | convolution fusion | flops 12921610240 | bytes 21004288 | tf_op jit(solution)/shard_map/dot_general | solution.py:490
  1198.1 21.0 %convolution_convert_fusion.y_ref = bf16[2048,2048]{1,0:T(8,128)(2,1)} fusion(bf16[2048,1540]{0,1:T(8,128)(2,1)} %concatenate.97, bf16[2048,1540]{1,0:T(8,128)(2,1)} %all-gather.8.cloned.1.call-done), kind=kOutput, calls=%fused_computation.3 | convolution fusion | flops 12922650624 | bytes 21004288 | tf_op jit(solution)/shard_map/dot_general | solution.py:496
  1219.1 90.4 %ring_scatter_head.3 = f32[256,2048]{1,0:T(8,128)} custom-call(bf16[2048,2048]{1,0:T(8,128)(2,1)} %convolution_convert_fusion.y_ref), custom_call_target="tpu_custom_call" | custom-call | tf_op jit(solution)/shard_map/ring_scatter_head/pallas_call | solution.py:458
  1312.5 39.7 %all-reduce.36 = (f32[16]{0:T(128)}, f32[16]{0:T(128)}, f32[256]{0:T(256)}, f32[2048]{0:T(1024)}, f32[2048]{0:T(1024)}) all-reduce(f32[16]{0:T(128)S(1)} %dynamic_update_slice.6, f32[16]{0:T(128)S(1)} %dynamic_update_slice.7, f32[256]{0:T(256)S(1)} %copy-done.142, ...), channel_id=1, replica_groups=mesh['head'=8,'row'=4] {'head','row'}, use_global_device_ids=true, to_apply=%region_40.41 | all-reduce | flops 4384 | bytes 35072 | tf_op jit(solution)/shard_map/psum | solution.py:668
  (553 shorter events, 433.5 us)
Async XLA Ops:
  7.2 106.8 %all-gather.6.cloned.1.call-start = ((), (), s32[]{:S(2)}) async-start(), calls=%async_computation.5 | async-start | bytes 2621440 | tf_op jit(solution)/shard_map/all_gather | solution.py:549
  9.5 116.3 %all-gather.8.cloned.1.call-start = ((), (), s32[]{:S(2)}) async-start(), calls=%async_computation.6 | async-start | bytes 8519680 | tf_op jit(solution)/shard_map/all_gather | solution.py:539
  14.7 452.1 %all-gather.12.cloned.1.call-start = ((), (), s32[]{:S(2)}) async-start(), calls=%async_computation.12 | async-start | bytes 5242880 | tf_op jit(solution)/shard_map/all_gather | solution.py:553
  15.5 451.4 %all-gather.10.cloned.1.call-start = ((), (), s32[]{:S(2)}) async-start(), calls=%async_computation.7 | async-start | bytes 19464192 | tf_op jit(solution)/shard_map/all_gather | solution.py:556
  19.1 91.9 %copy-start.140 = (f32[256]{0:T(256)}, f32[256]{0:T(256)S(1)}, u32[]{:S(2)}) copy-start(f32[256]{0:T(256)S(1)} %fusion.52) | copy-start | bytes 3076
  114.1 1017.4 %reduce-scatter.8.cloned.1.call-start = ((), (), s32[]{:S(2)}) async-start(), calls=%async_computation.8 | async-start | bytes 5242880 | tf_op jit(solution)/shard_map/reduce_scatter | solution.py:619
  122.2 339.1 %copy-start.102 = (f32[2048]{0:T(1024)}, f32[2048]{0:T(1024)S(1)}, u32[]{:S(2)}) copy-start(f32[2048]{0:T(1024)S(1)} %fusion.79) | copy-start | bytes 24580
  123.5 228.4 %copy-start.116 = (f32[2,256]{1,0:T(2,128)}, f32[2,256]{1,0:T(2,128)S(1)}, u32[]{:S(2)}) copy-start(f32[2,256]{1,0:T(2,128)S(1)} %get-tuple-element.270) | copy-start | bytes 6148
  123.5 228.4 %copy-start.118 = (f32[2,256]{1,0:T(2,128)}, f32[2,256]{1,0:T(2,128)S(1)}, u32[]{:S(2)}) copy-start(f32[2,256]{1,0:T(2,128)S(1)} %get-tuple-element.273) | copy-start | bytes 6148
  123.5 228.4 %copy-start.120 = (f32[2,256]{1,0:T(2,128)}, f32[2,256]{1,0:T(2,128)S(1)}, u32[]{:S(2)}) copy-start(f32[2,256]{1,0:T(2,128)S(1)} %get-tuple-element.272) | copy-start | bytes 6148
  123.5 228.4 %copy-start.122 = (f32[2,256]{1,0:T(2,128)}, f32[2,256]{1,0:T(2,128)S(1)}, u32[]{:S(2)}) copy-start(f32[2,256]{1,0:T(2,128)S(1)} %get-tuple-element.271) | copy-start | bytes 6148
  123.6 243.2 %copy-start.100 = (f32[32,64]{1,0:T(8,128)}, f32[32,64]{1,0:T(8,128)S(1)}, u32[]{:S(2)}) copy-start(f32[32,64]{1,0:T(8,128)S(1)} %compare_convert_fusion) | copy-start | bytes 24580
  124.2 227.7 %copy-start.85 = (f32[2048]{0:T(1024)}, f32[2048]{0:T(1024)S(1)}, u32[]{:S(2)}) copy-start(f32[2048]{0:T(1024)S(1)} %get-tuple-element.264) | copy-start | bytes 24580
  124.2 227.7 %copy-start.87 = (f32[2048]{0:T(1024)}, f32[2048]{0:T(1024)S(1)}, u32[]{:S(2)}) copy-start(f32[2048]{0:T(1024)S(1)} %get-tuple-element.265) | copy-start | bytes 24580
  124.2 227.7 %copy-start.89 = (f32[2048]{0:T(1024)}, f32[2048]{0:T(1024)S(1)}, u32[]{:S(2)}) copy-start(f32[2048]{0:T(1024)S(1)} %get-tuple-element.266) | copy-start | bytes 24580
  149.5 218.6 %copy-start.66 = (f32[2,32,64]{2,1,0:T(8,128)}, f32[2,32,64]{2,1,0:T(8,128)S(1)}, u32[]{:S(2)}) copy-start(f32[2,32,64]{2,1,0:T(8,128)S(1)} %mul.969) | copy-start | bytes 49156
  151.6 215.3 %copy-start.75 = (f32[2,32,64]{2,1,0:T(8,128)}, f32[2,32,64]{2,1,0:T(8,128)S(1)}, u32[]{:S(2)}) copy-start(f32[2,32,64]{2,1,0:T(8,128)S(1)} %reduce_window_sum.22) | copy-start | bytes 49156
  174.3 193.2 %copy-start.5 = (f32[2,2048,128]{2,1,0:T(8,128)}, f32[2,2048,128]{2,1,0:T(8,128)S(1)}, u32[]{:S(2)}) copy-start(f32[2,2048,128]{2,1,0:T(8,128)S(1)} %get-tuple-element.202) | copy-start | bytes 6291460
  567.1 170.8 %copy-start.17 = (f32[256,2048]{1,0:T(8,128)}, f32[256,2048]{1,0:T(8,128)S(1)}, u32[]{:S(2)}) copy-start(f32[256,2048]{1,0:T(8,128)S(1)} %get-tuple-element.200) | copy-start | bytes 6291460
  567.2 170.8 %copy-start.114 = (f32[256]{0:T(256)}, f32[256]{0:T(256)S(1)}, u32[]{:S(2)}) copy-start(f32[256]{0:T(256)S(1)} %fusion.82) | copy-start | bytes 3076
  658.4 495.3 %reduce-scatter.10.cloned.1.call-start = ((), (), s32[]{:S(2)}) async-start(), calls=%async_computation.9 | async-start | bytes 19464192 | tf_op jit(solution)/shard_map/reduce_scatter | solution.py:621
  857.8 451.8 %reduce-scatter.12.cloned.1.call-start = ((), (), s32[]{:S(2)}) async-start(), calls=%async_computation.10 | async-start | bytes 2621440 | tf_op jit(solution)/shard_map/reduce_scatter | solution.py:624
  1104.0 267.7 %reduce-scatter.16.cloned.1.call-start = ((), (), s32[]{:S(2)}) async-start(), calls=%async_computation.13 | async-start | bytes 327680
  1154.9 218.9 %reduce-scatter.14.cloned.1.call-start = ((), (), s32[]{:S(2)}) async-start(), calls=%async_computation.11 | async-start | bytes 7905280 | tf_op jit(solution)/shard_map/reduce_scatter | solution.py:645
  (147 other events, 1745.8 us)
Sparse Core Ops, SparseCore 0:
  10.2 25.2 all-gather.5
  37.6 49.3 all-gather.7
  88.6 34.5 all-gather.11
  124.5 334.2 all-gather.9
  658.6 58.3 reduce-scatter.7
  857.9 295.7 reduce-scatter.9
  1156.2 30.4 reduce-scatter.11
  1189.9 20.0 reduce-scatter.15
  1212.5 58.5 reduce-scatter.13

commit v6 on v4

--- a/solution.py
+++ b/solution.py
@@ -633,9 +633,13 @@
         axis=1,
     ).astype(jnp.bfloat16)
     grad_inward = contract_rows(all_rows, grad_proj).astype(jnp.bfloat16)
-    grad_norm_one = ring_scatter(contract_cols(grad_proj, w_inward).astype(jnp.bfloat16), ring, 3)
+    norm_one_partial = contract_cols(grad_proj, w_inward).astype(jnp.bfloat16)
+    grad_gain_in = jnp.sum(
+        norm_one_partial.astype(jnp.float32) * all_rows.astype(jnp.float32), axis=0
+    ) / gain_in
+    grad_norm_one = ring_scatter(norm_one_partial, ring, 3)
     grad_norm_one, wout_grad = lax.optimization_barrier((grad_norm_one, wout_grad))
-    grad_in_part, grad_gain_in = pull_one(grad_norm_one)
+    grad_in_part = pull_one(grad_norm_one)[0]
     grad_input = grad_middle + grad_in_part
     inward_all = lax.psum_scatter(
         grad_inward, "row", scatter_dimension=0, tiled=True
@@ -660,9 +664,12 @@
     grad_dt_full = lax.dynamic_update_slice_in_dim(
         jnp.zeros((head_total,), jnp.float32), core_grads[10], head_first, 0
     )
-    small_sums = lax.psum(
-        (grad_gain_in, grad_gain_ffn, core_grads[11], grad_a_full, grad_dt_full), ("head", "row")
-    )
+    small_parts = (grad_gain_in, grad_gain_ffn, core_grads[11], grad_a_full, grad_dt_full)
+    small_all = lax.psum(jnp.pad(jnp.concatenate(small_parts), (0, 16384 - 4384)), ("head", "row"))
+    small_edges = [0]
+    for part in small_parts:
+        small_edges.append(small_edges[-1] + part.shape[0])
+    small_sums = [small_all[small_edges[i] : small_edges[i + 1]] for i in range(5)]
     return (
         final_out[None],
         grad_input[None],

time: 1320 us -> 1350 us (1.023)
  waiting for transfers between devices: 42.3 us -> 101 us
  blocking collectives: 45 us -> 5.16 us
    reduce_scatter x1, waiting for transfers between devices: 0.01 us -> 58.1 us  [on_device(): lax.psum_scatter(grad_inward, 'row', scatter_dimension=0, tiled=True)]
    psum x1 -> x0, blocking collectives: 39.8 us -> none  [on_device(): lax.psum((grad_gain_in, grad_gain_ffn, core_grads[11], grad_a_full, grad_...]
  transfers between devices with their start and end apart: 11 -> 12, of which waited for: 3 -> 5; matrix products, arithmetic and copies ran while one was open for 51% -> 50% of each run, Pallas kernels for 28% -> 27%
where the time goes in v6:
time: 1350 us; the launch traced here: 1340 us
  Pallas kernels  455 us (34%)
  matrix products  296 us (22%)
  other arithmetic  293 us (22%)
  local copies, waits for them, and re-layouts  173 us (13%)
  waiting for transfers between devices  101 us (7%)
  between operations  17.3 us (1%)
    pallas_call x2, Pallas kernels, ring_scatter(): pl.pallas_call(partial(_ring_scatter_kernel, major, minor), out_shape=jax...  180 us
    pallas_call x2, Pallas kernels, ring_gather(): pl.pallas_call(partial(_ring_gather_kernel, major, minor), out_shape=jax....  179 us
    another operation x4, other arithmetic, chunk_prepare(): lax.linalg.triangular_solve(system, right_side, left_side=True, lower=Tru...  134 us
    dot_general x5, matrix products, contract_cols(): lax.dot_general(left, right, (((1,), (1,)), ((), ())), preferred_element_...  62.8 us
    reduce_scatter x1, waiting for transfers between devices, on_device(): lax.psum_scatter(grad_inward, 'row', scatter_dimension=0, tiled=True)  58.1 us
    pallas_call x1, Pallas kernels, _recur_forward(): pl.pallas_call(partial(_recur_fwd_kernel, nb), grid=(heads, blocks), in_s...  49.4 us
    dot_general x5, matrix products, contract_rows(): lax.dot_general(left, right, (((0,), (0,)), ((), ())), preferred_element_...  48.1 us
    pallas_call x1, Pallas kernels, delta_rule(): states, updates = state_recurrence(u0, w, kt, c)  46.2 us
  transfers between devices with their start and end apart: 12, of which 5 were waited for; matrix products, arithmetic and copies ran while one was open for 50% of the time, Pallas kernels for 27%

profile of v6, /device:TPU:0, one launch (start us, length us, event | category | flops | bytes accessed | tf_op | source)
XLA Modules:
  0.0 1340.4 jit_solution(3728616343064069277)
XLA Ops:
  20.4 90.6 %ring_gather_head.2 = bf16[2048,2048]{1,0:T(8,128)(2,1)} custom-call(bf16[256,2048]{1,0:T(8,128)(2,1)} %fusion.54.x_ref), custom_call_target="tpu_custom_call" | custom-call | tf_op jit(solution)/shard_map/ring_gather_head/pallas_call | solution.py:435
  126.1 18.9 %fusion.107 = f32[2048,1540]{0,1:T(8,128)S(1)} fusion(bf16[2048,2048]{1,0:T(8,128)(2,1)} %ring_gather_head.2, bf16[2048,1540]{1,0:T(8,128)(2,1)} %all-gather.9.cloned.1.call-done), kind=kOutput, calls=%fused_computation.270 | convolution fusion | flops 12918456320 | bytes 27312128 | tf_op jit(solution)/shard_map/dot_general | solution.py:551
  195.8 10.4 fusion.38
  206.2 134.0 %custom-call.7 = f32[2,32,1,64,64]{1,3,4,2,0:T(8,128)} custom-call(f32[2,32,1,64,64]{1,4,3,2,0:T(8,128)} %get-tuple-element.224), custom_call_target="InvertDiagBlocksLowerTriangular" | custom-call | tf_op jit(solution)/shard_map/jvp(vmap())/triangular_solve | solution.py:223
  388.4 49.4 %jvp_delta_state_forward_.1 = (f32[2,32,256,128]{3,2,1,0:T(8,128)}, f32[2,32,64,256]{3,2,1,0:T(8,128)}) custom-call(f32[2,32,64,256]{3,2,1,0:T(8,128)} %slice.289.u0_ref, f32[2,32,64,128]{3,2,1,0:T(8,128)} %slice.290.w_ref, f32[2,32,64,128]{3,2,1,0:T(8,128)} %get-tuple-element.194.kt_ref, f32[2,32,1,128]{3,2,1,0:T(1,128)} %broadcast_in_dim.34.c_ref), custom_call_target="tpu_custom_call" | custom-call | flops 3221225472 | bytes 20971520 | tf_op jit(solution)/shard_map/jvp(delta_state_forward)/pallas_call | solution.py:121
  437.9 11.7 fusion.109
  476.5 89.3 %ring_scatter_head.2 = f32[256,2048]{1,0:T(8,128)} custom-call(bf16[2048,2048]{1,0:T(8,128)(2,1)} %convolution_convert_fusion.4.y_ref), custom_call_target="tpu_custom_call" | custom-call | tf_op jit(solution)/shard_map/ring_scatter_head/pallas_call | solution.py:454
  569.2 12.0 fusion.20
  581.2 21.7 %all-gather.13.cloned.1.call-done = bf16[1024,2048]{1,0:T(8,128)(2,1)} async-done(((bf16[256,2048]{1,0:T(8,128)(2,1)}), bf16[1024,2048]{1,0:T(8,128)(2,1)}) %all-gather.13.cloned.1.call-update) | async-done | bytes 4194320 | tf_op jit(solution)/shard_map/all_gather | solution.py:586
  602.9 11.9 fusion.12
  614.8 14.6 %multiply_convert_fusion = (bf16[1024,1408]{1,0:T(8,128)(2,1)}, bf16[1024,1408]{1,0:T(8,128)(2,1)S(1)}, bf16[1024,1408]{1,0:T(8,128)(2,1)}) fusion(f32[1024,1408]{1,0:T(8,128)} %fusion.12, f32[1024,1408]{1,0:T(8,128)} %fusion.20, bf16[1024,2048]{1,0:T(8,128)(2,1)S(1)} %copy-done.153, bf16[2048,4224]{0,1:T(8,128)(2,1)} %all-gather.11.cloned.1.call-done), kind=kOutput, calls=%fused_computation.21 | convolution fusion | flops 5928648704 | bytes 30146560 | tf_op jit(solution)/shard_map/dot_general | solution.py:588
  639.3 10.8 add_convert_fusion
  650.2 11.0 fusion.33
  699.8 88.8 %ring_gather_head.3 = bf16[2048,2048]{1,0:T(8,128)(2,1)} custom-call(bf16[256,2048]{1,0:T(8,128)(2,1)} %fusion.89.x_ref), custom_call_target="tpu_custom_call" | custom-call | tf_op jit(solution)/shard_map/ring_gather_head/pallas_call | solution.py:435
  834.8 17.4 %fusion.29.ds_ref = f32[2,32,256,128]{3,2,1,0:T(8,128)} fusion(f32[2,32,64,128]{3,2,1,0:T(8,128)S(1)} %bitcast.284, f32[2,32,64,256]{3,2,1,0:T(8,128)S(1)} %bitcast.278, f32[2,32,64]{2,1,0:T(8,128)S(1)} %copy-done.72), kind=kOutput, calls=%fused_computation.77 | convolution fusion | flops 1611661312 | bytes 14696448 | tf_op jit(solution)/shard_map/transpose(jvp(vmap(nid,nvd->niv)))/dot_general | solution.py:235
  852.2 46.2 %transpose_jvp_delta_state_backward__.1 = (f32[2,32,64,256]{3,2,1,0:T(8,128)}, f32[2,32,64,128]{3,2,1,0:T(8,128)}, f32[2,32,64,128]{3,2,1,0:T(8,128)}, f32[2,32,1,128]{3,2,1,0:T(1,128)}) custom-call(f32[2,32,256,128]{3,2,1,0:T(8,128)} %get-tuple-element.51.s_ref, f32[2,32,64,256]{3,2,1,0:T(8,128)} %get-tuple-element.52.u_ref, ...), custom_call_target="tpu_custom_call" | custom-call | flops 6442450944 | bytes 41943040 | tf_op jit(solution)/shard_map/transpose(jvp(delta_state_backward))/pallas_call | solution.py:246
  899.5 11.6 fusion.8
  942.0 11.5 multiply_reduce_fusion.6
  1063.0 17.2 %reduce-scatter.13.cloned.1.call-done = bf16[256,4224]{0,1:T(8,128)(2,1)} async-done(((bf16[2048,4224]{0,1:T(8,128)(2,1)}), bf16[256,4224]{0,1:T(8,128)(2,1)}) %reduce-scatter.13.cloned.1.call-update) | async-done | bytes 2162704 | tf_op jit(solution)/shard_map/reduce_scatter | solution.py:616
  1081.5 23.6 %concatenate.100 = bf16[2048,1540]{0,1:T(8,128)(2,1)} concatenate(bf16[2048,256]{0,1:T(8,128)(2,1)S(1)} %bitcast.297, bf16[2048,256]{0,1:T(8,128)(2,1)} %bitcast.298, bf16[2048,512]{0,1:T(8,128)(2,1)S(1)} %bitcast.293, bf16[2048,512]{0,1:T(8,128)(2,1)} %bitcast.296, bf16[2048,2]{0,1:T(2,128)(2,1)S(1)} %bitcast.308, bf16[2048,2]{0,1:T(2,128)(2,1)S(1)} %fusion.70), dimensions={1} | concatenate | bytes 12615680 | tf_op jit(solution)/shard_map/concatenate | solution.py:631
  1105.1 23.5 %multiply_reduce_fusion = (f32[2048]{0:T(1024)S(1)}, bf16[2048,2048]{1,0:T(8,128)(2,1)}) fusion(bf16[2048,2048]{1,0:T(8,128)(2,1)} %ring_gather_head.2, bf16[2048,1540]{0,1:T(8,128)(2,1)} %concatenate.100, bf16[2048,1540]{1,0:T(8,128)(2,1)} %all-gather.9.cloned.1.call-done), kind=kOutput, calls=%fused_computation.1 | convolution fusion | flops 12939425792 | bytes 29401088 | tf_op jit(solution)/shard_map/dot_general | solution.py:491
  1129.9 19.5 %convolution_convert_fusion.5 = bf16[2048,1540]{0,1:T(8,128)(2,1)} fusion(bf16[2048,2048]{1,0:T(8,128)(2,1)} %ring_gather_head.2, bf16[2048,1540]{0,1:T(8,128)(2,1)} %concatenate.100), kind=kOutput, calls=%fused_computation.9 | convolution fusion | flops 12921610240 | bytes 21004288 | tf_op jit(solution)/shard_map/dot_general | solution.py:485
  1159.7 90.3 %ring_scatter_head.3 = f32[256,2048]{1,0:T(8,128)} custom-call(bf16[2048,2048]{1,0:T(8,128)(2,1)} %get-tuple-element.286.y_ref), custom_call_target="tpu_custom_call" | custom-call | tf_op jit(solution)/shard_map/ring_scatter_head/pallas_call | solution.py:454
  1266.4 58.1 %reduce-scatter.17.cloned.1.call-done = bf16[512,1540]{0,1:T(8,128)(2,1)} async-done(((bf16[2048,1540]{0,1:T(8,128)(2,1)}), bf16[512,1540]{0,1:T(8,128)(2,1)}) %reduce-scatter.17.cloned.1.call-update) | async-done | bytes 1576976 | tf_op jit(solution)/shard_map/reduce_scatter | solution.py:644
  (567 shorter events, 428.9 us)
Async XLA Ops:
  7.2 106.8 %all-gather.7.cloned.1.call-start = ((), (), s32[]{:S(2)}) async-start(), calls=%async_computation.6 | async-start | bytes 2621440 | tf_op jit(solution)/shard_map/all_gather | solution.py:543
  9.5 116.7 %all-gather.9.cloned.1.call-start = ((), (), s32[]{:S(2)}) async-start(), calls=%async_computation.7 | async-start | bytes 8519680 | tf_op jit(solution)/shard_map/all_gather | solution.py:533
  14.7 452.6 %all-gather.15.cloned.1.call-start = ((), (), s32[]{:S(2)}) async-start(), calls=%async_computation.16 | async-start | bytes 5242880 | tf_op jit(solution)/shard_map/all_gather | solution.py:547
  15.5 451.9 %all-gather.11.cloned.1.call-start = ((), (), s32[]{:S(2)}) async-start(), calls=%async_computation.8 | async-start | bytes 19464192 | tf_op jit(solution)/shard_map/all_gather | solution.py:550
  114.0 488.9 %all-gather.13.cloned.1.call-start = ((), (), s32[]{:S(2)}) async-start(), calls=%async_computation.9 | async-start | bytes 5242880 | tf_op jit(solution)/shard_map/all_gather | solution.py:586
  122.2 339.7 %copy-start.103 = (f32[2048]{0:T(1024)}, f32[2048]{0:T(1024)S(1)}, u32[]{:S(2)}) copy-start(f32[2048]{0:T(1024)S(1)} %fusion.81) | copy-start | bytes 24580
  123.5 228.5 %copy-start.117 = (f32[2,256]{1,0:T(2,128)}, f32[2,256]{1,0:T(2,128)S(1)}, u32[]{:S(2)}) copy-start(f32[2,256]{1,0:T(2,128)S(1)} %get-tuple-element.267) | copy-start | bytes 6148
  123.5 228.5 %copy-start.119 = (f32[2,256]{1,0:T(2,128)}, f32[2,256]{1,0:T(2,128)S(1)}, u32[]{:S(2)}) copy-start(f32[2,256]{1,0:T(2,128)S(1)} %get-tuple-element.270) | copy-start | bytes 6148
  123.6 228.5 %copy-start.121 = (f32[2,256]{1,0:T(2,128)}, f32[2,256]{1,0:T(2,128)S(1)}, u32[]{:S(2)}) copy-start(f32[2,256]{1,0:T(2,128)S(1)} %get-tuple-element.269) | copy-start | bytes 6148
  123.6 228.5 %copy-start.123 = (f32[2,256]{1,0:T(2,128)}, f32[2,256]{1,0:T(2,128)S(1)}, u32[]{:S(2)}) copy-start(f32[2,256]{1,0:T(2,128)S(1)} %get-tuple-element.268) | copy-start | bytes 6148
  123.7 243.4 %copy-start.101 = (f32[32,64]{1,0:T(8,128)}, f32[32,64]{1,0:T(8,128)S(1)}, u32[]{:S(2)}) copy-start(f32[32,64]{1,0:T(8,128)S(1)} %compare_convert_fusion) | copy-start | bytes 24580
  124.3 227.8 %copy-start.86 = (f32[2048]{0:T(1024)}, f32[2048]{0:T(1024)S(1)}, u32[]{:S(2)}) copy-start(f32[2048]{0:T(1024)S(1)} %get-tuple-element.261) | copy-start | bytes 24580
  124.3 227.8 %copy-start.88 = (f32[2048]{0:T(1024)}, f32[2048]{0:T(1024)S(1)}, u32[]{:S(2)}) copy-start(f32[2048]{0:T(1024)S(1)} %get-tuple-element.262) | copy-start | bytes 24580
  124.3 227.8 %copy-start.90 = (f32[2048]{0:T(1024)}, f32[2048]{0:T(1024)S(1)}, u32[]{:S(2)}) copy-start(f32[2048]{0:T(1024)S(1)} %get-tuple-element.263) | copy-start | bytes 24580
  149.8 218.5 %copy-start.66 = (f32[2,32,64]{2,1,0:T(8,128)}, f32[2,32,64]{2,1,0:T(8,128)S(1)}, u32[]{:S(2)}) copy-start(f32[2,32,64]{2,1,0:T(8,128)S(1)} %mul.969) | copy-start | bytes 49156
  151.9 215.2 %copy-start.76 = (f32[2,32,64]{2,1,0:T(8,128)}, f32[2,32,64]{2,1,0:T(8,128)S(1)}, u32[]{:S(2)}) copy-start(f32[2,32,64]{2,1,0:T(8,128)S(1)} %reduce_window_sum.22) | copy-start | bytes 49156
  174.5 193.2 %copy-start.5 = (f32[2,2048,128]{2,1,0:T(8,128)}, f32[2,2048,128]{2,1,0:T(8,128)S(1)}, u32[]{:S(2)}) copy-start(f32[2,2048,128]{2,1,0:T(8,128)S(1)} %get-tuple-element.195) | copy-start | bytes 6291460
  569.2 125.7 %reduce-scatter.9.cloned.1.call-start = ((), (), s32[]{:S(2)}) async-start(), calls=%async_computation.10 | async-start | bytes 5242880 | tf_op jit(solution)/shard_map/reduce_scatter | solution.py:599
  650.2 412.8 %reduce-scatter.11.cloned.1.call-start = ((), (), s32[]{:S(2)}) async-start(), calls=%async_computation.11 | async-start | bytes 5242880 | tf_op jit(solution)/shard_map/reduce_scatter | solution.py:614
  661.2 419.0 %reduce-scatter.13.cloned.1.call-start = ((), (), s32[]{:S(2)}) async-start(), calls=%async_computation.12 | async-start | bytes 19464192 | tf_op jit(solution)/shard_map/reduce_scatter | solution.py:616
  788.7 461.4 %reduce-scatter.15.cloned.1.call-start = ((), (), s32[]{:S(2)}) async-start(), calls=%async_computation.13 | async-start | bytes 2621440 | tf_op jit(solution)/shard_map/reduce_scatter | solution.py:619
  1035.2 224.9 %reduce-scatter.19.cloned.1.call-start = ((), (), s32[]{:S(2)}) async-start(), calls=%async_computation.17 | async-start | bytes 327680
  1081.4 181.1 %all-reduce.39.cloned.1.call-start = ((), (), s32[]{:S(2)}) async-start(), calls=%async_computation.15 | async-start | bytes 131072 | tf_op jit(solution)/shard_map/psum | solution.py:668
  1129.8 194.7 %reduce-scatter.17.cloned.1.call-start = ((), (), s32[]{:S(2)}) async-start(), calls=%async_computation.14 | async-start | bytes 7905280 | tf_op jit(solution)/shard_map/reduce_scatter | solution.py:644
  (151 other events, 1793.5 us)
Sparse Core Ops, SparseCore 0:
  10.2 25.2 all-gather.6
  37.6 49.3 all-gather.8
  88.6 34.5 all-gather.14
  124.5 334.2 all-gather.10
  569.3 33.5 all-gather.12
  650.3 44.5 reduce-scatter.8
  697.5 44.5 reduce-scatter.10
  788.8 291.4 reduce-scatter.12
  1082.9 30.4 reduce-scatter.14
  1116.3 20.0 reduce-scatter.18
  1143.5 118.9 all-reduce.38
  1265.1 59.3 reduce-scatter.16

commit v7 on v6

--- a/solution.py
+++ b/solution.py
@@ -665,7 +665,7 @@
         jnp.zeros((head_total,), jnp.float32), core_grads[10], head_first, 0
     )
     small_parts = (grad_gain_in, grad_gain_ffn, core_grads[11], grad_a_full, grad_dt_full)
-    small_all = lax.psum(jnp.pad(jnp.concatenate(small_parts), (0, 16384 - 4384)), ("head", "row"))
+    small_all = lax.psum(lax.psum(jnp.concatenate(small_parts), "row"), "head")
     small_edges = [0]
     for part in small_parts:
         small_edges.append(small_edges[-1] + part.shape[0])

time: 1350 us -> 1330 us (0.985)
  waiting for transfers between devices: 101 us -> 32.3 us
  blocking collectives: 5.16 us -> 52.9 us
    reduce_scatter x1, waiting for transfers between devices: 58.1 us -> 0.01 us  [on_device(): lax.psum_scatter(grad_inward, 'row', scatter_dimension=0, tiled=True)]
    psum x0 -> x2, blocking collectives: none -> 47.7 us  [on_device(): small_all = lax.psum(lax.psum(jnp.concatenate(small_parts), 'row'), 'head')]
    unnamed x340 -> x344, local copies, waits for them, and re-layouts: 38.4 us -> 38.3 us
  transfers between devices with their start and end apart: 12 -> 11, of which waited for: 5 -> 3; matrix products, arithmetic and copies ran while one was open for 50% -> 51% of each run, Pallas kernels for 27% -> 27%
where the time goes in v7:
time: 1330 us; the launch traced here: 1320 us
  Pallas kernels  450 us (34%)
  matrix products  306 us (23%)
  other arithmetic  293 us (22%)
  local copies, waits for them, and re-layouts  170 us (13%)
  blocking collectives  52.9 us (4%)
  waiting for transfers between devices  32.3 us (2%)
  between operations  17 us (1%)
    pallas_call x2, Pallas kernels, ring_gather(): pl.pallas_call(partial(_ring_gather_kernel, major, minor), out_shape=jax....  180 us
    pallas_call x2, Pallas kernels, ring_scatter(): pl.pallas_call(partial(_ring_scatter_kernel, major, minor), out_shape=jax...  175 us
    another operation x4, other arithmetic, chunk_prepare(): lax.linalg.triangular_solve(system, right_side, left_side=True, lower=Tru...  134 us
    dot_general x5, matrix products, contract_cols(): lax.dot_general(left, right, (((1,), (1,)), ((), ())), preferred_element_...  62.9 us
    dot_general x5, matrix products, contract_rows(): lax.dot_general(left, right, (((0,), (0,)), ((), ())), preferred_element_...  58.3 us
    pallas_call x1, Pallas kernels, _recur_forward(): pl.pallas_call(partial(_recur_fwd_kernel, nb), grid=(heads, blocks), in_s...  49.5 us
    psum x2, blocking collectives, on_device(): small_all = lax.psum(lax.psum(jnp.concatenate(small_parts), 'row'), 'head')  47.7 us
    pallas_call x1, Pallas kernels, delta_rule(): states, updates = state_recurrence(u0, w, kt, c)  46.1 us
  transfers between devices with their start and end apart: 11, of which 3 were waited for; matrix products, arithmetic and copies ran while one was open for 51% of the time, Pallas kernels for 27%

profile of v7, /device:TPU:0, one launch (start us, length us, event | category | flops | bytes accessed | tf_op | source)
XLA Modules:
  0.0 1321.7 jit_solution(813958431429581399)
XLA Ops:
  20.4 90.6 %ring_gather_head.2 = bf16[2048,2048]{1,0:T(8,128)(2,1)} custom-call(bf16[256,2048]{1,0:T(8,128)(2,1)} %fusion.54.x_ref), custom_call_target="tpu_custom_call" | custom-call | tf_op jit(solution)/shard_map/ring_gather_head/pallas_call | solution.py:435
  126.2 18.9 %fusion.107 = f32[2048,1540]{0,1:T(8,128)S(1)} fusion(bf16[2048,2048]{1,0:T(8,128)(2,1)} %ring_gather_head.2, bf16[2048,1540]{1,0:T(8,128)(2,1)} %all-gather.9.cloned.1.call-done), kind=kOutput, calls=%fused_computation.270 | convolution fusion | flops 12918456320 | bytes 27312128 | tf_op jit(solution)/shard_map/dot_general | solution.py:551
  206.2 134.0 %custom-call.7 = f32[2,32,1,64,64]{1,3,4,2,0:T(8,128)} custom-call(f32[2,32,1,64,64]{1,4,3,2,0:T(8,128)} %get-tuple-element.224), custom_call_target="InvertDiagBlocksLowerTriangular" | custom-call | tf_op jit(solution)/shard_map/jvp(vmap())/triangular_solve | solution.py:223
  388.3 49.5 %jvp_delta_state_forward_.1 = (f32[2,32,256,128]{3,2,1,0:T(8,128)}, f32[2,32,64,256]{3,2,1,0:T(8,128)}) custom-call(f32[2,32,64,256]{3,2,1,0:T(8,128)} %slice.289.u0_ref, f32[2,32,64,128]{3,2,1,0:T(8,128)} %slice.290.w_ref, f32[2,32,64,128]{3,2,1,0:T(8,128)} %get-tuple-element.194.kt_ref, f32[2,32,1,128]{3,2,1,0:T(1,128)} %broadcast_in_dim.34.c_ref), custom_call_target="tpu_custom_call" | custom-call | flops 3221225472 | bytes 20971520 | tf_op jit(solution)/shard_map/jvp(delta_state_forward)/pallas_call | solution.py:121
  437.7 11.7 fusion.109
  476.3 89.2 %ring_scatter_head.2 = f32[256,2048]{1,0:T(8,128)} custom-call(bf16[2048,2048]{1,0:T(8,128)(2,1)} %convolution_convert_fusion.4.y_ref), custom_call_target="tpu_custom_call" | custom-call | tf_op jit(solution)/shard_map/ring_scatter_head/pallas_call | solution.py:454
  569.0 12.0 fusion.20
  581.0 21.8 %all-gather.13.cloned.1.call-done = bf16[1024,2048]{1,0:T(8,128)(2,1)} async-done(((bf16[256,2048]{1,0:T(8,128)(2,1)}), bf16[1024,2048]{1,0:T(8,128)(2,1)}) %all-gather.13.cloned.1.call-update) | async-done | bytes 4194320 | tf_op jit(solution)/shard_map/all_gather | solution.py:586
  602.8 11.9 fusion.12
  614.7 14.6 %multiply_convert_fusion = (bf16[1024,1408]{1,0:T(8,128)(2,1)}, bf16[1024,1408]{1,0:T(8,128)(2,1)S(1)}, bf16[1024,1408]{1,0:T(8,128)(2,1)}) fusion(f32[1024,1408]{1,0:T(8,128)} %fusion.12, f32[1024,1408]{1,0:T(8,128)} %fusion.20, bf16[1024,2048]{1,0:T(8,128)(2,1)S(1)} %copy-done.155, bf16[2048,4224]{0,1:T(8,128)(2,1)} %all-gather.11.cloned.1.call-done), kind=kOutput, calls=%fused_computation.21 | convolution fusion | flops 5928648704 | bytes 30146560 | tf_op jit(solution)/shard_map/dot_general | solution.py:588
  639.2 10.8 add_convert_fusion
  650.1 11.0 fusion.33
  699.6 88.9 %ring_gather_head.3 = bf16[2048,2048]{1,0:T(8,128)(2,1)} custom-call(bf16[256,2048]{1,0:T(8,128)(2,1)} %fusion.89.x_ref), custom_call_target="tpu_custom_call" | custom-call | tf_op jit(solution)/shard_map/ring_gather_head/pallas_call | solution.py:435
  834.7 17.4 %fusion.29.ds_ref = f32[2,32,256,128]{3,2,1,0:T(8,128)} fusion(f32[2,32,64,128]{3,2,1,0:T(8,128)S(1)} %bitcast.284, f32[2,32,64,256]{3,2,1,0:T(8,128)S(1)} %bitcast.278, f32[2,32,64]{2,1,0:T(8,128)S(1)} %copy-done.72), kind=kOutput, calls=%fused_computation.77 | convolution fusion | flops 1611661312 | bytes 14696448 | tf_op jit(solution)/shard_map/transpose(jvp(vmap(nid,nvd->niv)))/dot_general | solution.py:235
  852.1 46.1 %transpose_jvp_delta_state_backward__.1 = (f32[2,32,64,256]{3,2,1,0:T(8,128)}, f32[2,32,64,128]{3,2,1,0:T(8,128)}, f32[2,32,64,128]{3,2,1,0:T(8,128)}, f32[2,32,1,128]{3,2,1,0:T(1,128)}) custom-call(f32[2,32,256,128]{3,2,1,0:T(8,128)} %get-tuple-element.51.s_ref, f32[2,32,64,256]{3,2,1,0:T(8,128)} %get-tuple-element.52.u_ref, ...), custom_call_target="tpu_custom_call" | custom-call | flops 6442450944 | bytes 41943040 | tf_op jit(solution)/shard_map/transpose(jvp(delta_state_backward))/pallas_call | solution.py:246
  899.4 11.6 fusion.8
  941.9 11.5 multiply_reduce_fusion.6
  1029.9 16.4 %convolution_convert_fusion.6 = bf16[512,2048]{1,0:T(8,128)(2,1)} fusion(bf16[2048,2048]{1,0:T(8,128)(2,1)S(1)} %bitcast.292, bf16[2048,512]{0,1:T(8,128)(2,1)S(1)} %bitcast.300), kind=kOutput, calls=%fused_computation.92 | convolution fusion | flops 4296015872 | bytes 12582912 | tf_op jit(solution)/shard_map/dot_general | solution.py:485
  1081.4 23.3 %concatenate.100 = bf16[2048,1540]{0,1:T(8,128)(2,1)} concatenate(bf16[2048,256]{0,1:T(8,128)(2,1)S(1)} %bitcast.297, bf16[2048,256]{0,1:T(8,128)(2,1)} %bitcast.298, bf16[2048,512]{0,1:T(8,128)(2,1)S(1)} %bitcast.293, bf16[2048,512]{0,1:T(8,128)(2,1)} %bitcast.296, bf16[2048,2]{0,1:T(2,128)(2,1)S(1)} %bitcast.308, bf16[2048,2]{0,1:T(2,128)(2,1)S(1)} %fusion.70), dimensions={1} | concatenate | bytes 12615680 | tf_op jit(solution)/shard_map/concatenate | solution.py:631
  1104.8 19.2 %convolution_convert_fusion.5 = bf16[2048,1540]{0,1:T(8,128)(2,1)} fusion(bf16[2048,2048]{1,0:T(8,128)(2,1)} %ring_gather_head.2, bf16[2048,1540]{0,1:T(8,128)(2,1)} %concatenate.100), kind=kOutput, calls=%fused_computation.9 | convolution fusion | flops 12921610240 | bytes 21004288 | tf_op jit(solution)/shard_map/dot_general | solution.py:485
  1134.3 23.6 %multiply_reduce_fusion = (f32[2048]{0:T(1024)S(1)}, bf16[2048,2048]{1,0:T(8,128)(2,1)}) fusion(bf16[2048,2048]{1,0:T(8,128)(2,1)} %ring_gather_head.2, bf16[2048,1540]{0,1:T(8,128)(2,1)} %concatenate.100, bf16[2048,1540]{1,0:T(8,128)(2,1)} %all-gather.9.cloned.1.call-done), kind=kOutput, calls=%fused_computation.1 | convolution fusion | flops 12939425792 | bytes 29401088 | tf_op jit(solution)/shard_map/dot_general | solution.py:491
  1158.5 12.3 psum.14
  1170.9 35.4 %psum.15 = f32[4384]{0:T(1024)S(1)} all-reduce(f32[4384]{0:T(1024)S(1)} %psum.14), channel_id=1, replica_groups=mesh['head'=8,'row'=4] {'head'}, use_global_device_ids=true, to_apply=%region_44.45 | all-reduce | flops 4384 | bytes 35072 | tf_op jit(solution)/shard_map/psum | solution.py:668
  1206.8 85.9 %ring_scatter_head.3 = f32[256,2048]{1,0:T(8,128)} custom-call(bf16[2048,2048]{1,0:T(8,128)(2,1)} %get-tuple-element.286.y_ref), custom_call_target="tpu_custom_call" | custom-call | tf_op jit(solution)/shard_map/ring_scatter_head/pallas_call | solution.py:454
  (569 shorter events, 437.1 us)
Async XLA Ops:
  7.2 106.8 %all-gather.7.cloned.1.call-start = ((), (), s32[]{:S(2)}) async-start(), calls=%async_computation.6 | async-start | bytes 2621440 | tf_op jit(solution)/shard_map/all_gather | solution.py:543
  9.5 116.7 %all-gather.9.cloned.1.call-start = ((), (), s32[]{:S(2)}) async-start(), calls=%async_computation.7 | async-start | bytes 8519680 | tf_op jit(solution)/shard_map/all_gather | solution.py:533
  14.7 452.5 %all-gather.15.cloned.1.call-start = ((), (), s32[]{:S(2)}) async-start(), calls=%async_computation.15 | async-start | bytes 5242880 | tf_op jit(solution)/shard_map/all_gather | solution.py:547
  15.5 451.8 %all-gather.11.cloned.1.call-start = ((), (), s32[]{:S(2)}) async-start(), calls=%async_computation.8 | async-start | bytes 19464192 | tf_op jit(solution)/shard_map/all_gather | solution.py:550
  114.0 488.7 %all-gather.13.cloned.1.call-start = ((), (), s32[]{:S(2)}) async-start(), calls=%async_computation.9 | async-start | bytes 5242880 | tf_op jit(solution)/shard_map/all_gather | solution.py:586
  122.2 339.5 %copy-start.103 = (f32[2048]{0:T(1024)}, f32[2048]{0:T(1024)S(1)}, u32[]{:S(2)}) copy-start(f32[2048]{0:T(1024)S(1)} %fusion.81) | copy-start | bytes 24580
  123.5 228.5 %copy-start.117 = (f32[2,256]{1,0:T(2,128)}, f32[2,256]{1,0:T(2,128)S(1)}, u32[]{:S(2)}) copy-start(f32[2,256]{1,0:T(2,128)S(1)} %get-tuple-element.267) | copy-start | bytes 6148
  123.5 228.5 %copy-start.119 = (f32[2,256]{1,0:T(2,128)}, f32[2,256]{1,0:T(2,128)S(1)}, u32[]{:S(2)}) copy-start(f32[2,256]{1,0:T(2,128)S(1)} %get-tuple-element.270) | copy-start | bytes 6148
  123.5 228.5 %copy-start.121 = (f32[2,256]{1,0:T(2,128)}, f32[2,256]{1,0:T(2,128)S(1)}, u32[]{:S(2)}) copy-start(f32[2,256]{1,0:T(2,128)S(1)} %get-tuple-element.269) | copy-start | bytes 6148
  123.5 228.5 %copy-start.123 = (f32[2,256]{1,0:T(2,128)}, f32[2,256]{1,0:T(2,128)S(1)}, u32[]{:S(2)}) copy-start(f32[2,256]{1,0:T(2,128)S(1)} %get-tuple-element.268) | copy-start | bytes 6148
  123.6 243.3 %copy-start.101 = (f32[32,64]{1,0:T(8,128)}, f32[32,64]{1,0:T(8,128)S(1)}, u32[]{:S(2)}) copy-start(f32[32,64]{1,0:T(8,128)S(1)} %compare_convert_fusion) | copy-start | bytes 24580
  124.2 227.8 %copy-start.86 = (f32[2048]{0:T(1024)}, f32[2048]{0:T(1024)S(1)}, u32[]{:S(2)}) copy-start(f32[2048]{0:T(1024)S(1)} %get-tuple-element.261) | copy-start | bytes 24580
  124.2 227.8 %copy-start.88 = (f32[2048]{0:T(1024)}, f32[2048]{0:T(1024)S(1)}, u32[]{:S(2)}) copy-start(f32[2048]{0:T(1024)S(1)} %get-tuple-element.262) | copy-start | bytes 24580
  124.2 227.8 %copy-start.90 = (f32[2048]{0:T(1024)}, f32[2048]{0:T(1024)S(1)}, u32[]{:S(2)}) copy-start(f32[2048]{0:T(1024)S(1)} %get-tuple-element.263) | copy-start | bytes 24580
  149.8 218.4 %copy-start.66 = (f32[2,32,64]{2,1,0:T(8,128)}, f32[2,32,64]{2,1,0:T(8,128)S(1)}, u32[]{:S(2)}) copy-start(f32[2,32,64]{2,1,0:T(8,128)S(1)} %mul.969) | copy-start | bytes 49156
  151.9 215.0 %copy-start.76 = (f32[2,32,64]{2,1,0:T(8,128)}, f32[2,32,64]{2,1,0:T(8,128)S(1)}, u32[]{:S(2)}) copy-start(f32[2,32,64]{2,1,0:T(8,128)S(1)} %reduce_window_sum.22) | copy-start | bytes 49156
  174.5 193.1 %copy-start.5 = (f32[2,2048,128]{2,1,0:T(8,128)}, f32[2,2048,128]{2,1,0:T(8,128)S(1)}, u32[]{:S(2)}) copy-start(f32[2,2048,128]{2,1,0:T(8,128)S(1)} %get-tuple-element.195) | copy-start | bytes 6291460
  567.5 129.8 %copy-start.17 = (f32[256,2048]{1,0:T(8,128)}, f32[256,2048]{1,0:T(8,128)S(1)}, u32[]{:S(2)}) copy-start(f32[256,2048]{1,0:T(8,128)S(1)} %get-tuple-element.193) | copy-start | bytes 6291460
  569.0 125.7 %reduce-scatter.9.cloned.1.call-start = ((), (), s32[]{:S(2)}) async-start(), calls=%async_computation.10 | async-start | bytes 5242880 | tf_op jit(solution)/shard_map/reduce_scatter | solution.py:599
  650.1 423.7 %reduce-scatter.11.cloned.1.call-start = ((), (), s32[]{:S(2)}) async-start(), calls=%async_computation.11 | async-start | bytes 5242880 | tf_op jit(solution)/shard_map/reduce_scatter | solution.py:614
  661.1 419.1 %reduce-scatter.13.cloned.1.call-start = ((), (), s32[]{:S(2)}) async-start(), calls=%async_computation.12 | async-start | bytes 19464192 | tf_op jit(solution)/shard_map/reduce_scatter | solution.py:616
  788.6 504.1 %reduce-scatter.15.cloned.1.call-start = ((), (), s32[]{:S(2)}) async-start(), calls=%async_computation.13 | async-start | bytes 2621440 | tf_op jit(solution)/shard_map/reduce_scatter | solution.py:619
  1046.3 257.6 %reduce-scatter.19.cloned.1.call-start = ((), (), s32[]{:S(2)}) async-start(), calls=%async_computation.16 | async-start | bytes 327680
  1081.4 224.7 %reduce-scatter.17.cloned.1.call-start = ((), (), s32[]{:S(2)}) async-start(), calls=%async_computation.14 | async-start | bytes 7905280 | tf_op jit(solution)/shard_map/reduce_scatter | solution.py:644
  (152 other events, 1727.3 us)
Sparse Core Ops, SparseCore 0:
  10.2 25.2 all-gather.6
  37.6 49.3 all-gather.8
  88.6 34.5 all-gather.14
  124.5 334.2 all-gather.10
  569.1 33.6 all-gather.12
  650.2 44.4 reduce-scatter.8
  697.4 44.4 reduce-scatter.10
  788.7 291.4 reduce-scatter.12
  1082.9 30.4 reduce-scatter.14
  1116.3 20.0 reduce-scatter.18
  1139.1 59.1 reduce-scatter.16

commit v8 on v4

--- a/solution.py
+++ b/solution.py
@@ -200,6 +200,71 @@
 state_recurrence.defvjp(_recurrence_fwd, _recurrence_bwd)
 
 
+def _unit_lower_inverse_small(system):
+    size = system.shape[-1]
+    strict = system - jnp.eye(size, dtype=system.dtype)
+    power = -strict
+    inverse = jnp.eye(size, dtype=system.dtype) + power
+    done = 2
+    while done < size:
+        power = jnp.matmul(power, power, precision=precise)
+        inverse = inverse + jnp.matmul(power, inverse, precision=precise)
+        done *= 2
+    return inverse
+
+
+def _unit_lower_inverse_forward(system):
+    size = system.shape[-1]
+    base = min(8, size)
+    lead = system.shape[:-2]
+    count = size // base
+    blocks = system.reshape(lead + (count, base, count, base))
+    diag = jnp.stack([blocks[..., i, :, i, :] for i in range(count)], axis=-3)
+    inverse = _unit_lower_inverse_small(diag)
+    width = base
+    while width < size:
+        pairs = inverse.shape[-3] // 2
+        upper = inverse[..., 0::2, :, :]
+        lower = inverse[..., 1::2, :, :]
+        below = jnp.stack(
+            [
+                system[..., (2 * i + 1) * width : (2 * i + 2) * width, 2 * i * width : (2 * i + 1) * width]
+                for i in range(pairs)
+            ],
+            axis=-3,
+        )
+        corner = -jnp.matmul(
+            lower, jnp.matmul(below, upper, precision=precise), precision=precise
+        )
+        zeros = jnp.zeros_like(upper)
+        top = jnp.concatenate([upper, zeros], axis=-1)
+        bottom = jnp.concatenate([corner, lower], axis=-1)
+        inverse = jnp.concatenate([top, bottom], axis=-2)
+        width *= 2
+    return inverse[..., 0, :, :]
+
+
+@jax.custom_vjp
+def unit_lower_inverse(system):
+    return _unit_lower_inverse_forward(system)
+
+
+def _inverse_fwd(system):
+    inverse = _unit_lower_inverse_forward(system)
+    return inverse, inverse
+
+
+def _inverse_bwd(inverse, grad):
+    size = inverse.shape[-1]
+    flipped = jnp.swapaxes(inverse, -1, -2)
+    full = -jnp.matmul(jnp.matmul(flipped, grad, precision=precise), flipped, precision=precise)
+    places = jnp.arange(size)
+    return (full * (places[:, None] > places[None, :]).astype(full.dtype),)
+
+
+unit_lower_inverse.defvjp(_inverse_fwd, _inverse_bwd)
+
+
 def chunk_prepare(queries, keys_n, values, decays, beta_rate, seg_ids):
     length, dk = keys_n.shape
     count = length // BLOCK
@@ -220,9 +285,7 @@
     key_gram = jnp.einsum("nid,njd->nij", k, k, precision=precise)
     system = jnp.eye(BLOCK, dtype=jnp.float32) + beta[:, :, None] * strict * key_gram
     right_side = jnp.concatenate([beta[:, :, None] * v, (beta * carried)[:, :, None] * k], axis=2)
-    solved = lax.linalg.triangular_solve(
-        system, right_side, left_side=True, lower=True, unit_diagonal=True
-    )
+    solved = jnp.matmul(unit_lower_inverse(system), right_side, precision=precise)
     dv = v.shape[2]
     kt = within[:, BLOCK - 1, :, None] * k
     scores = jnp.einsum("nid,njd->nij", q, k, precision=precise) * within

time: 1320 us -> 1310 us (level)
  other arithmetic: 295 us -> 142 us
  waiting for transfers between devices: 42.3 us -> 155 us
  matrix products: 293 us -> 324 us
    another operation x13 -> x9, other arithmetic: 137 us -> 1.44 us  [the longest x4 134 us: chunk_prepare(): lax.linalg.triangular_solve(system, right_side, left_side=True, lower=Tru...]
    all_gather x1, waiting for transfers between devices: 0.02 us -> 93.6 us  [on_device(): ffn_all = lax.all_gather(ffn_local, 'head', axis=0, tiled=True)]
    dot_general x1 -> x15, matrix products: 11.6 us -> 64.8 us  [the longest x3 25.7 us: chunk_prepare(): jnp.matmul(unit_lower_inverse(system), right_side, precision=precise)]
    reduce_scatter x1, waiting for transfers between devices: 16.5 us -> 35.6 us  [on_device(): lax.psum_scatter(ffn_grad_cat, 'head', scatter_dimension=0, tiled=True)]
    unnamed x340 -> x414, local copies, waits for them, and re-layouts: 38.3 us -> 56.8 us
    another operation x3 -> x0, matrix products: 18.2 us -> none  [chunk_prepare(): lax.linalg.triangular_solve(system, right_side, left_side=True, lower=Tru...]
    add x0 -> x1, local copies, waits for them, and re-layouts: none -> 16.5 us  [chunk_prepare(): jnp.eye(BLOCK, dtype=jnp.float32) + beta[:, :, None] * strict * key_gram]
    another operation x8 -> x7, local copies, waits for them, and re-layouts: 15.9 us -> 1.07 us  [the longest x2 0.67 us: _unit_lower_inverse_forward(): jnp.stack([system[..., (2 * i + 1) * width:(2 * i + 2) * width, 2 * i * w...]
  transfers between devices with their start and end apart: 11 -> 11, of which waited for: 3 -> 4; matrix products, arithmetic and copies ran while one was open for 51% -> 41% of each run, Pallas kernels for 28% -> 28%
where the time goes in v8:
time: 1310 us
  Pallas kernels  456 us (35%)
  matrix products  324 us (25%)
  local copies, waits for them, and re-layouts  168 us (13%)
  waiting for transfers between devices  155 us (12%)
  other arithmetic  142 us (11%)
  blocking collectives  44.9 us (3%)
  between operations  17.2 us (1%)
    pallas_call x2, Pallas kernels, ring_scatter(): pl.pallas_call(partial(_ring_scatter_kernel, major, minor), out_shape=jax...  180 us
    pallas_call x2, Pallas kernels, ring_gather(): pl.pallas_call(partial(_ring_gather_kernel, major, minor), out_shape=jax....  180 us
    all_gather x1, waiting for transfers between devices, on_device(): ffn_all = lax.all_gather(ffn_local, 'head', axis=0, tiled=True)  93.6 us
    dot_general x5, matrix products, contract_cols(): lax.dot_general(left, right, (((1,), (1,)), ((), ())), preferred_element_...  59.8 us
    unnamed x414, local copies, waits for them, and re-layouts  56.8 us
    pallas_call x1, Pallas kernels, _recur_forward(): pl.pallas_call(partial(_recur_fwd_kernel, nb), grid=(heads, blocks), in_s...  49.3 us
    dot_general x5, matrix products, contract_rows(): lax.dot_general(left, right, (((0,), (0,)), ((), ())), preferred_element_...  47.6 us
    pallas_call x1, Pallas kernels, delta_rule(): states, updates = state_recurrence(u0, w, kt, c)  46.2 us
  transfers between devices with their start and end apart: 11, of which 4 were waited for; matrix products, arithmetic and copies ran while one was open for 41% of the time, Pallas kernels for 28%

profile of v8, /device:TPU:0, one launch (start us, length us, event | category | flops | bytes accessed | tf_op | source)
XLA Modules:
  0.0 1307.2 jit_solution(13083078984059124151)
XLA Ops:
  19.4 90.9 %ring_gather_head.2 = bf16[2048,2048]{1,0:T(8,128)(2,1)} custom-call(bf16[256,2048]{1,0:T(8,128)(2,1)} %fusion.38.x_ref), custom_call_target="tpu_custom_call" | custom-call | tf_op jit(solution)/shard_map/ring_gather_head/pallas_call | solution.py:498
  126.7 18.6 %fusion.171 = f32[2048,1540]{0,1:T(8,128)S(1)} fusion(bf16[2048,2048]{1,0:T(8,128)(2,1)} %ring_gather_head.2, bf16[2048,1540]{1,0:T(8,128)(2,1)} %all-gather.9.cloned.1.call-done), kind=kOutput, calls=%fused_computation.349 | convolution fusion | flops 12918456320 | bytes 27312128 | tf_op jit(solution)/shard_map/dot_general | solution.py:614
  179.5 16.5 %copy.227 = f32[2,32,64,64]{1,3,2,0:T(8,128)} copy(f32[2,32,64,64]{2,3,1,0:T(8,128)} %get-tuple-element.322) | data formatting | bytes 2097152 | tf_op jit(solution)/shard_map/jvp(vmap())/add | solution.py:286
  216.9 9.6 fusion.24
  282.2 49.3 %jvp_delta_state_forward_.1 = (f32[2,32,256,128]{3,2,1,0:T(8,128)}, f32[2,32,64,256]{3,2,1,0:T(8,128)}) custom-call(f32[2,32,64,256]{3,2,1,0:T(8,128)} %slice.360.u0_ref, f32[2,32,64,128]{3,2,1,0:T(8,128)} %slice.361.w_ref, f32[2,32,64,128]{3,2,1,0:T(8,128)} %get-tuple-element.221.kt_ref, f32[2,32,1,128]{3,2,1,0:T(1,128)} %broadcast_in_dim.34.c_ref), custom_call_target="tpu_custom_call" | custom-call | flops 3221225472 | bytes 20971520 | tf_op jit(solution)/shard_map/jvp(delta_state_forward)/pallas_call | solution.py:121
  365.3 93.6 %all-gather.11.cloned.1.call-done = bf16[2048,4224]{0,1:T(8,128)(2,1)} async-done(((bf16[256,4224]{0,1:T(8,128)(2,1)}), bf16[2048,4224]{0,1:T(8,128)(2,1)}) %all-gather.11.cloned.1.call-update) | async-done | bytes 17301520 | tf_op jit(solution)/shard_map/all_gather | solution.py:613
  467.2 89.8 %ring_scatter_head.2 = f32[256,2048]{1,0:T(8,128)} custom-call(bf16[2048,2048]{1,0:T(8,128)(2,1)} %convolution_convert_fusion.4.y_ref), custom_call_target="tpu_custom_call" | custom-call | tf_op jit(solution)/shard_map/ring_scatter_head/pallas_call | solution.py:517
  560.5 12.0 fusion.17
  572.4 21.7 %all-gather.13.cloned.1.call-done = bf16[1024,2048]{1,0:T(8,128)(2,1)} async-done(((bf16[256,2048]{1,0:T(8,128)(2,1)}), bf16[1024,2048]{1,0:T(8,128)(2,1)}) %all-gather.13.cloned.1.call-update) | async-done | bytes 4194320 | tf_op jit(solution)/shard_map/all_gather | solution.py:649
  594.1 12.0 fusion.9
  606.1 14.6 %multiply_convert_fusion = (bf16[1024,1408]{1,0:T(8,128)(2,1)}, bf16[1024,1408]{1,0:T(8,128)(2,1)S(1)}, bf16[1024,1408]{1,0:T(8,128)(2,1)}) fusion(f32[1024,1408]{1,0:T(8,128)} %fusion.9, f32[1024,1408]{1,0:T(8,128)} %fusion.17, bf16[1024,2048]{1,0:T(8,128)(2,1)S(1)} %copy-done.182, bf16[2048,4224]{0,1:T(8,128)(2,1)} %all-gather.11.cloned.1.call-done), kind=kOutput, calls=%fused_computation.17 | convolution fusion | flops 5928648704 | bytes 30146560 | tf_op jit(solution)/shard_map/dot_general | solution.py:651
  620.7 9.8 fusion.7
  630.6 10.8 add_convert_fusion
  641.4 10.9 fusion.29
  690.9 88.8 %ring_gather_head.3 = bf16[2048,2048]{1,0:T(8,128)(2,1)} custom-call(bf16[256,2048]{1,0:T(8,128)(2,1)} %fusion.147.x_ref), custom_call_target="tpu_custom_call" | custom-call | tf_op jit(solution)/shard_map/ring_gather_head/pallas_call | solution.py:498
  809.9 17.8 %fusion.25.ds_ref = f32[2,32,256,128]{3,2,1,0:T(8,128)} fusion(f32[2,32,64,128]{3,2,1,0:T(8,128)S(1)} %bitcast.323, f32[2,32,64,256]{3,2,1,0:T(8,128)S(1)} %bitcast.315, f32[2,32,64]{2,1,0:T(8,128)S(1)} %copy-done.90), kind=kOutput, calls=%fused_computation.68 | convolution fusion | flops 1611661312 | bytes 14696448 | tf_op jit(solution)/shard_map/transpose(jvp(vmap(nid,nvd->niv)))/dot_general | solution.py:298
  827.7 46.2 %transpose_jvp_delta_state_backward__.1 = (f32[2,32,64,256]{3,2,1,0:T(8,128)}, f32[2,32,64,128]{3,2,1,0:T(8,128)}, f32[2,32,64,128]{3,2,1,0:T(8,128)}, f32[2,32,1,128]{3,2,1,0:T(1,128)}) custom-call(f32[2,32,256,128]{3,2,1,0:T(8,128)} %get-tuple-element.51.s_ref, f32[2,32,64,256]{3,2,1,0:T(8,128)} %get-tuple-element.52.u_ref, ...), custom_call_target="tpu_custom_call" | custom-call | flops 6442450944 | bytes 41943040 | tf_op jit(solution)/shard_map/transpose(jvp(delta_state_backward))/pallas_call | solution.py:309
  900.5 10.8 fusion.4
  1036.0 35.6 %reduce-scatter.13.cloned.1.call-done = bf16[256,4224]{0,1:T(8,128)(2,1)} async-done(((bf16[2048,4224]{0,1:T(8,128)(2,1)}), bf16[256,4224]{0,1:T(8,128)(2,1)}) %reduce-scatter.13.cloned.1.call-update) | async-done | bytes 2162704 | tf_op jit(solution)/shard_map/reduce_scatter | solution.py:679
  1072.8 23.9 %concatenate.133 = bf16[2048,1540]{0,1:T(8,128)(2,1)} concatenate(bf16[2048,256]{0,1:T(8,128)(2,1)S(1)} %bitcast.335, bf16[2048,256]{0,1:T(8,128)(2,1)} %bitcast.336, bf16[2048,512]{0,1:T(8,128)(2,1)S(1)} %bitcast.330, bf16[2048,512]{0,1:T(8,128)(2,1)} %bitcast.333, bf16[2048,2]{0,1:T(2,128)(2,1)S(1)} %bitcast.346, bf16[2048,2]{0,1:T(2,128)(2,1)S(1)} %fusion.112), dimensions={1} | concatenate | bytes 12615680 | tf_op jit(solution)/shard_map/concatenate | solution.py:694
  1096.6 19.2 %convolution_convert_fusion.5 = bf16[2048,1540]{0,1:T(8,128)(2,1)} fusion(bf16[2048,2048]{1,0:T(8,128)(2,1)} %ring_gather_head.2, bf16[2048,1540]{0,1:T(8,128)(2,1)} %concatenate.133), kind=kOutput, calls=%fused_computation.8 | convolution fusion | flops 12921610240 | bytes 21004288 | tf_op jit(solution)/shard_map/dot_general | solution.py:548
  1115.9 21.0 %convolution_convert_fusion.y_ref = bf16[2048,2048]{1,0:T(8,128)(2,1)} fusion(bf16[2048,1540]{0,1:T(8,128)(2,1)} %concatenate.133, bf16[2048,1540]{1,0:T(8,128)(2,1)} %all-gather.9.cloned.1.call-done), kind=kOutput, calls=%fused_computation.3 | convolution fusion | flops 12922650624 | bytes 21004288 | tf_op jit(solution)/shard_map/dot_general | solution.py:554
  1136.9 90.5 %ring_scatter_head.3 = f32[256,2048]{1,0:T(8,128)} custom-call(bf16[2048,2048]{1,0:T(8,128)(2,1)} %convolution_convert_fusion.y_ref), custom_call_target="tpu_custom_call" | custom-call | tf_op jit(solution)/shard_map/ring_scatter_head/pallas_call | solution.py:517
  1230.4 39.8 %all-reduce.39 = (f32[16]{0:T(128)}, f32[16]{0:T(128)}, f32[256]{0:T(256)}, f32[2048]{0:T(1024)}, f32[2048]{0:T(1024)}) all-reduce(f32[16]{0:T(128)S(1)} %dynamic_update_slice.6, f32[16]{0:T(128)S(1)} %dynamic_update_slice.7, f32[256]{0:T(256)S(1)} %copy-done.171, ...), channel_id=1, replica_groups=mesh['head'=8,'row'=4] {'head','row'}, use_global_device_ids=true, to_apply=%region_41.42 | all-reduce | flops 4384 | bytes 35072 | tf_op jit(solution)/shard_map/psum | solution.py:726
  (633 shorter events, 436.3 us)
Async XLA Ops:
  7.2 106.0 %all-gather.7.cloned.1.call-start = ((), (), s32[]{:S(2)}) async-start(), calls=%async_computation.6 | async-start | bytes 2621440 | tf_op jit(solution)/shard_map/all_gather | solution.py:606
  9.5 117.2 %all-gather.9.cloned.1.call-start = ((), (), s32[]{:S(2)}) async-start(), calls=%async_computation.7 | async-start | bytes 8519680 | tf_op jit(solution)/shard_map/all_gather | solution.py:596
  13.5 351.8 %all-gather.15.cloned.1.call-start = ((), (), s32[]{:S(2)}) async-start(), calls=%async_computation.15 | async-start | bytes 5242880 | tf_op jit(solution)/shard_map/all_gather | solution.py:610
  14.2 444.6 %all-gather.11.cloned.1.call-start = ((), (), s32[]{:S(2)}) async-start(), calls=%async_computation.8 | async-start | bytes 19464192 | tf_op jit(solution)/shard_map/all_gather | solution.py:613
  113.2 480.9 %all-gather.13.cloned.1.call-start = ((), (), s32[]{:S(2)}) async-start(), calls=%async_computation.9 | async-start | bytes 5242880 | tf_op jit(solution)/shard_map/all_gather | solution.py:649
  126.7 220.3 %copy-start.13 = (f32[32,64,64]{1,2,0:T(8,128)}, f32[32,64,64]{1,2,0:T(8,128)S(1)}, u32[]{:S(2)}) copy-start(f32[32,64,64]{1,2,0:T(8,128)S(1)} %get-tuple-element.291) | copy-start | bytes 1572868
  126.7 220.3 %copy-start.40 = (pred[32,64,64]{1,2,0:T(8,128)(4,1)}, pred[32,64,64]{1,2,0:T(8,128)(4,1)S(1)}, u32[]{:S(2)}) copy-start(pred[32,64,64]{1,2,0:T(8,128)(4,1)S(1)} %get-tuple-element.290) | copy-start | bytes 393220
  150.0 118.1 %copy-start.79 = (f32[2,32,64]{2,1,0:T(8,128)}, f32[2,32,64]{2,1,0:T(8,128)S(1)}, u32[]{:S(2)}) copy-start(f32[2,32,64]{2,1,0:T(8,128)S(1)} %mul.977) | copy-start | bytes 49156
  163.7 183.3 %copy-start.65 = (f32[2,32,64]{2,1,0:T(8,128)}, f32[2,32,64]{2,1,0:T(8,128)S(1)}, u32[]{:S(2)}) copy-start(f32[2,32,64]{2,1,0:T(8,128)S(1)} %reduce_window_sum.22) | copy-start | bytes 49156
  174.3 159.6 %copy-start.6 = (f32[2,2048,128]{2,1,0:T(8,128)}, f32[2,2048,128]{2,1,0:T(8,128)S(1)}, u32[]{:S(2)}) copy-start(f32[2,2048,128]{2,1,0:T(8,128)S(1)} %get-tuple-element.222) | copy-start | bytes 6291460
  365.2 101.9 %copy-start.81 = (bf16[2,2048,256]{1,2,0:T(8,128)(2,1)}, bf16[2,2048,256]{1,2,0:T(8,128)(2,1)S(1)}, u32[]{:S(2)}) copy-start(bf16[2,2048,256]{1,2,0:T(8,128)(2,1)S(1)} %multiply_multiply_fusion) | copy-start | bytes 6291460
  558.9 129.7 %copy-start.20 = (f32[256,2048]{1,0:T(8,128)}, f32[256,2048]{1,0:T(8,128)S(1)}, u32[]{:S(2)}) copy-start(f32[256,2048]{1,0:T(8,128)S(1)} %get-tuple-element.220) | copy-start | bytes 6291460
  558.9 129.7 %copy-start.136 = (f32[256]{0:T(256)}, f32[256]{0:T(256)S(1)}, u32[]{:S(2)}) copy-start(f32[256]{0:T(256)S(1)} %fusion.128) | copy-start | bytes 3076
  560.4 125.6 %reduce-scatter.9.cloned.1.call-start = ((), (), s32[]{:S(2)}) async-start(), calls=%async_computation.10 | async-start | bytes 5242880 | tf_op jit(solution)/shard_map/reduce_scatter | solution.py:662
  641.4 394.6 %reduce-scatter.11.cloned.1.call-start = ((), (), s32[]{:S(2)}) async-start(), calls=%async_computation.11 | async-start | bytes 5242880 | tf_op jit(solution)/shard_map/reduce_scatter | solution.py:677
  652.4 419.1 %reduce-scatter.13.cloned.1.call-start = ((), (), s32[]{:S(2)}) async-start(), calls=%async_computation.12 | async-start | bytes 19464192 | tf_op jit(solution)/shard_map/reduce_scatter | solution.py:679
  779.8 447.7 %reduce-scatter.15.cloned.1.call-start = ((), (), s32[]{:S(2)}) async-start(), calls=%async_computation.13 | async-start | bytes 2621440 | tf_op jit(solution)/shard_map/reduce_scatter | solution.py:682
  1007.7 281.7 %reduce-scatter.19.cloned.1.call-start = ((), (), s32[]{:S(2)}) async-start(), calls=%async_computation.16 | async-start | bytes 327680
  1072.7 218.9 %reduce-scatter.17.cloned.1.call-start = ((), (), s32[]{:S(2)}) async-start(), calls=%async_computation.14 | async-start | bytes 7905280 | tf_op jit(solution)/shard_map/reduce_scatter | solution.py:703
  1136.9 90.7 %copy-start.181 = (f32[2]{0:T(128)S(1)}, f32[2]{0:T(128)}, u32[]{:S(2)}) copy-start(f32[2]{0:T(128)} %get-tuple-element.76) | copy-start | bytes 28
  1136.9 90.9 %copy-start.180 = (f32[2]{0:T(128)S(1)}, f32[2]{0:T(128)}, u32[]{:S(2)}) copy-start(f32[2]{0:T(128)} %negate_multiply_fusion.1) | copy-start | bytes 28
  1136.9 91.1 %copy-start.44 = (bf16[1,256,2048]{2,1,0:T(8,128)(2,1)S(1)}, bf16[1,256,2048]{2,1,0:T(8,128)(2,1)}, u32[]{:S(2)}) copy-start(bf16[1,256,2048]{2,1,0:T(8,128)(2,1)} %param.22) | copy-start | bytes 3145732
  1136.9 91.1 %copy-start.130 = (f32[2048]{0:T(1024)S(1)}, f32[2048]{0:T(1024)}, u32[]{:S(2)}) copy-start(f32[2048]{0:T(1024)} %param.36) | copy-start | bytes 24580
  1136.9 91.1 %copy-start.150 = (f32[256]{0:T(256)S(1)}, f32[256]{0:T(256)}, u32[]{:S(2)}) copy-start(f32[256]{0:T(256)} %copy-done.149) | copy-start | bytes 3076
  (179 other events, 1491.7 us)
Sparse Core Ops, SparseCore 0:
  10.2 25.3 all-gather.6
  37.7 49.2 all-gather.8
  88.6 34.5 all-gather.14
  124.5 334.2 all-gather.10
  560.5 33.5 all-gather.12
  641.5 44.4 reduce-scatter.8
  688.7 44.4 reduce-scatter.10
  780.0 291.5 reduce-scatter.12
  1074.2 30.4 reduce-scatter.14
  1107.6 20.0 reduce-scatter.18
  1130.4 58.5 reduce-scatter.16

commit v9 on v8

--- a/solution.py
+++ b/solution.py
@@ -605,7 +605,8 @@
     ]
     out_matrix = lax.all_gather(w_out.astype(jnp.bfloat16), "row", axis=1, tiled=True)
     ff_width = w_gate.shape[1]
-    ffn_local = jnp.concatenate([w_gate, w_up, w_down.T], axis=1).astype(jnp.bfloat16)
+    ffn_local = jnp.concatenate([w_gate, w_up], axis=1).astype(jnp.bfloat16)
+    down_local = w_down.T.astype(jnp.bfloat16)
     grad_out = cotangent[0]
     grad_out_rows = lax.all_gather(grad_out, "row", axis=0, tiled=True)
     all_rows = ring_gather(normed_one, ring, 0)
@@ -633,10 +634,12 @@
         dt_here,
         o_gain,
     )
-    mixed, ffn_all, grad_out_rows = lax.optimization_barrier((mixed, ffn_all, grad_out_rows))
+    mixed, ffn_all, grad_out_rows, down_local = lax.optimization_barrier(
+        (mixed, ffn_all, grad_out_rows, down_local)
+    )
+    w_down_t = ring_gather(down_local, ring, 4)
     w_gate_all = ffn_all[:, :ff_width]
     w_up_all = ffn_all[:, ff_width : 2 * ff_width]
-    w_down_t = ffn_all[:, 2 * ff_width :]
     mixed_half = mixed.astype(jnp.bfloat16)
     mixer_output = ring_scatter(
         jnp.dot(mixed_half, out_matrix, preferred_element_type=jnp.float32).astype(jnp.bfloat16),

time: 1310 us -> 1250 us (0.954)
  waiting for transfers between devices: 155 us -> 37.5 us
  Pallas kernels: 456 us -> 519 us
    all_gather x1, waiting for transfers between devices: 93.6 us -> 0.02 us  [on_device(): ffn_all = lax.all_gather(ffn_local, 'head', axis=0, tiled=True)]
    pallas_call x2 -> x3, Pallas kernels: 180 us -> 246 us  [ring_gather(): pl.pallas_call(partial(_ring_gather_kernel, major, minor), out_shape=jax....]
    all_gather x1, waiting for transfers between devices: 21.7 us -> 0.01 us  [on_device(): ffn_inputs = lax.all_gather(normed_two, 'row', axis=0, tiled=True)]
    unnamed x414 -> x415, local copies, waits for them, and re-layouts: 56.8 us -> 55.9 us
  transfers between devices with their start and end apart: 11 -> 11, of which waited for: 4 -> 2; matrix products, arithmetic and copies ran while one was open for 41% -> 43% of each run, Pallas kernels for 28% -> 35%
where the time goes in v9:
time: 1250 us
  Pallas kernels  519 us (42%)
  matrix products  326 us (26%)
  local copies, waits for them, and re-layouts  157 us (13%)
  other arithmetic  143 us (11%)
  blocking collectives  45.8 us (4%)
  waiting for transfers between devices  37.5 us (3%)
  between operations  17.3 us (1%)
    pallas_call x3, Pallas kernels, ring_gather(): pl.pallas_call(partial(_ring_gather_kernel, major, minor), out_shape=jax....  246 us
    pallas_call x2, Pallas kernels, ring_scatter(): pl.pallas_call(partial(_ring_scatter_kernel, major, minor), out_shape=jax...  178 us
    dot_general x5, matrix products, contract_cols(): lax.dot_general(left, right, (((1,), (1,)), ((), ())), preferred_element_...  60.2 us
    unnamed x415, local copies, waits for them, and re-layouts  55.9 us
    pallas_call x1, Pallas kernels, _recur_forward(): pl.pallas_call(partial(_recur_fwd_kernel, nb), grid=(heads, blocks), in_s...  49.3 us
    dot_general x5, matrix products, contract_rows(): lax.dot_general(left, right, (((0,), (0,)), ((), ())), preferred_element_...  47.6 us
    pallas_call x1, Pallas kernels, delta_rule(): states, updates = state_recurrence(u0, w, kt, c)  46.2 us
    psum x1, blocking collectives, on_device(): lax.psum((grad_gain_in, grad_gain_ffn, core_grads[11], grad_a_full, grad_...  39.7 us
  transfers between devices with their start and end apart: 11, of which 2 were waited for; matrix products, arithmetic and copies ran while one was open for 43% of the time, Pallas kernels for 35%

profile of v9, /device:TPU:0, one launch (start us, length us, event | category | flops | bytes accessed | tf_op | source)
XLA Modules:
  0.0 1245.4 jit_solution(9943740562249040066)
XLA Ops:
  28.9 91.6 %ring_gather_head.3 = bf16[2048,2048]{1,0:T(8,128)(2,1)} custom-call(bf16[256,2048]{1,0:T(8,128)(2,1)} %fusion.31.x_ref), custom_call_target="tpu_custom_call" | custom-call | tf_op jit(solution)/shard_map/ring_gather_head/pallas_call | solution.py:498
  127.7 18.2 %fusion.164 = f32[2048,1540]{0,1:T(8,128)S(1)} fusion(bf16[2048,2048]{1,0:T(8,128)(2,1)} %ring_gather_head.3, bf16[2048,1540]{1,0:T(8,128)(2,1)} %all-gather.9.cloned.1.call-done), kind=kOutput, calls=%fused_computation.345 | convolution fusion | flops 12918456320 | bytes 27312128 | tf_op jit(solution)/shard_map/dot_general | solution.py:615
  207.2 9.4 fusion.20
  272.1 49.3 %jvp_delta_state_forward_.1 = (f32[2,32,256,128]{3,2,1,0:T(8,128)}, f32[2,32,64,256]{3,2,1,0:T(8,128)}) custom-call(f32[2,32,64,256]{3,2,1,0:T(8,128)} %slice.356.u0_ref, f32[2,32,64,128]{3,2,1,0:T(8,128)} %slice.357.w_ref, f32[2,32,64,128]{3,2,1,0:T(8,128)} %get-tuple-element.223.kt_ref, f32[2,32,1,128]{3,2,1,0:T(1,128)} %broadcast_in_dim.34.c_ref), custom_call_target="tpu_custom_call" | custom-call | flops 3221225472 | bytes 20971520 | tf_op jit(solution)/shard_map/jvp(delta_state_forward)/pallas_call | solution.py:121
  327.5 9.5 fusion.166
  364.1 87.7 %ring_scatter_head.2 = f32[256,2048]{1,0:T(8,128)} custom-call(bf16[2048,2048]{1,0:T(8,128)(2,1)} %convolution_convert_fusion.4.y_ref), custom_call_target="tpu_custom_call" | custom-call | tf_op jit(solution)/shard_map/ring_scatter_head/pallas_call | solution.py:517
  455.3 65.1 %ring_gather_head.4 = bf16[2048,1408]{1,0:T(8,128)(2,1)} custom-call(bf16[256,1408]{1,0:T(8,128)(2,1)} %bitcast.340), custom_call_target="tpu_custom_call" | custom-call | tf_op jit(solution)/shard_map/ring_gather_head/pallas_call | solution.py:498
  520.4 11.9 fusion.168
  532.3 11.9 fusion.9
  544.2 16.5 %multiply_convert_fusion = (bf16[1024,1408]{1,0:T(8,128)(2,1)}, bf16[1024,1408]{1,0:T(8,128)(2,1)}, bf16[1024,1408]{1,0:T(8,128)(2,1)}) fusion(f32[1024,1408]{1,0:T(8,128)} %fusion.9, f32[1024,1408]{1,0:T(8,128)} %fusion.168, bf16[1024,2048]{1,0:T(8,128)(2,1)} %all-gather.13.cloned.1.call-done, bf16[2048,2816]{1,0:T(8,128)(2,1)} %all-gather.11.cloned.1.call-done), kind=kOutput, calls=%fused_computation.17 | convolution fusion | flops 5928648704 | bytes 30146560 | tf_op jit(solution)/shard_map/dot_general | solution.py:654
  560.8 10.5 fusion.7
  571.2 10.5 add_convert_fusion
  581.8 11.0 convolution_convert_fusion.6
  592.9 9.5 convolution_convert_fusion.1
  629.2 88.9 %ring_gather_head.5 = bf16[2048,2048]{1,0:T(8,128)(2,1)} custom-call(bf16[256,2048]{1,0:T(8,128)(2,1)} %fusion.140.x_ref), custom_call_target="tpu_custom_call" | custom-call | tf_op jit(solution)/shard_map/ring_gather_head/pallas_call | solution.py:498
  748.2 17.9 %fusion.21.ds_ref = f32[2,32,256,128]{3,2,1,0:T(8,128)} fusion(f32[2,32,64,128]{3,2,1,0:T(8,128)S(1)} %bitcast.326, f32[2,32,64,256]{3,2,1,0:T(8,128)S(1)} %bitcast.318, f32[2,32,64]{2,1,0:T(8,128)S(1)} %copy-done.90), kind=kOutput, calls=%fused_computation.64 | convolution fusion | flops 1611661312 | bytes 14696448 | tf_op jit(solution)/shard_map/transpose(jvp(vmap(nid,nvd->niv)))/dot_general | solution.py:298
  766.0 46.2 %transpose_jvp_delta_state_backward__.1 = (f32[2,32,64,256]{3,2,1,0:T(8,128)}, f32[2,32,64,128]{3,2,1,0:T(8,128)}, f32[2,32,64,128]{3,2,1,0:T(8,128)}, f32[2,32,1,128]{3,2,1,0:T(1,128)}) custom-call(f32[2,32,256,128]{3,2,1,0:T(8,128)} %get-tuple-element.52.s_ref, f32[2,32,64,256]{3,2,1,0:T(8,128)} %get-tuple-element.53.u_ref, ...), custom_call_target="tpu_custom_call" | custom-call | flops 6442450944 | bytes 41943040 | tf_op jit(solution)/shard_map/transpose(jvp(delta_state_backward))/pallas_call | solution.py:309
  838.8 10.8 fusion.4
  974.2 35.5 %reduce-scatter.13.cloned.1.call-done = bf16[256,4224]{0,1:T(8,128)(2,1)} async-done(((bf16[2048,4224]{0,1:T(8,128)(2,1)}), bf16[256,4224]{0,1:T(8,128)(2,1)}) %reduce-scatter.13.cloned.1.call-update) | async-done | bytes 2162704 | tf_op jit(solution)/shard_map/reduce_scatter | solution.py:682
  1010.9 23.9 %concatenate.133 = bf16[2048,1540]{0,1:T(8,128)(2,1)} concatenate(bf16[2048,256]{0,1:T(8,128)(2,1)S(1)} %bitcast.338, bf16[2048,256]{0,1:T(8,128)(2,1)} %bitcast.339, bf16[2048,512]{0,1:T(8,128)(2,1)S(1)} %bitcast.333, bf16[2048,512]{0,1:T(8,128)(2,1)} %bitcast.336, bf16[2048,2]{0,1:T(2,128)(2,1)S(1)} %bitcast.350, bf16[2048,2]{0,1:T(2,128)(2,1)S(1)} %fusion.105), dimensions={1} | concatenate | bytes 12615680 | tf_op jit(solution)/shard_map/concatenate | solution.py:697
  1034.8 19.2 %convolution_convert_fusion.5 = bf16[2048,1540]{0,1:T(8,128)(2,1)} fusion(bf16[2048,2048]{1,0:T(8,128)(2,1)} %ring_gather_head.3, bf16[2048,1540]{0,1:T(8,128)(2,1)} %concatenate.133), kind=kOutput, calls=%fused_computation.8 | convolution fusion | flops 12921610240 | bytes 21004288 | tf_op jit(solution)/shard_map/dot_general | solution.py:548
  1054.0 21.0 %convolution_convert_fusion.y_ref = bf16[2048,2048]{1,0:T(8,128)(2,1)} fusion(bf16[2048,1540]{0,1:T(8,128)(2,1)} %concatenate.133, bf16[2048,1540]{1,0:T(8,128)(2,1)} %all-gather.9.cloned.1.call-done), kind=kOutput, calls=%fused_computation.3 | convolution fusion | flops 12922650624 | bytes 21004288 | tf_op jit(solution)/shard_map/dot_general | solution.py:554
  1075.1 90.6 %ring_scatter_head.3 = f32[256,2048]{1,0:T(8,128)} custom-call(bf16[2048,2048]{1,0:T(8,128)(2,1)} %convolution_convert_fusion.y_ref), custom_call_target="tpu_custom_call" | custom-call | tf_op jit(solution)/shard_map/ring_scatter_head/pallas_call | solution.py:517
  1168.6 39.7 %all-reduce.39 = (f32[16]{0:T(128)}, f32[16]{0:T(128)}, f32[256]{0:T(256)}, f32[2048]{0:T(1024)}, f32[2048]{0:T(1024)}) all-reduce(f32[16]{0:T(128)S(1)} %dynamic_update_slice.6, f32[16]{0:T(128)S(1)} %dynamic_update_slice.7, f32[256]{0:T(256)S(1)} %copy-done.171, ...), channel_id=1, replica_groups=mesh['head'=8,'row'=4] {'head','row'}, use_global_device_ids=true, to_apply=%region_41.42 | all-reduce | flops 4384 | bytes 35072 | tf_op jit(solution)/shard_map/psum | solution.py:729
  (637 shorter events, 421.9 us)
Async XLA Ops:
  7.2 120.1 %all-gather.7.cloned.1.call-start = ((), (), s32[]{:S(2)}) async-start(), calls=%async_computation.6 | async-start | bytes 2621440 | tf_op jit(solution)/shard_map/all_gather | solution.py:606
  9.5 118.2 %all-gather.9.cloned.1.call-start = ((), (), s32[]{:S(2)}) async-start(), calls=%async_computation.7 | async-start | bytes 8519680 | tf_op jit(solution)/shard_map/all_gather | solution.py:596
  13.5 341.5 %all-gather.15.cloned.1.call-start = ((), (), s32[]{:S(2)}) async-start(), calls=%async_computation.15 | async-start | bytes 5242880 | tf_op jit(solution)/shard_map/all_gather | solution.py:611
  14.2 340.8 %all-gather.11.cloned.1.call-start = ((), (), s32[]{:S(2)}) async-start(), calls=%async_computation.8 | async-start | bytes 12976128 | tf_op jit(solution)/shard_map/all_gather | solution.py:614
  27.6 92.9 %copy-start.167 = (f32[256]{0:T(256)}, f32[256]{0:T(256)S(1)}, u32[]{:S(2)}) copy-start(f32[256]{0:T(256)S(1)} %fusion.42) | copy-start | bytes 3076
  27.6 92.9 %copy-start.149 = (f32[256]{0:T(256)}, f32[256]{0:T(256)S(1)}, u32[]{:S(2)}) copy-start(f32[256]{0:T(256)S(1)} %fusion.120) | copy-start | bytes 3076
  28.9 91.6 %copy-start.184 = (f32[16]{0:T(128)S(1)}, f32[16]{0:T(128)}, u32[]{:S(2)}) copy-start(f32[16]{0:T(128)} %param.33) | copy-start | bytes 196
  28.9 91.7 %copy-start.179 = (f32[16]{0:T(128)S(1)}, f32[16]{0:T(128)}, u32[]{:S(2)}) copy-start(f32[16]{0:T(128)} %param.32) | copy-start | bytes 196
  126.0 211.0 %copy-start.13 = (f32[32,64,64]{1,2,0:T(8,128)}, f32[32,64,64]{1,2,0:T(8,128)S(1)}, u32[]{:S(2)}) copy-start(f32[32,64,64]{1,2,0:T(8,128)S(1)} %get-tuple-element.293) | copy-start | bytes 1572868
  126.0 211.0 %copy-start.40 = (pred[32,64,64]{1,2,0:T(8,128)(4,1)}, pred[32,64,64]{1,2,0:T(8,128)(4,1)S(1)}, u32[]{:S(2)}) copy-start(pred[32,64,64]{1,2,0:T(8,128)(4,1)S(1)} %get-tuple-element.292) | copy-start | bytes 393220
  127.3 405.0 %all-gather.13.cloned.1.call-start = ((), (), s32[]{:S(2)}) async-start(), calls=%async_computation.9 | async-start | bytes 5242880 | tf_op jit(solution)/shard_map/all_gather | solution.py:652
  150.6 107.4 %copy-start.79 = (f32[2,32,64]{2,1,0:T(8,128)}, f32[2,32,64]{2,1,0:T(8,128)S(1)}, u32[]{:S(2)}) copy-start(f32[2,32,64]{2,1,0:T(8,128)S(1)} %mul.977) | copy-start | bytes 49156
  164.4 172.6 %copy-start.65 = (f32[2,32,64]{2,1,0:T(8,128)}, f32[2,32,64]{2,1,0:T(8,128)S(1)}, u32[]{:S(2)}) copy-start(f32[2,32,64]{2,1,0:T(8,128)S(1)} %reduce_window_sum.22) | copy-start | bytes 49156
  175.0 148.9 %copy-start.6 = (f32[2,2048,128]{2,1,0:T(8,128)}, f32[2,2048,128]{2,1,0:T(8,128)S(1)}, u32[]{:S(2)}) copy-start(f32[2,2048,128]{2,1,0:T(8,128)S(1)} %get-tuple-element.224) | copy-start | bytes 6291460
  453.8 173.1 %copy-start.20 = (f32[256,2048]{1,0:T(8,128)}, f32[256,2048]{1,0:T(8,128)S(1)}, u32[]{:S(2)}) copy-start(f32[256,2048]{1,0:T(8,128)S(1)} %get-tuple-element.222) | copy-start | bytes 6291460
  453.8 173.1 %copy-start.136 = (f32[256]{0:T(256)}, f32[256]{0:T(256)S(1)}, u32[]{:S(2)}) copy-start(f32[256]{0:T(256)S(1)} %fusion.121) | copy-start | bytes 3076
  455.3 169.1 %reduce-scatter.9.cloned.1.call-start = ((), (), s32[]{:S(2)}) async-start(), calls=%async_computation.10 | async-start | bytes 5242880 | tf_op jit(solution)/shard_map/reduce_scatter | solution.py:665
  581.7 392.4 %reduce-scatter.11.cloned.1.call-start = ((), (), s32[]{:S(2)}) async-start(), calls=%async_computation.11 | async-start | bytes 5242880 | tf_op jit(solution)/shard_map/reduce_scatter | solution.py:680
  592.8 416.9 %reduce-scatter.13.cloned.1.call-start = ((), (), s32[]{:S(2)}) async-start(), calls=%async_computation.12 | async-start | bytes 19464192 | tf_op jit(solution)/shard_map/reduce_scatter | solution.py:682
  718.1 447.6 %reduce-scatter.15.cloned.1.call-start = ((), (), s32[]{:S(2)}) async-start(), calls=%async_computation.13 | async-start | bytes 2621440 | tf_op jit(solution)/shard_map/reduce_scatter | solution.py:685
  945.9 281.6 %reduce-scatter.19.cloned.1.call-start = ((), (), s32[]{:S(2)}) async-start(), calls=%async_computation.16 | async-start | bytes 327680
  1010.9 218.9 %reduce-scatter.17.cloned.1.call-start = ((), (), s32[]{:S(2)}) async-start(), calls=%async_computation.14 | async-start | bytes 7905280 | tf_op jit(solution)/shard_map/reduce_scatter | solution.py:706
  1075.0 91.2 %copy-start.44 = (bf16[1,256,2048]{2,1,0:T(8,128)(2,1)S(1)}, bf16[1,256,2048]{2,1,0:T(8,128)(2,1)}, u32[]{:S(2)}) copy-start(bf16[1,256,2048]{2,1,0:T(8,128)(2,1)} %param.22) | copy-start | bytes 3145732
  1075.0 91.2 %copy-start.130 = (f32[2048]{0:T(1024)S(1)}, f32[2048]{0:T(1024)}, u32[]{:S(2)}) copy-start(f32[2048]{0:T(1024)} %param.36) | copy-start | bytes 24580
  (180 other events, 1804.7 us)
Sparse Core Ops, SparseCore 0:
  10.2 25.2 all-gather.6
  37.7 49.3 all-gather.8
  88.6 34.4 all-gather.14
  127.5 162.5 all-gather.10
  455.4 33.6 all-gather.12
  581.9 42.4 reduce-scatter.8
  627.0 44.5 reduce-scatter.10
  718.2 291.4 reduce-scatter.12
  1012.4 30.4 reduce-scatter.14
  1045.8 20.0 reduce-scatter.18
  1068.6 58.5 reduce-scatter.16

commit v10 on v9

--- a/solution.py
+++ b/solution.py
@@ -684,21 +684,20 @@
     grad_wout = contract_rows(mixed_half, grad_mid_rows).astype(jnp.bfloat16)
     wout_grad = lax.psum_scatter(grad_wout, "row", scatter_dimension=1, tiled=True)
     core_grads = pull_core(grad_mixed)
-    core_grads, ffn_output, ffn_grad_all = lax.optimization_barrier(
-        (core_grads, ffn_output, ffn_grad_all)
-    )
+    core_grads, ffn_output = lax.optimization_barrier((core_grads, ffn_output))
     final_out = (middle + ffn_output.astype(jnp.float32)).astype(jnp.bfloat16)
+    grad_proj = jnp.concatenate(
+        [core_grads[0], core_grads[1], core_grads[2], core_grads[3], core_grads[4], core_grads[5]],
+        axis=1,
+    ).astype(jnp.bfloat16)
+    grad_inward = contract_rows(all_rows, grad_proj).astype(jnp.bfloat16)
+    grad_inward, ffn_grad_all = lax.optimization_barrier((grad_inward, ffn_grad_all))
     ffn_grad_all = ffn_grad_all.astype(jnp.float32)
     ffn_grads = (
         ffn_grad_all[:, :ff_width],
         ffn_grad_all[:, ff_width : 2 * ff_width],
         ffn_grad_all[:, 2 * ff_width :].T,
     )
-    grad_proj = jnp.concatenate(
-        [core_grads[0], core_grads[1], core_grads[2], core_grads[3], core_grads[4], core_grads[5]],
-        axis=1,
-    ).astype(jnp.bfloat16)
-    grad_inward = contract_rows(all_rows, grad_proj).astype(jnp.bfloat16)
     grad_norm_one = ring_scatter(contract_cols(grad_proj, w_inward).astype(jnp.bfloat16), ring, 3)
     grad_norm_one, wout_grad = lax.optimization_barrier((grad_norm_one, wout_grad))
     grad_in_part, grad_gain_in = pull_one(grad_norm_one)

time: 1250 us -> 1220 us (0.976)
  waiting for transfers between devices: 37.5 us -> 2.17 us
    reduce_scatter x1, waiting for transfers between devices: 35.5 us -> 0.01 us  [on_device(): lax.psum_scatter(ffn_grad_cat, 'head', scatter_dimension=0, tiled=True)]
    unnamed x415 -> x413, local copies, waits for them, and re-layouts: 55.9 us -> 53.4 us
  transfers between devices with their start and end apart: 11 -> 11, of which waited for: 2 -> 1; matrix products, arithmetic and copies ran while one was open for 43% -> 44% of each run, Pallas kernels for 35% -> 36%
where the time goes in v10:
time: 1220 us; the launch traced here: 1210 us
  Pallas kernels  518 us (42%)
  matrix products  329 us (27%)
  local copies, waits for them, and re-layouts  157 us (13%)
  other arithmetic  139 us (11%)
  blocking collectives  46.9 us (4%)
  between operations  17.3 us (1%)
    pallas_call x3, Pallas kernels, ring_gather(): pl.pallas_call(partial(_ring_gather_kernel, major, minor), out_shape=jax....  248 us
    pallas_call x2, Pallas kernels, ring_scatter(): pl.pallas_call(partial(_ring_scatter_kernel, major, minor), out_shape=jax...  175 us
    dot_general x5, matrix products, contract_cols(): lax.dot_general(left, right, (((1,), (1,)), ((), ())), preferred_element_...  60.1 us
    unnamed x413, local copies, waits for them, and re-layouts  53.4 us
    dot_general x5, matrix products, contract_rows(): lax.dot_general(left, right, (((0,), (0,)), ((), ())), preferred_element_...  52.1 us
    pallas_call x1, Pallas kernels, _recur_forward(): pl.pallas_call(partial(_recur_fwd_kernel, nb), grid=(heads, blocks), in_s...  49.3 us
    pallas_call x1, Pallas kernels, delta_rule(): states, updates = state_recurrence(u0, w, kt, c)  46.3 us
    psum x1, blocking collectives, on_device(): lax.psum((grad_gain_in, grad_gain_ffn, core_grads[11], grad_a_full, grad_...  40.8 us
  transfers between devices with their start and end apart: 11, of which 1 were waited for; matrix products, arithmetic and copies ran while one was open for 44% of the time, Pallas kernels for 36%

profile of v10, /device:TPU:0, one launch (start us, length us, event | category | flops | bytes accessed | tf_op | source)
XLA Modules:
  0.0 1210.3 jit_solution(8588392191232517249)
XLA Ops:
  28.9 91.6 %ring_gather_head.3 = bf16[2048,2048]{1,0:T(8,128)(2,1)} custom-call(bf16[256,2048]{1,0:T(8,128)(2,1)} %fusion.31.x_ref), custom_call_target="tpu_custom_call" | custom-call | tf_op jit(solution)/shard_map/ring_gather_head/pallas_call | solution.py:498
  127.7 18.2 %fusion.164 = f32[2048,1540]{0,1:T(8,128)S(1)} fusion(bf16[2048,2048]{1,0:T(8,128)(2,1)} %ring_gather_head.3, bf16[2048,1540]{1,0:T(8,128)(2,1)} %all-gather.9.cloned.1.call-done), kind=kOutput, calls=%fused_computation.345 | convolution fusion | flops 12918456320 | bytes 27312128 | tf_op jit(solution)/shard_map/dot_general | solution.py:615
  207.4 9.5 fusion.20
  272.2 49.3 %jvp_delta_state_forward_.1 = (f32[2,32,256,128]{3,2,1,0:T(8,128)}, f32[2,32,64,256]{3,2,1,0:T(8,128)}) custom-call(f32[2,32,64,256]{3,2,1,0:T(8,128)} %slice.356.u0_ref, f32[2,32,64,128]{3,2,1,0:T(8,128)} %slice.357.w_ref, f32[2,32,64,128]{3,2,1,0:T(8,128)} %get-tuple-element.225.kt_ref, f32[2,32,1,128]{3,2,1,0:T(1,128)} %broadcast_in_dim.34.c_ref), custom_call_target="tpu_custom_call" | custom-call | flops 3221225472 | bytes 20971520 | tf_op jit(solution)/shard_map/jvp(delta_state_forward)/pallas_call | solution.py:121
  327.6 9.5 fusion.166
  364.8 88.1 %ring_scatter_head.2 = f32[256,2048]{1,0:T(8,128)} custom-call(bf16[2048,2048]{1,0:T(8,128)(2,1)} %convolution_convert_fusion.4.y_ref), custom_call_target="tpu_custom_call" | custom-call | tf_op jit(solution)/shard_map/ring_scatter_head/pallas_call | solution.py:517
  456.4 67.7 %ring_gather_head.4 = bf16[2048,1408]{1,0:T(8,128)(2,1)} custom-call(bf16[256,1408]{1,0:T(8,128)(2,1)} %bitcast.340), custom_call_target="tpu_custom_call" | custom-call | tf_op jit(solution)/shard_map/ring_gather_head/pallas_call | solution.py:498
  524.2 11.9 fusion.168
  536.1 11.9 fusion.9
  548.0 16.6 %multiply_convert_fusion = (bf16[1024,1408]{1,0:T(8,128)(2,1)}, bf16[1024,1408]{1,0:T(8,128)(2,1)}, bf16[1024,1408]{1,0:T(8,128)(2,1)}) fusion(f32[1024,1408]{1,0:T(8,128)} %fusion.9, f32[1024,1408]{1,0:T(8,128)} %fusion.168, bf16[1024,2048]{1,0:T(8,128)(2,1)} %all-gather.13.cloned.1.call-done, bf16[2048,2816]{1,0:T(8,128)(2,1)} %all-gather.11.cloned.1.call-done), kind=kOutput, calls=%fused_computation.17 | convolution fusion | flops 5928648704 | bytes 30146560 | tf_op jit(solution)/shard_map/dot_general | solution.py:654
  564.6 10.4 fusion.7
  575.0 10.5 add_convert_fusion
  585.6 11.0 convolution_convert_fusion.6
  596.7 9.5 convolution_convert_fusion.1
  633.2 88.9 %ring_gather_head.5 = bf16[2048,2048]{1,0:T(8,128)(2,1)} custom-call(bf16[256,2048]{1,0:T(8,128)(2,1)} %fusion.140.x_ref), custom_call_target="tpu_custom_call" | custom-call | tf_op jit(solution)/shard_map/ring_gather_head/pallas_call | solution.py:498
  752.2 17.9 %fusion.21.ds_ref = f32[2,32,256,128]{3,2,1,0:T(8,128)} fusion(f32[2,32,64,128]{3,2,1,0:T(8,128)S(1)} %bitcast.327, f32[2,32,64,256]{3,2,1,0:T(8,128)S(1)} %bitcast.319, f32[2,32,64]{2,1,0:T(8,128)S(1)} %copy-done.85), kind=kOutput, calls=%fused_computation.64 | convolution fusion | flops 1611661312 | bytes 14696448 | tf_op jit(solution)/shard_map/transpose(jvp(vmap(nid,nvd->niv)))/dot_general | solution.py:298
  770.0 46.3 %transpose_jvp_delta_state_backward__.1 = (f32[2,32,64,256]{3,2,1,0:T(8,128)}, f32[2,32,64,128]{3,2,1,0:T(8,128)}, f32[2,32,64,128]{3,2,1,0:T(8,128)}, f32[2,32,1,128]{3,2,1,0:T(1,128)}) custom-call(f32[2,32,256,128]{3,2,1,0:T(8,128)} %get-tuple-element.53.s_ref, f32[2,32,64,256]{3,2,1,0:T(8,128)} %get-tuple-element.54.u_ref, ...), custom_call_target="tpu_custom_call" | custom-call | flops 6442450944 | bytes 41943040 | tf_op jit(solution)/shard_map/transpose(jvp(delta_state_backward))/pallas_call | solution.py:309
  845.0 10.8 fusion.4
  972.1 10.1 convolution_convert_fusion.7
  982.3 23.9 %concatenate.133 = bf16[2048,1540]{0,1:T(8,128)(2,1)} concatenate(bf16[2048,256]{0,1:T(8,128)(2,1)S(1)} %bitcast.338, bf16[2048,256]{0,1:T(8,128)(2,1)} %bitcast.339, bf16[2048,512]{0,1:T(8,128)(2,1)S(1)} %bitcast.333, bf16[2048,512]{0,1:T(8,128)(2,1)} %bitcast.336, bf16[2048,2]{0,1:T(2,128)(2,1)S(1)} %bitcast.350, bf16[2048,2]{0,1:T(2,128)(2,1)S(1)} %fusion.105), dimensions={1} | concatenate | bytes 12615680 | tf_op jit(solution)/shard_map/concatenate | solution.py:689
  1006.3 19.3 %convolution_convert_fusion.5 = bf16[2048,1540]{0,1:T(8,128)(2,1)} fusion(bf16[2048,2048]{1,0:T(8,128)(2,1)} %ring_gather_head.3, bf16[2048,1540]{0,1:T(8,128)(2,1)} %concatenate.133), kind=kOutput, calls=%fused_computation.8 | convolution fusion | flops 12921610240 | bytes 21004288 | tf_op jit(solution)/shard_map/dot_general | solution.py:548
  1025.6 21.0 %convolution_convert_fusion.y_ref = bf16[2048,2048]{1,0:T(8,128)(2,1)} fusion(bf16[2048,1540]{0,1:T(8,128)(2,1)} %concatenate.133, bf16[2048,1540]{1,0:T(8,128)(2,1)} %all-gather.9.cloned.1.call-done), kind=kOutput, calls=%fused_computation.3 | convolution fusion | flops 12922650624 | bytes 21004288 | tf_op jit(solution)/shard_map/dot_general | solution.py:554
  1046.6 86.4 %ring_scatter_head.3 = f32[256,2048]{1,0:T(8,128)} custom-call(bf16[2048,2048]{1,0:T(8,128)(2,1)} %convolution_convert_fusion.y_ref), custom_call_target="tpu_custom_call" | custom-call | tf_op jit(solution)/shard_map/ring_scatter_head/pallas_call | solution.py:517
  1138.2 40.8 %all-reduce.39 = (f32[16]{0:T(128)}, f32[16]{0:T(128)}, f32[256]{0:T(256)}, f32[2048]{0:T(1024)}, f32[2048]{0:T(1024)}) all-reduce(f32[16]{0:T(128)S(1)} %dynamic_update_slice.6, f32[16]{0:T(128)S(1)} %dynamic_update_slice.7, f32[256]{0:T(256)S(1)} %copy-done.169, ...), channel_id=1, replica_groups=mesh['head'=8,'row'=4] {'head','row'}, use_global_device_ids=true, to_apply=%region_41.42 | all-reduce | flops 4384 | bytes 35072 | tf_op jit(solution)/shard_map/psum | solution.py:728
  (635 shorter events, 411.8 us)
Async XLA Ops:
  7.2 120.1 %all-gather.7.cloned.1.call-start = ((), (), s32[]{:S(2)}) async-start(), calls=%async_computation.6 | async-start | bytes 2621440 | tf_op jit(solution)/shard_map/all_gather | solution.py:606
  9.5 118.2 %all-gather.9.cloned.1.call-start = ((), (), s32[]{:S(2)}) async-start(), calls=%async_computation.7 | async-start | bytes 8519680 | tf_op jit(solution)/shard_map/all_gather | solution.py:596
  13.5 342.3 %all-gather.15.cloned.1.call-start = ((), (), s32[]{:S(2)}) async-start(), calls=%async_computation.15 | async-start | bytes 5242880 | tf_op jit(solution)/shard_map/all_gather | solution.py:611
  14.2 341.5 %all-gather.11.cloned.1.call-start = ((), (), s32[]{:S(2)}) async-start(), calls=%async_computation.8 | async-start | bytes 12976128 | tf_op jit(solution)/shard_map/all_gather | solution.py:614
  27.6 92.9 %copy-start.165 = (f32[256]{0:T(256)}, f32[256]{0:T(256)S(1)}, u32[]{:S(2)}) copy-start(f32[256]{0:T(256)S(1)} %fusion.42) | copy-start | bytes 3076
  27.6 92.9 %copy-start.147 = (f32[256]{0:T(256)}, f32[256]{0:T(256)S(1)}, u32[]{:S(2)}) copy-start(f32[256]{0:T(256)S(1)} %fusion.120) | copy-start | bytes 3076
  28.9 91.6 %copy-start.183 = (f32[16]{0:T(128)S(1)}, f32[16]{0:T(128)}, u32[]{:S(2)}) copy-start(f32[16]{0:T(128)} %param.33) | copy-start | bytes 196
  28.9 91.7 %copy-start.179 = (f32[16]{0:T(128)S(1)}, f32[16]{0:T(128)}, u32[]{:S(2)}) copy-start(f32[16]{0:T(128)} %param.32) | copy-start | bytes 196
  126.0 211.2 %copy-start.13 = (f32[32,64,64]{1,2,0:T(8,128)}, f32[32,64,64]{1,2,0:T(8,128)S(1)}, u32[]{:S(2)}) copy-start(f32[32,64,64]{1,2,0:T(8,128)S(1)} %get-tuple-element.295) | copy-start | bytes 1572868
  126.0 211.2 %copy-start.40 = (pred[32,64,64]{1,2,0:T(8,128)(4,1)}, pred[32,64,64]{1,2,0:T(8,128)(4,1)S(1)}, u32[]{:S(2)}) copy-start(pred[32,64,64]{1,2,0:T(8,128)(4,1)S(1)} %get-tuple-element.294) | copy-start | bytes 393220
  127.4 408.7 %all-gather.13.cloned.1.call-start = ((), (), s32[]{:S(2)}) async-start(), calls=%async_computation.9 | async-start | bytes 5242880 | tf_op jit(solution)/shard_map/all_gather | solution.py:652
  150.7 107.6 %copy-start.75 = (f32[2,32,64]{2,1,0:T(8,128)}, f32[2,32,64]{2,1,0:T(8,128)S(1)}, u32[]{:S(2)}) copy-start(f32[2,32,64]{2,1,0:T(8,128)S(1)} %mul.977) | copy-start | bytes 49156
  164.5 172.7 %copy-start.61 = (f32[2,32,64]{2,1,0:T(8,128)}, f32[2,32,64]{2,1,0:T(8,128)S(1)}, u32[]{:S(2)}) copy-start(f32[2,32,64]{2,1,0:T(8,128)S(1)} %reduce_window_sum.22) | copy-start | bytes 49156
  175.2 148.9 %copy-start.6 = (f32[2,2048,128]{2,1,0:T(8,128)}, f32[2,2048,128]{2,1,0:T(8,128)S(1)}, u32[]{:S(2)}) copy-start(f32[2,2048,128]{2,1,0:T(8,128)S(1)} %get-tuple-element.226) | copy-start | bytes 6291460
  455.0 176.0 %copy-start.21 = (f32[256,2048]{1,0:T(8,128)}, f32[256,2048]{1,0:T(8,128)S(1)}, u32[]{:S(2)}) copy-start(f32[256,2048]{1,0:T(8,128)S(1)} %get-tuple-element.224) | copy-start | bytes 6291460
  455.0 176.0 %copy-start.133 = (f32[256]{0:T(256)}, f32[256]{0:T(256)S(1)}, u32[]{:S(2)}) copy-start(f32[256]{0:T(256)S(1)} %fusion.121) | copy-start | bytes 3076
  456.4 172.0 %reduce-scatter.9.cloned.1.call-start = ((), (), s32[]{:S(2)}) async-start(), calls=%async_computation.10 | async-start | bytes 5242880 | tf_op jit(solution)/shard_map/reduce_scatter | solution.py:665
  585.5 385.3 %reduce-scatter.11.cloned.1.call-start = ((), (), s32[]{:S(2)}) async-start(), calls=%async_computation.11 | async-start | bytes 5242880 | tf_op jit(solution)/shard_map/reduce_scatter | solution.py:680
  596.6 429.0 %reduce-scatter.15.cloned.1.call-start = ((), (), s32[]{:S(2)}) async-start(), calls=%async_computation.13 | async-start | bytes 19464192 | tf_op jit(solution)/shard_map/reduce_scatter | solution.py:682
  722.1 411.4 %reduce-scatter.19.cloned.1.call-start = ((), (), s32[]{:S(2)}) async-start(), calls=%async_computation.16 | async-start | bytes 327680
  972.1 163.6 %reduce-scatter.13.cloned.1.call-start = ((), (), s32[]{:S(2)}) async-start(), calls=%async_computation.12 | async-start | bytes 2621440 | tf_op jit(solution)/shard_map/reduce_scatter | solution.py:685
  982.3 212.4 %reduce-scatter.17.cloned.1.call-start = ((), (), s32[]{:S(2)}) async-start(), calls=%async_computation.14 | async-start | bytes 7905280 | tf_op jit(solution)/shard_map/reduce_scatter | solution.py:705
  1046.6 89.1 %copy-start.123 = (f32[2048]{0:T(1024)S(1)}, f32[2048]{0:T(1024)}, u32[]{:S(2)}) copy-start(f32[2048]{0:T(1024)} %param.36) | copy-start | bytes 24580
  1046.6 89.1 %copy-start.148 = (f32[256]{0:T(256)S(1)}, f32[256]{0:T(256)}, u32[]{:S(2)}) copy-start(f32[256]{0:T(256)} %copy-done.147) | copy-start | bytes 3076
  (179 other events, 1791.1 us)
Sparse Core Ops, SparseCore 0:
  10.2 25.2 all-gather.6
  37.7 49.3 all-gather.8
  88.6 34.4 all-gather.14
  127.5 162.5 all-gather.10
  456.5 32.8 all-gather.12
  585.7 42.6 reduce-scatter.8
  631.0 44.5 reduce-scatter.10
  722.2 291.4 reduce-scatter.14
  1016.9 19.0 reduce-scatter.18
  1038.4 31.4 reduce-scatter.12
  1072.6 58.5 reduce-scatter.16

commit v11 on v10

--- a/solution.py
+++ b/solution.py
@@ -610,8 +610,11 @@
     grad_out = cotangent[0]
     grad_out_rows = lax.all_gather(grad_out, "row", axis=0, tiled=True)
     all_rows = ring_gather(normed_one, ring, 0)
-    all_rows, out_matrix, ffn_local = lax.optimization_barrier((all_rows, out_matrix, ffn_local))
+    all_rows, out_matrix, ffn_local, down_local = lax.optimization_barrier(
+        (all_rows, out_matrix, ffn_local, down_local)
+    )
     ffn_all = lax.all_gather(ffn_local, "head", axis=0, tiled=True)
+    down_all = lax.all_gather(down_local, "head", axis=0, tiled=True)
     projected = jnp.dot(all_rows, w_inward, preferred_element_type=jnp.float32)
     proj_parts = [projected[:, edges[spot] : edges[spot + 1]] for spot in range(6)]
     seg_ids = segments[0]
@@ -634,10 +637,9 @@
         dt_here,
         o_gain,
     )
-    mixed, ffn_all, grad_out_rows, down_local = lax.optimization_barrier(
-        (mixed, ffn_all, grad_out_rows, down_local)
-    )
-    w_down_t = ring_gather(down_local, ring, 4)
+    mixed, ffn_all, grad_out_rows, w_down_t = lax.optimization_barrier(
+        (mixed, ffn_all, grad_out_rows, down_all)
+    )
     w_gate_all = ffn_all[:, :ff_width]
     w_up_all = ffn_all[:, ff_width : 2 * ff_width]
     mixed_half = mixed.astype(jnp.bfloat16)

time: 1220 us -> 1200 us (0.984)
  Pallas kernels: 518 us -> 450 us
  waiting for transfers between devices: 2.17 us -> 53.8 us
    pallas_call x3 -> x2, Pallas kernels: 248 us -> 180 us  [ring_gather(): pl.pallas_call(partial(_ring_gather_kernel, major, minor), out_shape=jax....]
    all_gather x1, waiting for transfers between devices: 0.02 us -> 28 us  [on_device(): ffn_all = lax.all_gather(ffn_local, 'head', axis=0, tiled=True)]
    all_gather x1, waiting for transfers between devices: 0.01 us -> 21.7 us  [on_device(): ffn_inputs = lax.all_gather(normed_two, 'row', axis=0, tiled=True)]
    unnamed x413 -> x412, local copies, waits for them, and re-layouts: 53.4 us -> 52.7 us
  transfers between devices with their start and end apart: 11 -> 12, of which waited for: 1 -> 3; matrix products, arithmetic and copies ran while one was open for 44% -> 45% of each run, Pallas kernels for 36% -> 30%
where the time goes in v11:
time: 1200 us; the launch traced here: 1190 us
  Pallas kernels  450 us (38%)
  matrix products  328 us (27%)
  local copies, waits for them, and re-layouts  156 us (13%)
  other arithmetic  141 us (12%)
  waiting for transfers between devices  53.8 us (4%)
  blocking collectives  45.4 us (4%)
  between operations  17.6 us (1%)
    pallas_call x2, Pallas kernels, ring_gather(): pl.pallas_call(partial(_ring_gather_kernel, major, minor), out_shape=jax....  180 us
    pallas_call x2, Pallas kernels, ring_scatter(): pl.pallas_call(partial(_ring_scatter_kernel, major, minor), out_shape=jax...  175 us
    dot_general x5, matrix products, contract_cols(): lax.dot_general(left, right, (((1,), (1,)), ((), ())), preferred_element_...  60.2 us
    unnamed x412, local copies, waits for them, and re-layouts  52.7 us
    dot_general x5, matrix products, contract_rows(): lax.dot_general(left, right, (((0,), (0,)), ((), ())), preferred_element_...  52.2 us
    pallas_call x1, Pallas kernels, _recur_forward(): pl.pallas_call(partial(_recur_fwd_kernel, nb), grid=(heads, blocks), in_s...  49.3 us
    pallas_call x1, Pallas kernels, delta_rule(): states, updates = state_recurrence(u0, w, kt, c)  46.2 us
    psum x1, blocking collectives, on_device(): lax.psum((grad_gain_in, grad_gain_ffn, core_grads[11], grad_a_full, grad_...  40.2 us
  transfers between devices with their start and end apart: 12, of which 3 were waited for; matrix products, arithmetic and copies ran while one was open for 45% of the time, Pallas kernels for 30%

profile of v11, /device:TPU:0, one launch (start us, length us, event | category | flops | bytes accessed | tf_op | source)
XLA Modules:
  0.0 1193.6 jit_solution(2721904900371130332)
XLA Ops:
  19.1 91.2 %ring_gather_head.2 = bf16[2048,2048]{1,0:T(8,128)(2,1)} custom-call(bf16[256,2048]{1,0:T(8,128)(2,1)} %fusion.31.x_ref), custom_call_target="tpu_custom_call" | custom-call | tf_op jit(solution)/shard_map/ring_gather_head/pallas_call | solution.py:498
  127.7 18.2 %fusion.164 = f32[2048,1540]{0,1:T(8,128)S(1)} fusion(bf16[2048,2048]{1,0:T(8,128)(2,1)} %ring_gather_head.2, bf16[2048,1540]{1,0:T(8,128)(2,1)} %all-gather.10.cloned.1.call-done), kind=kOutput, calls=%fused_computation.345 | convolution fusion | flops 12918456320 | bytes 27312128 | tf_op jit(solution)/shard_map/dot_general | solution.py:618
  272.4 49.3 %jvp_delta_state_forward_.1 = (f32[2,32,256,128]{3,2,1,0:T(8,128)}, f32[2,32,64,256]{3,2,1,0:T(8,128)}) custom-call(f32[2,32,64,256]{3,2,1,0:T(8,128)} %slice.356.u0_ref, f32[2,32,64,128]{3,2,1,0:T(8,128)} %slice.357.w_ref, f32[2,32,64,128]{3,2,1,0:T(8,128)} %get-tuple-element.227.kt_ref, f32[2,32,1,128]{3,2,1,0:T(1,128)} %broadcast_in_dim.34.c_ref), custom_call_target="tpu_custom_call" | custom-call | flops 3221225472 | bytes 20971520 | tf_op jit(solution)/shard_map/jvp(delta_state_forward)/pallas_call | solution.py:121
  327.8 9.5 fusion.166
  356.0 28.0 %all-gather.12.cloned.1.call-done = bf16[2048,2816]{1,0:T(8,128)(2,1)} async-done(((bf16[256,2816]{1,0:T(8,128)(2,1)}), bf16[2048,2816]{1,0:T(8,128)(2,1)}) %all-gather.12.cloned.1.call-update) | async-done | bytes 11534352 | tf_op jit(solution)/shard_map/all_gather | solution.py:616
  392.5 87.6 %ring_scatter_head.2 = f32[256,2048]{1,0:T(8,128)} custom-call(bf16[2048,2048]{1,0:T(8,128)(2,1)} %convolution_convert_fusion.4.y_ref), custom_call_target="tpu_custom_call" | custom-call | tf_op jit(solution)/shard_map/ring_scatter_head/pallas_call | solution.py:517
  483.6 12.0 %fusion.168 = f32[1024,1408]{1,0:T(8,128)} fusion(bf16[1024,2048]{1,0:T(8,128)(2,1)} %bitcast.371, bf16[2048,1408]{0,1:T(8,128)(2,1)} %all-gather.14.cloned.1.call-done), kind=kOutput, calls=%fused_computation.349 | convolution fusion | flops 5905580032 | bytes 15728640 | tf_op jit(solution)/shard_map/dot_general | solution.py:660
  495.6 21.7 %all-gather.16.cloned.1.call-done = bf16[1024,2048]{1,0:T(8,128)(2,1)} async-done(((bf16[256,2048]{1,0:T(8,128)(2,1)}), bf16[1024,2048]{1,0:T(8,128)(2,1)}) %all-gather.16.cloned.1.call-update) | async-done | bytes 4194320 | tf_op jit(solution)/shard_map/all_gather | solution.py:654
  517.3 11.8 fusion.9
  529.1 16.5 %multiply_convert_fusion = (bf16[1024,1408]{1,0:T(8,128)(2,1)}, bf16[1024,1408]{1,0:T(8,128)(2,1)}, bf16[1024,1408]{1,0:T(8,128)(2,1)}) fusion(f32[1024,1408]{1,0:T(8,128)} %fusion.9, f32[1024,1408]{1,0:T(8,128)} %fusion.168, bf16[1024,2048]{1,0:T(8,128)(2,1)} %all-gather.16.cloned.1.call-done, bf16[2048,2816]{1,0:T(8,128)(2,1)} %all-gather.12.cloned.1.call-done), kind=kOutput, calls=%fused_computation.17 | convolution fusion | flops 5928648704 | bytes 30146560 | tf_op jit(solution)/shard_map/dot_general | solution.py:656
  545.6 10.5 fusion.7
  556.1 10.5 add_convert_fusion
  566.7 10.9 convolution_convert_fusion.6
  577.7 9.5 convolution_convert_fusion.1
  616.2 88.9 %ring_gather_head.3 = bf16[2048,2048]{1,0:T(8,128)(2,1)} custom-call(bf16[256,2048]{1,0:T(8,128)(2,1)} %fusion.140.x_ref), custom_call_target="tpu_custom_call" | custom-call | tf_op jit(solution)/shard_map/ring_gather_head/pallas_call | solution.py:498
  735.3 17.9 %fusion.21.ds_ref = f32[2,32,256,128]{3,2,1,0:T(8,128)} fusion(f32[2,32,64,128]{3,2,1,0:T(8,128)S(1)} %bitcast.326, f32[2,32,64,256]{3,2,1,0:T(8,128)S(1)} %bitcast.318, f32[2,32,64]{2,1,0:T(8,128)S(1)} %copy-done.85), kind=kOutput, calls=%fused_computation.64 | convolution fusion | flops 1611661312 | bytes 14696448 | tf_op jit(solution)/shard_map/transpose(jvp(vmap(nid,nvd->niv)))/dot_general | solution.py:298
  753.1 46.2 %transpose_jvp_delta_state_backward__.1 = (f32[2,32,64,256]{3,2,1,0:T(8,128)}, f32[2,32,64,128]{3,2,1,0:T(8,128)}, f32[2,32,64,128]{3,2,1,0:T(8,128)}, f32[2,32,1,128]{3,2,1,0:T(1,128)}) custom-call(f32[2,32,256,128]{3,2,1,0:T(8,128)} %get-tuple-element.54.s_ref, f32[2,32,64,256]{3,2,1,0:T(8,128)} %get-tuple-element.55.u_ref, ...), custom_call_target="tpu_custom_call" | custom-call | flops 6442450944 | bytes 41943040 | tf_op jit(solution)/shard_map/transpose(jvp(delta_state_backward))/pallas_call | solution.py:309
  828.0 10.8 fusion.4
  955.2 10.1 convolution_convert_fusion.7
  965.4 23.8 %concatenate.133 = bf16[2048,1540]{0,1:T(8,128)(2,1)} concatenate(bf16[2048,256]{0,1:T(8,128)(2,1)S(1)} %bitcast.337, bf16[2048,256]{0,1:T(8,128)(2,1)} %bitcast.338, bf16[2048,512]{0,1:T(8,128)(2,1)S(1)} %bitcast.332, bf16[2048,512]{0,1:T(8,128)(2,1)} %bitcast.335, bf16[2048,2]{0,1:T(2,128)(2,1)S(1)} %bitcast.348, bf16[2048,2]{0,1:T(2,128)(2,1)S(1)} %fusion.105), dimensions={1} | concatenate | bytes 12615680 | tf_op jit(solution)/shard_map/concatenate | solution.py:691
  989.2 19.3 %convolution_convert_fusion.5 = bf16[2048,1540]{0,1:T(8,128)(2,1)} fusion(bf16[2048,2048]{1,0:T(8,128)(2,1)} %ring_gather_head.2, bf16[2048,1540]{0,1:T(8,128)(2,1)} %concatenate.133), kind=kOutput, calls=%fused_computation.8 | convolution fusion | flops 12921610240 | bytes 21004288 | tf_op jit(solution)/shard_map/dot_general | solution.py:548
  1008.6 21.0 %convolution_convert_fusion.y_ref = bf16[2048,2048]{1,0:T(8,128)(2,1)} fusion(bf16[2048,1540]{0,1:T(8,128)(2,1)} %concatenate.133, bf16[2048,1540]{1,0:T(8,128)(2,1)} %all-gather.10.cloned.1.call-done), kind=kOutput, calls=%fused_computation.3 | convolution fusion | flops 12922650624 | bytes 21004288 | tf_op jit(solution)/shard_map/dot_general | solution.py:554
  1029.6 87.0 %ring_scatter_head.3 = f32[256,2048]{1,0:T(8,128)} custom-call(bf16[2048,2048]{1,0:T(8,128)(2,1)} %convolution_convert_fusion.y_ref), custom_call_target="tpu_custom_call" | custom-call | tf_op jit(solution)/shard_map/ring_scatter_head/pallas_call | solution.py:517
  1121.7 40.2 %all-reduce.39 = (f32[16]{0:T(128)}, f32[16]{0:T(128)}, f32[256]{0:T(256)}, f32[2048]{0:T(1024)}, f32[2048]{0:T(1024)}) all-reduce(f32[16]{0:T(128)S(1)} %dynamic_update_slice.6, f32[16]{0:T(128)S(1)} %dynamic_update_slice.7, f32[256]{0:T(256)S(1)} %copy-done.169, ...), channel_id=1, replica_groups=mesh['head'=8,'row'=4] {'head','row'}, use_global_device_ids=true, to_apply=%region_41.42 | all-reduce | flops 4384 | bytes 35072 | tf_op jit(solution)/shard_map/psum | solution.py:730
  (637 shorter events, 423.3 us)
Async XLA Ops:
  7.2 106.6 %all-gather.8.cloned.1.call-start = ((), (), s32[]{:S(2)}) async-start(), calls=%async_computation.6 | async-start | bytes 2621440 | tf_op jit(solution)/shard_map/all_gather | solution.py:606
  9.5 118.2 %all-gather.10.cloned.1.call-start = ((), (), s32[]{:S(2)}) async-start(), calls=%async_computation.7 | async-start | bytes 8519680 | tf_op jit(solution)/shard_map/all_gather | solution.py:596
  13.5 342.5 %all-gather.18.cloned.1.call-start = ((), (), s32[]{:S(2)}) async-start(), calls=%async_computation.16 | async-start | bytes 5242880 | tf_op jit(solution)/shard_map/all_gather | solution.py:611
  14.2 341.8 %all-gather.14.cloned.1.call-start = ((), (), s32[]{:S(2)}) async-start(), calls=%async_computation.9 | async-start | bytes 6488064 | tf_op jit(solution)/shard_map/all_gather | solution.py:617
  113.9 270.1 %all-gather.12.cloned.1.call-start = ((), (), s32[]{:S(2)}) async-start(), calls=%async_computation.8 | async-start | bytes 12976128 | tf_op jit(solution)/shard_map/all_gather | solution.py:616
  127.0 80.5 %copy-start.98 = (f32[2048]{0:T(1024)}, f32[2048]{0:T(1024)S(1)}, u32[]{:S(2)}) copy-start(f32[2048]{0:T(1024)S(1)} %get-tuple-element.307) | copy-start | bytes 24580
  127.3 210.1 %copy-start.13 = (f32[32,64,64]{1,2,0:T(8,128)}, f32[32,64,64]{1,2,0:T(8,128)S(1)}, u32[]{:S(2)}) copy-start(f32[32,64,64]{1,2,0:T(8,128)S(1)} %get-tuple-element.297) | copy-start | bytes 1572868
  127.3 210.1 %copy-start.40 = (pred[32,64,64]{1,2,0:T(8,128)(4,1)}, pred[32,64,64]{1,2,0:T(8,128)(4,1)S(1)}, u32[]{:S(2)}) copy-start(pred[32,64,64]{1,2,0:T(8,128)(4,1)S(1)} %get-tuple-element.296) | copy-start | bytes 393220
  127.3 389.9 %all-gather.16.cloned.1.call-start = ((), (), s32[]{:S(2)}) async-start(), calls=%async_computation.10 | async-start | bytes 5242880 | tf_op jit(solution)/shard_map/all_gather | solution.py:654
  150.7 107.8 %copy-start.75 = (f32[2,32,64]{2,1,0:T(8,128)}, f32[2,32,64]{2,1,0:T(8,128)S(1)}, u32[]{:S(2)}) copy-start(f32[2,32,64]{2,1,0:T(8,128)S(1)} %mul.977) | copy-start | bytes 49156
  164.5 172.9 %copy-start.61 = (f32[2,32,64]{2,1,0:T(8,128)}, f32[2,32,64]{2,1,0:T(8,128)S(1)}, u32[]{:S(2)}) copy-start(f32[2,32,64]{2,1,0:T(8,128)S(1)} %reduce_window_sum.22) | copy-start | bytes 49156
  175.1 149.2 %copy-start.6 = (f32[2,2048,128]{2,1,0:T(8,128)}, f32[2,2048,128]{2,1,0:T(8,128)S(1)}, u32[]{:S(2)}) copy-start(f32[2,2048,128]{2,1,0:T(8,128)S(1)} %get-tuple-element.228) | copy-start | bytes 6291460
  392.5 87.6 %copy-start.43 = (bf16[1,256,2048]{2,1,0:T(8,128)(2,1)S(1)}, bf16[1,256,2048]{2,1,0:T(8,128)(2,1)}, u32[]{:S(2)}) copy-start(bf16[1,256,2048]{2,1,0:T(8,128)(2,1)} %param.22) | copy-start | bytes 3145732
  482.1 131.8 %copy-start.21 = (f32[256,2048]{1,0:T(8,128)}, f32[256,2048]{1,0:T(8,128)S(1)}, u32[]{:S(2)}) copy-start(f32[256,2048]{1,0:T(8,128)S(1)} %get-tuple-element.226) | copy-start | bytes 6291460
  482.1 131.8 %copy-start.133 = (f32[256]{0:T(256)}, f32[256]{0:T(256)S(1)}, u32[]{:S(2)}) copy-start(f32[256]{0:T(256)S(1)} %fusion.121) | copy-start | bytes 3076
  483.6 127.8 %reduce-scatter.9.cloned.1.call-start = ((), (), s32[]{:S(2)}) async-start(), calls=%async_computation.11 | async-start | bytes 5242880 | tf_op jit(solution)/shard_map/reduce_scatter | solution.py:667
  566.6 387.3 %reduce-scatter.11.cloned.1.call-start = ((), (), s32[]{:S(2)}) async-start(), calls=%async_computation.12 | async-start | bytes 5242880 | tf_op jit(solution)/shard_map/reduce_scatter | solution.py:682
  577.6 431.0 %reduce-scatter.15.cloned.1.call-start = ((), (), s32[]{:S(2)}) async-start(), calls=%async_computation.14 | async-start | bytes 19464192 | tf_op jit(solution)/shard_map/reduce_scatter | solution.py:684
  705.2 411.8 %reduce-scatter.19.cloned.1.call-start = ((), (), s32[]{:S(2)}) async-start(), calls=%async_computation.17 | async-start | bytes 327680
  955.2 164.1 %reduce-scatter.13.cloned.1.call-start = ((), (), s32[]{:S(2)}) async-start(), calls=%async_computation.13 | async-start | bytes 2621440 | tf_op jit(solution)/shard_map/reduce_scatter | solution.py:687
  965.4 212.3 %reduce-scatter.17.cloned.1.call-start = ((), (), s32[]{:S(2)}) async-start(), calls=%async_computation.15 | async-start | bytes 7905280 | tf_op jit(solution)/shard_map/reduce_scatter | solution.py:707
  1029.6 89.7 %copy-start.44 = (bf16[1,256,2048]{2,1,0:T(8,128)(2,1)S(1)}, bf16[1,256,2048]{2,1,0:T(8,128)(2,1)}, u32[]{:S(2)}) copy-start(bf16[1,256,2048]{2,1,0:T(8,128)(2,1)} %param.22) | copy-start | bytes 3145732
  1029.6 89.7 %copy-start.123 = (f32[2048]{0:T(1024)S(1)}, f32[2048]{0:T(1024)}, u32[]{:S(2)}) copy-start(f32[2048]{0:T(1024)} %param.36) | copy-start | bytes 24580
  1029.6 89.7 %copy-start.148 = (f32[256]{0:T(256)S(1)}, f32[256]{0:T(256)}, u32[]{:S(2)}) copy-start(f32[256]{0:T(256)} %copy-done.147) | copy-start | bytes 3076
  (180 other events, 1569.9 us)
Sparse Core Ops, SparseCore 0:
  10.2 25.2 all-gather.7
  37.7 49.3 all-gather.9
  88.6 34.5 all-gather.17
  125.7 93.5 all-gather.13
  221.9 162.0 all-gather.11
  483.7 33.5 all-gather.15
  566.8 44.5 reduce-scatter.8
  614.0 44.5 reduce-scatter.10
  705.3 291.4 reduce-scatter.14
  999.8 19.0 reduce-scatter.18
  1021.5 31.4 reduce-scatter.12
  1055.5 58.5 reduce-scatter.16

commit v12 on v11

--- a/solution.py
+++ b/solution.py
@@ -637,9 +637,8 @@
         dt_here,
         o_gain,
     )
-    mixed, ffn_all, grad_out_rows, w_down_t = lax.optimization_barrier(
-        (mixed, ffn_all, grad_out_rows, down_all)
-    )
+    mixed, ffn_all, grad_out_rows = lax.optimization_barrier((mixed, ffn_all, grad_out_rows))
+    w_down_t = down_all
     w_gate_all = ffn_all[:, :ff_width]
     w_up_all = ffn_all[:, ff_width : 2 * ff_width]
     mixed_half = mixed.astype(jnp.bfloat16)

time: 1200 us -> 1190 us (level)
  waiting for transfers between devices: 53.8 us -> 26 us
  Pallas kernels: 450 us -> 463 us
    all_gather x1, waiting for transfers between devices: 28 us -> 0.02 us  [on_device(): ffn_all = lax.all_gather(ffn_local, 'head', axis=0, tiled=True)]
    pallas_call x2, Pallas kernels: 175 us -> 188 us  [ring_scatter(): pl.pallas_call(partial(_ring_scatter_kernel, major, minor), out_shape=jax...]
    unnamed x412 -> x406, local copies, waits for them, and re-layouts: 52.7 us -> 51.5 us
  transfers between devices with their start and end apart: 12 -> 12, of which waited for: 3 -> 2; matrix products, arithmetic and copies ran while one was open for 45% -> 46% of each run, Pallas kernels for 30% -> 39%
where the time goes in v12:
time: 1190 us; the launch traced here: 1180 us
  Pallas kernels  463 us (39%)
  matrix products  329 us (28%)
  local copies, waits for them, and re-layouts  155 us (13%)
  other arithmetic  144 us (12%)
  blocking collectives  45.4 us (4%)
  waiting for transfers between devices  26 us (2%)
  between operations  17.5 us (1%)
    pallas_call x2, Pallas kernels, ring_scatter(): pl.pallas_call(partial(_ring_scatter_kernel, major, minor), out_shape=jax...  188 us
    pallas_call x2, Pallas kernels, ring_gather(): pl.pallas_call(partial(_ring_gather_kernel, major, minor), out_shape=jax....  180 us
    dot_general x5, matrix products, contract_cols(): lax.dot_general(left, right, (((1,), (1,)), ((), ())), preferred_element_...  60.2 us
    dot_general x5, matrix products, contract_rows(): lax.dot_general(left, right, (((0,), (0,)), ((), ())), preferred_element_...  51.9 us
    unnamed x406, local copies, waits for them, and re-layouts  51.5 us
    pallas_call x1, Pallas kernels, _recur_forward(): pl.pallas_call(partial(_recur_fwd_kernel, nb), grid=(heads, blocks), in_s...  49.3 us
    pallas_call x1, Pallas kernels, delta_rule(): states, updates = state_recurrence(u0, w, kt, c)  46.3 us
    psum x1, blocking collectives, on_device(): lax.psum((grad_gain_in, grad_gain_ffn, core_grads[11], grad_a_full, grad_...  40.2 us
  transfers between devices with their start and end apart: 12, of which 2 were waited for; matrix products, arithmetic and copies ran while one was open for 46% of the time, Pallas kernels for 39%

profile of v12, /device:TPU:0, one launch (start us, length us, event | category | flops | bytes accessed | tf_op | source)
XLA Modules:
  0.0 1181.6 jit_solution(14247372508941976901)
XLA Ops:
  19.0 91.0 %ring_gather_head.2 = bf16[2048,2048]{1,0:T(8,128)(2,1)} custom-call(bf16[256,2048]{1,0:T(8,128)(2,1)} %fusion.31.x_ref), custom_call_target="tpu_custom_call" | custom-call | tf_op jit(solution)/shard_map/ring_gather_head/pallas_call | solution.py:498
  127.6 18.2 %fusion.164 = f32[2048,1540]{0,1:T(8,128)S(1)} fusion(bf16[2048,2048]{1,0:T(8,128)(2,1)} %ring_gather_head.2, bf16[2048,1540]{1,0:T(8,128)(2,1)} %all-gather.10.cloned.1.call-done), kind=kOutput, calls=%fused_computation.345 | convolution fusion | flops 12918456320 | bytes 27312128 | tf_op jit(solution)/shard_map/dot_general | solution.py:618
  274.5 49.3 %jvp_delta_state_forward_.1 = (f32[2,32,256,128]{3,2,1,0:T(8,128)}, f32[2,32,64,256]{3,2,1,0:T(8,128)}) custom-call(f32[2,32,64,256]{3,2,1,0:T(8,128)} %slice.356.u0_ref, f32[2,32,64,128]{3,2,1,0:T(8,128)} %slice.357.w_ref, f32[2,32,64,128]{3,2,1,0:T(8,128)} %get-tuple-element.225.kt_ref, f32[2,32,1,128]{3,2,1,0:T(1,128)} %broadcast_in_dim.34.c_ref), custom_call_target="tpu_custom_call" | custom-call | flops 3221225472 | bytes 20971520 | tf_op jit(solution)/shard_map/jvp(delta_state_forward)/pallas_call | solution.py:121
  329.6 9.5 fusion.166
  357.8 9.2 convolution_convert_fusion.4.y_ref
  367.0 101.7 %ring_scatter_head.2 = f32[256,2048]{1,0:T(8,128)} custom-call(bf16[2048,2048]{1,0:T(8,128)(2,1)} %convolution_convert_fusion.4.y_ref), custom_call_target="tpu_custom_call" | custom-call | tf_op jit(solution)/shard_map/ring_scatter_head/pallas_call | solution.py:517
  472.3 12.1 %fusion.168 = f32[1024,1408]{1,0:T(8,128)} fusion(bf16[1024,2048]{1,0:T(8,128)(2,1)} %bitcast.371, bf16[2048,1408]{0,1:T(8,128)(2,1)} %all-gather.14.cloned.1.call-done), kind=kOutput, calls=%fused_computation.349 | convolution fusion | flops 5905580032 | bytes 15728640 | tf_op jit(solution)/shard_map/dot_general | solution.py:659
  484.4 21.6 %all-gather.16.cloned.1.call-done = bf16[1024,2048]{1,0:T(8,128)(2,1)} async-done(((bf16[256,2048]{1,0:T(8,128)(2,1)}), bf16[1024,2048]{1,0:T(8,128)(2,1)}) %all-gather.16.cloned.1.call-update) | async-done | bytes 4194320 | tf_op jit(solution)/shard_map/all_gather | solution.py:653
  506.0 11.8 fusion.9
  517.8 16.5 %multiply_convert_fusion = (bf16[1024,1408]{1,0:T(8,128)(2,1)}, bf16[1024,1408]{1,0:T(8,128)(2,1)}, bf16[1024,1408]{1,0:T(8,128)(2,1)}) fusion(f32[1024,1408]{1,0:T(8,128)} %fusion.9, f32[1024,1408]{1,0:T(8,128)} %fusion.168, bf16[1024,2048]{1,0:T(8,128)(2,1)} %all-gather.16.cloned.1.call-done, bf16[2048,2816]{1,0:T(8,128)(2,1)} %all-gather.12.cloned.1.call-done), kind=kOutput, calls=%fused_computation.17 | convolution fusion | flops 5928648704 | bytes 30146560 | tf_op jit(solution)/shard_map/dot_general | solution.py:655
  534.3 10.5 fusion.7
  544.8 10.5 add_convert_fusion
  555.4 10.9 convolution_convert_fusion.6
  566.4 9.2 convolution_convert_fusion.1
  604.8 89.0 %ring_gather_head.3 = bf16[2048,2048]{1,0:T(8,128)(2,1)} custom-call(bf16[256,2048]{1,0:T(8,128)(2,1)} %fusion.140.x_ref), custom_call_target="tpu_custom_call" | custom-call | tf_op jit(solution)/shard_map/ring_gather_head/pallas_call | solution.py:498
  724.0 17.9 %fusion.21.ds_ref = f32[2,32,256,128]{3,2,1,0:T(8,128)} fusion(f32[2,32,64,128]{3,2,1,0:T(8,128)S(1)} %bitcast.326, f32[2,32,64,256]{3,2,1,0:T(8,128)S(1)} %bitcast.318, f32[2,32,64]{2,1,0:T(8,128)S(1)} %copy-done.91), kind=kOutput, calls=%fused_computation.64 | convolution fusion | flops 1611661312 | bytes 14696448 | tf_op jit(solution)/shard_map/transpose(jvp(vmap(nid,nvd->niv)))/dot_general | solution.py:298
  741.9 46.3 %transpose_jvp_delta_state_backward__.1 = (f32[2,32,64,256]{3,2,1,0:T(8,128)}, f32[2,32,64,128]{3,2,1,0:T(8,128)}, f32[2,32,64,128]{3,2,1,0:T(8,128)}, f32[2,32,1,128]{3,2,1,0:T(1,128)}) custom-call(f32[2,32,256,128]{3,2,1,0:T(8,128)} %get-tuple-element.53.s_ref, f32[2,32,64,256]{3,2,1,0:T(8,128)} %get-tuple-element.54.u_ref, ...), custom_call_target="tpu_custom_call" | custom-call | flops 6442450944 | bytes 41943040 | tf_op jit(solution)/shard_map/transpose(jvp(delta_state_backward))/pallas_call | solution.py:309
  816.8 10.8 fusion.4
  943.9 10.1 convolution_convert_fusion.7
  954.1 23.9 %concatenate.133 = bf16[2048,1540]{0,1:T(8,128)(2,1)} concatenate(bf16[2048,256]{0,1:T(8,128)(2,1)S(1)} %bitcast.337, bf16[2048,256]{0,1:T(8,128)(2,1)} %bitcast.338, bf16[2048,512]{0,1:T(8,128)(2,1)S(1)} %bitcast.332, bf16[2048,512]{0,1:T(8,128)(2,1)} %bitcast.335, bf16[2048,2]{0,1:T(2,128)(2,1)S(1)} %bitcast.348, bf16[2048,2]{0,1:T(2,128)(2,1)S(1)} %fusion.105), dimensions={1} | concatenate | bytes 12615680 | tf_op jit(solution)/shard_map/concatenate | solution.py:690
  978.0 19.3 %convolution_convert_fusion.5 = bf16[2048,1540]{0,1:T(8,128)(2,1)} fusion(bf16[2048,2048]{1,0:T(8,128)(2,1)} %ring_gather_head.2, bf16[2048,1540]{0,1:T(8,128)(2,1)} %concatenate.133), kind=kOutput, calls=%fused_computation.8 | convolution fusion | flops 12921610240 | bytes 21004288 | tf_op jit(solution)/shard_map/dot_general | solution.py:548
  997.4 21.0 %convolution_convert_fusion.y_ref = bf16[2048,2048]{1,0:T(8,128)(2,1)} fusion(bf16[2048,1540]{0,1:T(8,128)(2,1)} %concatenate.133, bf16[2048,1540]{1,0:T(8,128)(2,1)} %all-gather.10.cloned.1.call-done), kind=kOutput, calls=%fused_computation.3 | convolution fusion | flops 12922650624 | bytes 21004288 | tf_op jit(solution)/shard_map/dot_general | solution.py:554
  1018.4 86.2 %ring_scatter_head.3 = f32[256,2048]{1,0:T(8,128)} custom-call(bf16[2048,2048]{1,0:T(8,128)(2,1)} %convolution_convert_fusion.y_ref), custom_call_target="tpu_custom_call" | custom-call | tf_op jit(solution)/shard_map/ring_scatter_head/pallas_call | solution.py:517
  1109.7 40.2 %all-reduce.39 = (f32[16]{0:T(128)}, f32[16]{0:T(128)}, f32[256]{0:T(256)}, f32[2048]{0:T(1024)}, f32[2048]{0:T(1024)}) all-reduce(f32[16]{0:T(128)S(1)} %dynamic_update_slice.6, f32[16]{0:T(128)S(1)} %dynamic_update_slice.7, f32[256]{0:T(256)S(1)} %copy-done.166, ...), channel_id=1, replica_groups=mesh['head'=8,'row'=4] {'head','row'}, use_global_device_ids=true, to_apply=%region_41.42 | all-reduce | flops 4384 | bytes 35072 | tf_op jit(solution)/shard_map/psum | solution.py:729
  (631 shorter events, 417.2 us)
Async XLA Ops:
  7.2 106.4 %all-gather.8.cloned.1.call-start = ((), (), s32[]{:S(2)}) async-start(), calls=%async_computation.6 | async-start | bytes 2621440 | tf_op jit(solution)/shard_map/all_gather | solution.py:606
  9.5 118.0 %all-gather.10.cloned.1.call-start = ((), (), s32[]{:S(2)}) async-start(), calls=%async_computation.7 | async-start | bytes 8519680 | tf_op jit(solution)/shard_map/all_gather | solution.py:596
  13.5 344.4 %all-gather.18.cloned.1.call-start = ((), (), s32[]{:S(2)}) async-start(), calls=%async_computation.16 | async-start | bytes 5242880 | tf_op jit(solution)/shard_map/all_gather | solution.py:611
  14.2 343.6 %all-gather.12.cloned.1.call-start = ((), (), s32[]{:S(2)}) async-start(), calls=%async_computation.8 | async-start | bytes 12976128 | tf_op jit(solution)/shard_map/all_gather | solution.py:616
  113.6 358.7 %all-gather.14.cloned.1.call-start = ((), (), s32[]{:S(2)}) async-start(), calls=%async_computation.9 | async-start | bytes 6488064 | tf_op jit(solution)/shard_map/all_gather | solution.py:617
  126.8 107.7 %copy-start.102 = (f32[2048]{0:T(1024)}, f32[2048]{0:T(1024)S(1)}, u32[]{:S(2)}) copy-start(f32[2048]{0:T(1024)S(1)} %get-tuple-element.304) | copy-start | bytes 24580
  126.8 107.7 %copy-start.104 = (f32[2048]{0:T(1024)}, f32[2048]{0:T(1024)S(1)}, u32[]{:S(2)}) copy-start(f32[2048]{0:T(1024)S(1)} %get-tuple-element.305) | copy-start | bytes 24580
  127.1 212.0 %copy-start.12 = (f32[32,64,64]{1,2,0:T(8,128)}, f32[32,64,64]{1,2,0:T(8,128)S(1)}, u32[]{:S(2)}) copy-start(f32[32,64,64]{1,2,0:T(8,128)S(1)} %get-tuple-element.295) | copy-start | bytes 1572868
  127.1 212.0 %copy-start.39 = (pred[32,64,64]{1,2,0:T(8,128)(4,1)}, pred[32,64,64]{1,2,0:T(8,128)(4,1)S(1)}, u32[]{:S(2)}) copy-start(pred[32,64,64]{1,2,0:T(8,128)(4,1)S(1)} %get-tuple-element.294) | copy-start | bytes 393220
  127.2 378.9 %all-gather.16.cloned.1.call-start = ((), (), s32[]{:S(2)}) async-start(), calls=%async_computation.10 | async-start | bytes 5242880 | tf_op jit(solution)/shard_map/all_gather | solution.py:653
  152.8 107.7 %copy-start.75 = (f32[2,32,64]{2,1,0:T(8,128)}, f32[2,32,64]{2,1,0:T(8,128)S(1)}, u32[]{:S(2)}) copy-start(f32[2,32,64]{2,1,0:T(8,128)S(1)} %mul.977) | copy-start | bytes 49156
  154.9 184.3 %copy-start.61 = (f32[2,32,64]{2,1,0:T(8,128)}, f32[2,32,64]{2,1,0:T(8,128)S(1)}, u32[]{:S(2)}) copy-start(f32[2,32,64]{2,1,0:T(8,128)S(1)} %reduce_window_sum.22) | copy-start | bytes 49156
  173.4 152.7 %copy-start.5 = (f32[2,2048,128]{2,1,0:T(8,128)}, f32[2,2048,128]{2,1,0:T(8,128)S(1)}, u32[]{:S(2)}) copy-start(f32[2,2048,128]{2,1,0:T(8,128)S(1)} %get-tuple-element.226) | copy-start | bytes 6291460
  367.0 101.7 %copy-start.42 = (bf16[1,256,2048]{2,1,0:T(8,128)(2,1)S(1)}, bf16[1,256,2048]{2,1,0:T(8,128)(2,1)}, u32[]{:S(2)}) copy-start(bf16[1,256,2048]{2,1,0:T(8,128)(2,1)} %param.22) | copy-start | bytes 3145732
  470.7 131.9 %copy-start.20 = (f32[256,2048]{1,0:T(8,128)}, f32[256,2048]{1,0:T(8,128)S(1)}, u32[]{:S(2)}) copy-start(f32[256,2048]{1,0:T(8,128)S(1)} %get-tuple-element.224) | copy-start | bytes 6291460
  470.7 131.9 %copy-start.138 = (f32[256]{0:T(256)}, f32[256]{0:T(256)S(1)}, u32[]{:S(2)}) copy-start(f32[256]{0:T(256)S(1)} %fusion.121) | copy-start | bytes 3076
  472.2 127.8 %reduce-scatter.9.cloned.1.call-start = ((), (), s32[]{:S(2)}) async-start(), calls=%async_computation.11 | async-start | bytes 5242880 | tf_op jit(solution)/shard_map/reduce_scatter | solution.py:666
  555.4 387.3 %reduce-scatter.11.cloned.1.call-start = ((), (), s32[]{:S(2)}) async-start(), calls=%async_computation.12 | async-start | bytes 5242880 | tf_op jit(solution)/shard_map/reduce_scatter | solution.py:681
  566.3 431.0 %reduce-scatter.15.cloned.1.call-start = ((), (), s32[]{:S(2)}) async-start(), calls=%async_computation.14 | async-start | bytes 19464192 | tf_op jit(solution)/shard_map/reduce_scatter | solution.py:683
  693.9 411.2 %reduce-scatter.19.cloned.1.call-start = ((), (), s32[]{:S(2)}) async-start(), calls=%async_computation.17 | async-start | bytes 327680
  943.8 163.4 %reduce-scatter.13.cloned.1.call-start = ((), (), s32[]{:S(2)}) async-start(), calls=%async_computation.13 | async-start | bytes 2621440 | tf_op jit(solution)/shard_map/reduce_scatter | solution.py:686
  954.0 211.7 %reduce-scatter.17.cloned.1.call-start = ((), (), s32[]{:S(2)}) async-start(), calls=%async_computation.15 | async-start | bytes 7905280 | tf_op jit(solution)/shard_map/reduce_scatter | solution.py:706
  1018.3 88.9 %copy-start.128 = (f32[2048]{0:T(1024)S(1)}, f32[2048]{0:T(1024)}, u32[]{:S(2)}) copy-start(f32[2048]{0:T(1024)} %param.36) | copy-start | bytes 24580
  1018.3 88.9 %copy-start.153 = (f32[256]{0:T(256)S(1)}, f32[256]{0:T(256)}, u32[]{:S(2)}) copy-start(f32[256]{0:T(256)} %copy-done.152) | copy-start | bytes 3076
  (177 other events, 1494.4 us)
Sparse Core Ops, SparseCore 0:
  10.2 25.2 all-gather.7
  37.7 49.3 all-gather.9
  88.6 34.5 all-gather.17
  125.8 163.6 all-gather.11
  292.0 99.2 all-gather.13
  472.4 33.6 all-gather.15
  555.5 44.4 reduce-scatter.8
  602.7 44.5 reduce-scatter.10
  694.0 291.4 reduce-scatter.14
  988.5 19.0 reduce-scatter.18
  1010.2 31.4 reduce-scatter.12
  1044.2 58.5 reduce-scatter.16

commit v13 on v12

--- a/solution.py
+++ b/solution.py
@@ -687,11 +687,13 @@
     core_grads = pull_core(grad_mixed)
     core_grads, ffn_output = lax.optimization_barrier((core_grads, ffn_output))
     final_out = (middle + ffn_output.astype(jnp.float32)).astype(jnp.bfloat16)
+    wide = edges[4]
     grad_proj = jnp.concatenate(
-        [core_grads[0], core_grads[1], core_grads[2], core_grads[3], core_grads[4], core_grads[5]],
-        axis=1,
+        [core_grads[0], core_grads[1], core_grads[2], core_grads[3]], axis=1
     ).astype(jnp.bfloat16)
+    grad_proj_ab = jnp.concatenate([core_grads[4], core_grads[5]], axis=1).astype(jnp.bfloat16)
     grad_inward = contract_rows(all_rows, grad_proj).astype(jnp.bfloat16)
+    grad_inward_ab = contract_rows(all_rows, grad_proj_ab).astype(jnp.bfloat16)
     grad_inward, ffn_grad_all = lax.optimization_barrier((grad_inward, ffn_grad_all))
     ffn_grad_all = ffn_grad_all.astype(jnp.float32)
     ffn_grads = (
@@ -699,12 +701,22 @@
         ffn_grad_all[:, ff_width : 2 * ff_width],
         ffn_grad_all[:, 2 * ff_width :].T,
     )
-    grad_norm_one = ring_scatter(contract_cols(grad_proj, w_inward).astype(jnp.bfloat16), ring, 3)
+    grad_norm_one = ring_scatter(
+        (
+            contract_cols(grad_proj, w_inward[:, :wide])
+            + contract_cols(grad_proj_ab, w_inward[:, wide:])
+        ).astype(jnp.bfloat16),
+        ring,
+        3,
+    )
     grad_norm_one, wout_grad = lax.optimization_barrier((grad_norm_one, wout_grad))
     grad_in_part, grad_gain_in = pull_one(grad_norm_one)
     grad_input = grad_middle + grad_in_part
     inward_all = lax.psum_scatter(
         grad_inward, "row", scatter_dimension=0, tiled=True
+    ).astype(jnp.float32)
+    inward_ab = lax.psum_scatter(
+        grad_inward_ab, "row", scatter_dimension=0, tiled=True
     ).astype(jnp.float32)
     conv_grad_local = jnp.concatenate(
         [
@@ -716,7 +728,10 @@
     conv_grad = lax.psum_scatter(
         conv_grad_local.astype(jnp.bfloat16), "row", scatter_dimension=1, tiled=True
     ).astype(jnp.float32)
-    mixer_grads = tuple(inward_all[:, edges[spot] : edges[spot + 1]] for spot in range(6)) + tuple(
+    mixer_grads = tuple(inward_all[:, edges[spot] : edges[spot + 1]] for spot in range(4)) + (
+        inward_ab[:, : edges[5] - wide],
+        inward_ab[:, edges[5] - wide :],
+    ) + tuple(
         conv_grad[:, conv_edges[i] : conv_edges[i + 1]] for i in range(3)
     ) + (wout_grad.astype(jnp.float32),)
     head_total = a_log.shape[0]

time: 1190 us -> 1180 us (level)
  local copies, waits for them, and re-layouts: 155 us -> 129 us
  matrix products: 329 us -> 344 us
    concatenate x1 -> x0, local copies, waits for them, and re-layouts: 23.9 us -> none  [on_device(): jnp.concatenate([core_grads[0], core_grads[1], core_grads[2], core_grads[...]
    dot_general x5 -> x6, matrix products: 60.2 us -> 70.8 us  [contract_cols(): lax.dot_general(left, right, (((1,), (1,)), ((), ())), preferred_element_...]
    dot_general x5 -> x6, matrix products: 51.9 us -> 55.6 us  [contract_rows(): lax.dot_general(left, right, (((0,), (0,)), ((), ())), preferred_element_...]
  transfers between devices with their start and end apart: 12 -> 13, of which waited for: 2 -> 3; matrix products, arithmetic and copies ran while one was open for 46% -> 45% of each run, Pallas kernels for 39% -> 40%
where the time goes in v13:
time: 1180 us
  Pallas kernels  466 us (39%)
  matrix products  344 us (29%)
  other arithmetic  142 us (12%)
  local copies, waits for them, and re-layouts  129 us (11%)
  blocking collectives  44.9 us (4%)
  waiting for transfers between devices  35 us (3%)
  between operations  17.3 us (1%)
    pallas_call x2, Pallas kernels, ring_scatter(): pl.pallas_call(partial(_ring_scatter_kernel, major, minor), out_shape=jax...  190 us
    pallas_call x2, Pallas kernels, ring_gather(): pl.pallas_call(partial(_ring_gather_kernel, major, minor), out_shape=jax....  180 us
    dot_general x6, matrix products, contract_cols(): lax.dot_general(left, right, (((1,), (1,)), ((), ())), preferred_element_...  70.8 us
    dot_general x6, matrix products, contract_rows(): lax.dot_general(left, right, (((0,), (0,)), ((), ())), preferred_element_...  55.6 us
    pallas_call x1, Pallas kernels, _recur_forward(): pl.pallas_call(partial(_recur_fwd_kernel, nb), grid=(heads, blocks), in_s...  49.4 us
    unnamed x406, local copies, waits for them, and re-layouts  49 us
    pallas_call x1, Pallas kernels, delta_rule(): states, updates = state_recurrence(u0, w, kt, c)  46.2 us
    psum x1, blocking collectives, on_device(): lax.psum((grad_gain_in, grad_gain_ffn, core_grads[11], grad_a_full, grad_...  39.8 us
  transfers between devices with their start and end apart: 13, of which 3 were waited for; matrix products, arithmetic and copies ran while one was open for 45% of the time, Pallas kernels for 40%

profile of v13, /device:TPU:0, one launch (start us, length us, event | category | flops | bytes accessed | tf_op | source)
XLA Modules:
  0.0 1178.8 jit_solution(13182340405133208491)
XLA Ops:
  19.1 91.0 %ring_gather_head.2 = bf16[2048,2048]{1,0:T(8,128)(2,1)} custom-call(bf16[256,2048]{1,0:T(8,128)(2,1)} %fusion.33.x_ref), custom_call_target="tpu_custom_call" | custom-call | tf_op jit(solution)/shard_map/ring_gather_head/pallas_call | solution.py:498
  127.5 18.3 %fusion.171 = f32[2048,1540]{0,1:T(8,128)S(1)} fusion(bf16[2048,2048]{1,0:T(8,128)(2,1)} %ring_gather_head.2, bf16[2048,1540]{1,0:T(8,128)(2,1)} %all-gather.10.cloned.1.call-done), kind=kOutput, calls=%fused_computation.355 | convolution fusion | flops 12918456320 | bytes 27312128 | tf_op jit(solution)/shard_map/dot_general | solution.py:618
  274.4 49.4 %jvp_delta_state_forward_.1 = (f32[2,32,256,128]{3,2,1,0:T(8,128)}, f32[2,32,64,256]{3,2,1,0:T(8,128)}) custom-call(f32[2,32,64,256]{3,2,1,0:T(8,128)} %slice.364.u0_ref, f32[2,32,64,128]{3,2,1,0:T(8,128)} %slice.365.w_ref, f32[2,32,64,128]{3,2,1,0:T(8,128)} %get-tuple-element.225.kt_ref, f32[2,32,1,128]{3,2,1,0:T(1,128)} %broadcast_in_dim.34.c_ref), custom_call_target="tpu_custom_call" | custom-call | flops 3221225472 | bytes 20971520 | tf_op jit(solution)/shard_map/jvp(delta_state_forward)/pallas_call | solution.py:121
  329.7 9.5 fusion.173
  357.9 9.1 convolution_convert_fusion.3.y_ref
  367.1 101.7 %ring_scatter_head.2 = f32[256,2048]{1,0:T(8,128)} custom-call(bf16[2048,2048]{1,0:T(8,128)(2,1)} %convolution_convert_fusion.3.y_ref), custom_call_target="tpu_custom_call" | custom-call | tf_op jit(solution)/shard_map/ring_scatter_head/pallas_call | solution.py:517
  472.3 12.1 %fusion.175 = f32[1024,1408]{1,0:T(8,128)} fusion(bf16[1024,2048]{1,0:T(8,128)(2,1)} %bitcast.375, bf16[2048,1408]{0,1:T(8,128)(2,1)} %all-gather.14.cloned.1.call-done), kind=kOutput, calls=%fused_computation.359 | convolution fusion | flops 5905580032 | bytes 15728640 | tf_op jit(solution)/shard_map/dot_general | solution.py:659
  484.4 21.6 %all-gather.16.cloned.1.call-done = bf16[1024,2048]{1,0:T(8,128)(2,1)} async-done(((bf16[256,2048]{1,0:T(8,128)(2,1)}), bf16[1024,2048]{1,0:T(8,128)(2,1)}) %all-gather.16.cloned.1.call-update) | async-done | bytes 4194320 | tf_op jit(solution)/shard_map/all_gather | solution.py:653
  506.0 11.8 %fusion.11 = f32[1024,1408]{1,0:T(8,128)} fusion(bf16[1024,2048]{1,0:T(8,128)(2,1)} %all-gather.16.cloned.1.call-done, bf16[2048,2816]{1,0:T(8,128)(2,1)} %all-gather.12.cloned.1.call-done), kind=kOutput, calls=%fused_computation.29 | convolution fusion | flops 5905580032 | bytes 15728640 | tf_op jit(solution)/shard_map/dot_general | solution.py:654
  517.8 16.5 %multiply_convert_fusion = (bf16[1024,1408]{1,0:T(8,128)(2,1)}, bf16[1024,1408]{1,0:T(8,128)(2,1)}, bf16[1024,1408]{1,0:T(8,128)(2,1)}) fusion(f32[1024,1408]{1,0:T(8,128)} %fusion.11, f32[1024,1408]{1,0:T(8,128)} %fusion.175, bf16[1024,2048]{1,0:T(8,128)(2,1)} %all-gather.16.cloned.1.call-done, bf16[2048,2816]{1,0:T(8,128)(2,1)} %all-gather.12.cloned.1.call-done), kind=kOutput, calls=%fused_computation.20 | convolution fusion | flops 5928648704 | bytes 30146560 | tf_op jit(solution)/shard_map/dot_general | solution.py:655
  534.3 10.5 fusion.9
  544.8 10.5 add_convert_fusion.1
  555.4 10.9 convolution_convert_fusion.5
  566.4 9.2 convolution_convert_fusion
  604.9 89.0 %ring_gather_head.3 = bf16[2048,2048]{1,0:T(8,128)(2,1)} custom-call(bf16[256,2048]{1,0:T(8,128)(2,1)} %fusion.147.x_ref), custom_call_target="tpu_custom_call" | custom-call | tf_op jit(solution)/shard_map/ring_gather_head/pallas_call | solution.py:498
  724.0 17.9 %fusion.23.ds_ref = f32[2,32,256,128]{3,2,1,0:T(8,128)} fusion(f32[2,32,64,128]{3,2,1,0:T(8,128)S(1)} %bitcast.325, f32[2,32,64,256]{3,2,1,0:T(8,128)S(1)} %bitcast.317, f32[2,32,64]{2,1,0:T(8,128)S(1)} %copy-done.92), kind=kOutput, calls=%fused_computation.67 | convolution fusion | flops 1611661312 | bytes 14696448 | tf_op jit(solution)/shard_map/transpose(jvp(vmap(nid,nvd->niv)))/dot_general | solution.py:298
  741.9 46.2 %transpose_jvp_delta_state_backward__.1 = (f32[2,32,64,256]{3,2,1,0:T(8,128)}, f32[2,32,64,128]{3,2,1,0:T(8,128)}, f32[2,32,64,128]{3,2,1,0:T(8,128)}, f32[2,32,1,128]{3,2,1,0:T(1,128)}) custom-call(f32[2,32,256,128]{3,2,1,0:T(8,128)} %get-tuple-element.53.s_ref, f32[2,32,64,256]{3,2,1,0:T(8,128)} %get-tuple-element.54.u_ref, ...), custom_call_target="tpu_custom_call" | custom-call | flops 6442450944 | bytes 41943040 | tf_op jit(solution)/shard_map/transpose(jvp(delta_state_backward))/pallas_call | solution.py:309
  816.7 10.8 fusion.6
  946.9 10.2 convolution_convert_fusion.6
  958.3 18.3 %convolution_convert_fusion.4 = bf16[2048,1536]{1,0:T(8,128)(2,1)} fusion(bf16[2048,2048]{1,0:T(8,128)(2,1)} %ring_gather_head.2, bf16[2048,512]{0,1:T(8,128)(2,1)} %bitcast.338, bf16[2048,512]{0,1:T(8,128)(2,1)S(1)} %bitcast.334, bf16[2048,256]{0,1:T(8,128)(2,1)} %bitcast.342, bf16[2048,256]{0,1:T(8,128)(2,1)S(1)} %bitcast.340), kind=kOutput, calls=%fused_computation.8 | convolution fusion | flops 12913213440 | bytes 20971520 | tf_op jit(solution)/shard_map/dot_general | solution.py:548
  985.5 19.7 %fusion = f32[2048,2048]{1,0:T(8,128)} fusion(bf16[2048,1540]{1,0:T(8,128)(2,1)} %all-gather.10.cloned.1.call-done, bf16[2048,512]{0,1:T(8,128)(2,1)} %bitcast.339, bf16[2048,512]{0,1:T(8,128)(2,1)S(1)} %bitcast.335, bf16[2048,256]{0,1:T(8,128)(2,1)} %bitcast.343, bf16[2048,256]{0,1:T(8,128)(2,1)S(1)} %bitcast.341), kind=kOutput, calls=%fused_computation.9 | convolution fusion | flops 12910067712 | bytes 29360128 | tf_op jit(solution)/shard_map/dot_general | solution.py:554
  1005.3 11.8 add_convert_fusion.y_ref
  1017.1 88.7 %ring_scatter_head.3 = f32[256,2048]{1,0:T(8,128)} custom-call(bf16[2048,2048]{1,0:T(8,128)(2,1)} %add_convert_fusion.y_ref), custom_call_target="tpu_custom_call" | custom-call | tf_op jit(solution)/shard_map/ring_scatter_head/pallas_call | solution.py:517
  1112.7 39.8 %all-reduce.39 = (f32[16]{0:T(128)}, f32[16]{0:T(128)}, f32[256]{0:T(256)}, f32[2048]{0:T(1024)}, f32[2048]{0:T(1024)}) all-reduce(f32[16]{0:T(128)S(1)} %dynamic_update_slice.6, f32[16]{0:T(128)S(1)} %dynamic_update_slice.7, f32[256]{0:T(256)S(1)} %copy-done.167, ...), channel_id=1, replica_groups=mesh['head'=8,'row'=4] {'head','row'}, use_global_device_ids=true, to_apply=%region_42.43 | all-reduce | flops 4384 | bytes 35072 | tf_op jit(solution)/shard_map/psum | solution.py:744
  (635 shorter events, 427.0 us)
Async XLA Ops:
  7.2 106.4 %all-gather.8.cloned.1.call-start = ((), (), s32[]{:S(2)}) async-start(), calls=%async_computation.7 | async-start | bytes 2621440 | tf_op jit(solution)/shard_map/all_gather | solution.py:606
  9.5 118.0 %all-gather.10.cloned.1.call-start = ((), (), s32[]{:S(2)}) async-start(), calls=%async_computation.8 | async-start | bytes 8519680 | tf_op jit(solution)/shard_map/all_gather | solution.py:596
  13.5 344.4 %all-gather.18.cloned.1.call-start = ((), (), s32[]{:S(2)}) async-start(), calls=%async_computation.17 | async-start | bytes 5242880 | tf_op jit(solution)/shard_map/all_gather | solution.py:611
  14.2 343.7 %all-gather.12.cloned.1.call-start = ((), (), s32[]{:S(2)}) async-start(), calls=%async_computation.9 | async-start | bytes 12976128 | tf_op jit(solution)/shard_map/all_gather | solution.py:616
  113.7 358.6 %all-gather.14.cloned.1.call-start = ((), (), s32[]{:S(2)}) async-start(), calls=%async_computation.10 | async-start | bytes 6488064 | tf_op jit(solution)/shard_map/all_gather | solution.py:617
  126.8 107.6 %copy-start.103 = (f32[2048]{0:T(1024)}, f32[2048]{0:T(1024)S(1)}, u32[]{:S(2)}) copy-start(f32[2048]{0:T(1024)S(1)} %get-tuple-element.302) | copy-start | bytes 24580
  126.8 107.6 %copy-start.105 = (f32[2048]{0:T(1024)}, f32[2048]{0:T(1024)S(1)}, u32[]{:S(2)}) copy-start(f32[2048]{0:T(1024)S(1)} %get-tuple-element.303) | copy-start | bytes 24580
  127.2 212.0 %copy-start.12 = (f32[32,64,64]{1,2,0:T(8,128)}, f32[32,64,64]{1,2,0:T(8,128)S(1)}, u32[]{:S(2)}) copy-start(f32[32,64,64]{1,2,0:T(8,128)S(1)} %get-tuple-element.293) | copy-start | bytes 1572868
  127.2 212.0 %copy-start.39 = (pred[32,64,64]{1,2,0:T(8,128)(4,1)}, pred[32,64,64]{1,2,0:T(8,128)(4,1)S(1)}, u32[]{:S(2)}) copy-start(pred[32,64,64]{1,2,0:T(8,128)(4,1)S(1)} %get-tuple-element.292) | copy-start | bytes 393220
  127.2 378.8 %all-gather.16.cloned.1.call-start = ((), (), s32[]{:S(2)}) async-start(), calls=%async_computation.11 | async-start | bytes 5242880 | tf_op jit(solution)/shard_map/all_gather | solution.py:653
  152.8 107.7 %copy-start.75 = (f32[2,32,64]{2,1,0:T(8,128)}, f32[2,32,64]{2,1,0:T(8,128)S(1)}, u32[]{:S(2)}) copy-start(f32[2,32,64]{2,1,0:T(8,128)S(1)} %mul.977) | copy-start | bytes 49156
  154.9 184.3 %copy-start.61 = (f32[2,32,64]{2,1,0:T(8,128)}, f32[2,32,64]{2,1,0:T(8,128)S(1)}, u32[]{:S(2)}) copy-start(f32[2,32,64]{2,1,0:T(8,128)S(1)} %reduce_window_sum.22) | copy-start | bytes 49156
  173.6 152.6 %copy-start.5 = (f32[2,2048,128]{2,1,0:T(8,128)}, f32[2,2048,128]{2,1,0:T(8,128)S(1)}, u32[]{:S(2)}) copy-start(f32[2,2048,128]{2,1,0:T(8,128)S(1)} %get-tuple-element.226) | copy-start | bytes 6291460
  367.1 101.7 %copy-start.42 = (bf16[1,256,2048]{2,1,0:T(8,128)(2,1)S(1)}, bf16[1,256,2048]{2,1,0:T(8,128)(2,1)}, u32[]{:S(2)}) copy-start(bf16[1,256,2048]{2,1,0:T(8,128)(2,1)} %param.22) | copy-start | bytes 3145732
  470.8 131.9 %copy-start.20 = (f32[256,2048]{1,0:T(8,128)}, f32[256,2048]{1,0:T(8,128)S(1)}, u32[]{:S(2)}) copy-start(f32[256,2048]{1,0:T(8,128)S(1)} %get-tuple-element.224) | copy-start | bytes 6291460
  470.8 131.9 %copy-start.139 = (f32[256]{0:T(256)}, f32[256]{0:T(256)S(1)}, u32[]{:S(2)}) copy-start(f32[256]{0:T(256)S(1)} %fusion.124) | copy-start | bytes 3076
  472.2 127.9 %reduce-scatter.12.cloned.1.call-start = ((), (), s32[]{:S(2)}) async-start(), calls=%async_computation.12 | async-start | bytes 5242880 | tf_op jit(solution)/shard_map/reduce_scatter | solution.py:666
  555.4 384.4 %reduce-scatter.14.cloned.1.call-start = ((), (), s32[]{:S(2)}) async-start(), calls=%async_computation.13 | async-start | bytes 5242880 | tf_op jit(solution)/shard_map/reduce_scatter | solution.py:681
  566.4 419.1 %reduce-scatter.18.cloned.1.call-start = ((), (), s32[]{:S(2)}) async-start(), calls=%async_computation.15 | async-start | bytes 19464192 | tf_op jit(solution)/shard_map/reduce_scatter | solution.py:683
  693.9 412.5 %reduce-scatter.24.cloned.1.call-start = ((), (), s32[]{:S(2)}) async-start(), calls=%async_computation.19 | async-start | bytes 327680
  940.9 167.7 %reduce-scatter.22.cloned.1.call-start = ((), (), s32[]{:S(2)}) async-start(), calls=%async_computation.18 | async-start | bytes 655360
  946.9 163.4 %reduce-scatter.16.cloned.1.call-start = ((), (), s32[]{:S(2)}) async-start(), calls=%async_computation.14 | async-start | bytes 2621440 | tf_op jit(solution)/shard_map/reduce_scatter | solution.py:686
  957.1 211.1 %reduce-scatter.20.cloned.1.call-start = ((), (), s32[]{:S(2)}) async-start(), calls=%async_computation.16 | async-start | bytes 7864320 | tf_op jit(solution)/shard_map/reduce_scatter | solution.py:715
  1017.1 93.2 %copy-start.154 = (f32[256]{0:T(256)S(1)}, f32[256]{0:T(256)}, u32[]{:S(2)}) copy-start(f32[256]{0:T(256)} %copy-done.153) | copy-start | bytes 3076
  (179 other events, 1585.9 us)
Sparse Core Ops, SparseCore 0:
  10.2 25.2 all-gather.7
  37.7 49.3 all-gather.9
  88.6 34.5 all-gather.17
  125.8 163.6 all-gather.11
  292.0 99.2 all-gather.13
  472.3 33.6 all-gather.15
  555.5 44.5 reduce-scatter.11
  602.8 44.5 reduce-scatter.13
  694.0 291.4 reduce-scatter.17
  988.5 19.0 reduce-scatter.23
  1010.7 21.6 reduce-scatter.21
  1035.0 31.4 reduce-scatter.15
  1069.0 58.9 reduce-scatter.19

commit v14 on v13

--- a/solution.py
+++ b/solution.py
@@ -694,6 +694,11 @@
     grad_proj_ab = jnp.concatenate([core_grads[4], core_grads[5]], axis=1).astype(jnp.bfloat16)
     grad_inward = contract_rows(all_rows, grad_proj).astype(jnp.bfloat16)
     grad_inward_ab = contract_rows(all_rows, grad_proj_ab).astype(jnp.bfloat16)
+    norm_one_partial = (
+        contract_cols(grad_proj, w_inward[:, :wide])
+        + contract_cols(grad_proj_ab, w_inward[:, wide:])
+    ).astype(jnp.bfloat16)
+    grad_inward, norm_one_partial = lax.optimization_barrier((grad_inward, norm_one_partial))
     grad_inward, ffn_grad_all = lax.optimization_barrier((grad_inward, ffn_grad_all))
     ffn_grad_all = ffn_grad_all.astype(jnp.float32)
     ffn_grads = (
@@ -701,14 +706,7 @@
         ffn_grad_all[:, ff_width : 2 * ff_width],
         ffn_grad_all[:, 2 * ff_width :].T,
     )
-    grad_norm_one = ring_scatter(
-        (
-            contract_cols(grad_proj, w_inward[:, :wide])
-            + contract_cols(grad_proj_ab, w_inward[:, wide:])
-        ).astype(jnp.bfloat16),
-        ring,
-        3,
-    )
+    grad_norm_one = ring_scatter(norm_one_partial, ring, 3)
     grad_norm_one, wout_grad = lax.optimization_barrier((grad_norm_one, wout_grad))
     grad_in_part, grad_gain_in = pull_one(grad_norm_one)
     grad_input = grad_middle + grad_in_part

time: 1180 us -> 1170 us (level)
    unnamed x406 -> x410, local copies, waits for them, and re-layouts: 49 us -> 49.2 us
  transfers between devices with their start and end apart: 13 -> 13, of which waited for: 3 -> 2; matrix products, arithmetic and copies ran while one was open for 45% -> 46% of each run, Pallas kernels for 40% -> 40%
where the time goes in v14:
time: 1170 us
  Pallas kernels  464 us (40%)
  matrix products  343 us (29%)
  other arithmetic  142 us (12%)
  local copies, waits for them, and re-layouts  129 us (11%)
  blocking collectives  46.7 us (4%)
  waiting for transfers between devices  25.9 us (2%)
  between operations  17.3 us (1%)
    pallas_call x2, Pallas kernels, ring_scatter(): pl.pallas_call(partial(_ring_scatter_kernel, major, minor), out_shape=jax...  188 us
    pallas_call x2, Pallas kernels, ring_gather(): pl.pallas_call(partial(_ring_gather_kernel, major, minor), out_shape=jax....  180 us
    dot_general x6, matrix products, contract_cols(): lax.dot_general(left, right, (((1,), (1,)), ((), ())), preferred_element_...  71.1 us
    dot_general x6, matrix products, contract_rows(): lax.dot_general(left, right, (((0,), (0,)), ((), ())), preferred_element_...  54.9 us
    pallas_call x1, Pallas kernels, _recur_forward(): pl.pallas_call(partial(_recur_fwd_kernel, nb), grid=(heads, blocks), in_s...  49.3 us
    unnamed x410, local copies, waits for them, and re-layouts  49.2 us
    pallas_call x1, Pallas kernels, delta_rule(): states, updates = state_recurrence(u0, w, kt, c)  46.2 us
    psum x1, blocking collectives, on_device(): lax.psum((grad_gain_in, grad_gain_ffn, core_grads[11], grad_a_full, grad_...  41.6 us
  transfers between devices with their start and end apart: 13, of which 2 were waited for; matrix products, arithmetic and copies ran while one was open for 46% of the time, Pallas kernels for 40%

profile of v14, /device:TPU:0, one launch (start us, length us, event | category | flops | bytes accessed | tf_op | source)
XLA Modules:
  0.0 1168.9 jit_solution(7227541775238542714)
XLA Ops:
  19.1 91.2 %ring_gather_head.2 = bf16[2048,2048]{1,0:T(8,128)(2,1)} custom-call(bf16[256,2048]{1,0:T(8,128)(2,1)} %fusion.33.x_ref), custom_call_target="tpu_custom_call" | custom-call | tf_op jit(solution)/shard_map/ring_gather_head/pallas_call | solution.py:498
  127.7 18.3 %fusion.171 = f32[2048,1540]{0,1:T(8,128)S(1)} fusion(bf16[2048,2048]{1,0:T(8,128)(2,1)} %ring_gather_head.2, bf16[2048,1540]{1,0:T(8,128)(2,1)} %all-gather.10.cloned.1.call-done), kind=kOutput, calls=%fused_computation.355 | convolution fusion | flops 12918456320 | bytes 27312128 | tf_op jit(solution)/shard_map/dot_general | solution.py:618
  274.5 49.3 %jvp_delta_state_forward_.1 = (f32[2,32,256,128]{3,2,1,0:T(8,128)}, f32[2,32,64,256]{3,2,1,0:T(8,128)}) custom-call(f32[2,32,64,256]{3,2,1,0:T(8,128)} %slice.364.u0_ref, f32[2,32,64,128]{3,2,1,0:T(8,128)} %slice.365.w_ref, f32[2,32,64,128]{3,2,1,0:T(8,128)} %get-tuple-element.229.kt_ref, f32[2,32,1,128]{3,2,1,0:T(1,128)} %broadcast_in_dim.34.c_ref), custom_call_target="tpu_custom_call" | custom-call | flops 3221225472 | bytes 20971520 | tf_op jit(solution)/shard_map/jvp(delta_state_forward)/pallas_call | solution.py:121
  329.7 9.5 fusion.173
  358.0 9.0 convolution_convert_fusion.3.y_ref
  367.0 102.1 %ring_scatter_head.2 = f32[256,2048]{1,0:T(8,128)} custom-call(bf16[2048,2048]{1,0:T(8,128)(2,1)} %convolution_convert_fusion.3.y_ref), custom_call_target="tpu_custom_call" | custom-call | tf_op jit(solution)/shard_map/ring_scatter_head/pallas_call | solution.py:517
  472.8 12.1 %fusion.175 = f32[1024,1408]{1,0:T(8,128)} fusion(bf16[1024,2048]{1,0:T(8,128)(2,1)} %bitcast.375, bf16[2048,1408]{0,1:T(8,128)(2,1)} %all-gather.14.cloned.1.call-done), kind=kOutput, calls=%fused_computation.359 | convolution fusion | flops 5905580032 | bytes 15728640 | tf_op jit(solution)/shard_map/dot_general | solution.py:659
  485.0 21.5 %all-gather.16.cloned.1.call-done = bf16[1024,2048]{1,0:T(8,128)(2,1)} async-done(((bf16[256,2048]{1,0:T(8,128)(2,1)}), bf16[1024,2048]{1,0:T(8,128)(2,1)}) %all-gather.16.cloned.1.call-update) | async-done | bytes 4194320 | tf_op jit(solution)/shard_map/all_gather | solution.py:653
  506.5 11.8 %fusion.11 = f32[1024,1408]{1,0:T(8,128)} fusion(bf16[1024,2048]{1,0:T(8,128)(2,1)} %all-gather.16.cloned.1.call-done, bf16[2048,2816]{1,0:T(8,128)(2,1)} %all-gather.12.cloned.1.call-done), kind=kOutput, calls=%fused_computation.29 | convolution fusion | flops 5905580032 | bytes 15728640 | tf_op jit(solution)/shard_map/dot_general | solution.py:654
  518.3 16.5 %multiply_convert_fusion = (bf16[1024,1408]{1,0:T(8,128)(2,1)}, bf16[1024,1408]{1,0:T(8,128)(2,1)}, bf16[1024,1408]{1,0:T(8,128)(2,1)}) fusion(f32[1024,1408]{1,0:T(8,128)} %fusion.11, f32[1024,1408]{1,0:T(8,128)} %fusion.175, bf16[1024,2048]{1,0:T(8,128)(2,1)} %all-gather.16.cloned.1.call-done, bf16[2048,2816]{1,0:T(8,128)(2,1)} %all-gather.12.cloned.1.call-done), kind=kOutput, calls=%fused_computation.20 | convolution fusion | flops 5928648704 | bytes 30146560 | tf_op jit(solution)/shard_map/dot_general | solution.py:655
  534.8 10.4 fusion.9
  545.2 10.5 add_convert_fusion.1
  555.8 11.0 convolution_convert_fusion.5
  566.9 9.2 convolution_convert_fusion
  605.3 89.0 %ring_gather_head.3 = bf16[2048,2048]{1,0:T(8,128)(2,1)} custom-call(bf16[256,2048]{1,0:T(8,128)(2,1)} %fusion.147.x_ref), custom_call_target="tpu_custom_call" | custom-call | tf_op jit(solution)/shard_map/ring_gather_head/pallas_call | solution.py:498
  724.5 17.8 %fusion.23.ds_ref = f32[2,32,256,128]{3,2,1,0:T(8,128)} fusion(f32[2,32,64,128]{3,2,1,0:T(8,128)S(1)} %bitcast.325, f32[2,32,64,256]{3,2,1,0:T(8,128)S(1)} %bitcast.317, f32[2,32,64]{2,1,0:T(8,128)S(1)} %copy-done.94), kind=kOutput, calls=%fused_computation.67 | convolution fusion | flops 1611661312 | bytes 14696448 | tf_op jit(solution)/shard_map/transpose(jvp(vmap(nid,nvd->niv)))/dot_general | solution.py:298
  742.3 46.2 %transpose_jvp_delta_state_backward__.1 = (f32[2,32,64,256]{3,2,1,0:T(8,128)}, f32[2,32,64,128]{3,2,1,0:T(8,128)}, f32[2,32,64,128]{3,2,1,0:T(8,128)}, f32[2,32,1,128]{3,2,1,0:T(1,128)}) custom-call(f32[2,32,256,128]{3,2,1,0:T(8,128)} %get-tuple-element.55.s_ref, f32[2,32,64,256]{3,2,1,0:T(8,128)} %get-tuple-element.56.u_ref, ...), custom_call_target="tpu_custom_call" | custom-call | flops 6442450944 | bytes 41943040 | tf_op jit(solution)/shard_map/transpose(jvp(delta_state_backward))/pallas_call | solution.py:309
  817.3 10.8 fusion.6
  947.3 10.1 convolution_convert_fusion.6
  958.6 20.1 %fusion = f32[2048,2048]{1,0:T(8,128)} fusion(bf16[2048,1540]{1,0:T(8,128)(2,1)} %all-gather.10.cloned.1.call-done, bf16[2048,512]{0,1:T(8,128)(2,1)} %bitcast.338, bf16[2048,512]{0,1:T(8,128)(2,1)S(1)} %bitcast.334, bf16[2048,256]{0,1:T(8,128)(2,1)} %bitcast.342, bf16[2048,256]{0,1:T(8,128)(2,1)S(1)} %bitcast.340), kind=kOutput, calls=%fused_computation.9 | convolution fusion | flops 12910067712 | bytes 29360128 | tf_op jit(solution)/shard_map/dot_general | solution.py:554
  978.7 11.9 %add_convert_fusion.y_ref = bf16[2048,2048]{1,0:T(8,128)(2,1)} fusion(f32[2048,2048]{1,0:T(8,128)} %fusion, bf16[2048,1540]{1,0:T(8,128)(2,1)} %all-gather.10.cloned.1.call-done, bf16[2048,2]{0,1:T(2,128)(2,1)S(1)} %fusion.108, bf16[2048,2]{0,1:T(2,128)(2,1)S(1)} %bitcast.351), kind=kOutput, calls=%fused_computation.1 | convolution fusion | flops 41975808 | bytes 25706496 | tf_op jit(solution)/shard_map/dot_general | solution.py:554
  990.6 17.6 %convolution_convert_fusion.4 = bf16[2048,1536]{1,0:T(8,128)(2,1)} fusion(bf16[2048,2048]{1,0:T(8,128)(2,1)} %ring_gather_head.2, bf16[2048,512]{0,1:T(8,128)(2,1)S(1)} %bitcast.339, bf16[2048,512]{0,1:T(8,128)(2,1)S(1)} %bitcast.335, bf16[2048,256]{0,1:T(8,128)(2,1)S(1)} %bitcast.343, bf16[2048,256]{0,1:T(8,128)(2,1)S(1)} %bitcast.341), kind=kOutput, calls=%fused_computation.8 | convolution fusion | flops 12913213440 | bytes 20971520 | tf_op jit(solution)/shard_map/dot_general | solution.py:548
  1008.2 86.1 %ring_scatter_head.3 = f32[256,2048]{1,0:T(8,128)} custom-call(bf16[2048,2048]{1,0:T(8,128)(2,1)} %add_convert_fusion.y_ref), custom_call_target="tpu_custom_call" | custom-call | tf_op jit(solution)/shard_map/ring_scatter_head/pallas_call | solution.py:517
  1101.1 41.6 %all-reduce.39 = (f32[16]{0:T(128)}, f32[16]{0:T(128)}, f32[256]{0:T(256)}, f32[2048]{0:T(1024)}, f32[2048]{0:T(1024)}) all-reduce(f32[16]{0:T(128)S(1)} %dynamic_update_slice.6, f32[16]{0:T(128)S(1)} %dynamic_update_slice.7, f32[256]{0:T(256)S(1)} %copy-done.169, ...), channel_id=1, replica_groups=mesh['head'=8,'row'=4] {'head','row'}, use_global_device_ids=true, to_apply=%region_42.43 | all-reduce | flops 4384 | bytes 35072 | tf_op jit(solution)/shard_map/psum | solution.py:742
  (639 shorter events, 417.9 us)
Async XLA Ops:
  7.2 106.7 %all-gather.8.cloned.1.call-start = ((), (), s32[]{:S(2)}) async-start(), calls=%async_computation.7 | async-start | bytes 2621440 | tf_op jit(solution)/shard_map/all_gather | solution.py:606
  9.5 118.2 %all-gather.10.cloned.1.call-start = ((), (), s32[]{:S(2)}) async-start(), calls=%async_computation.8 | async-start | bytes 8519680 | tf_op jit(solution)/shard_map/all_gather | solution.py:596
  13.5 344.5 %all-gather.18.cloned.1.call-start = ((), (), s32[]{:S(2)}) async-start(), calls=%async_computation.17 | async-start | bytes 5242880 | tf_op jit(solution)/shard_map/all_gather | solution.py:611
  14.2 343.8 %all-gather.12.cloned.1.call-start = ((), (), s32[]{:S(2)}) async-start(), calls=%async_computation.9 | async-start | bytes 12976128 | tf_op jit(solution)/shard_map/all_gather | solution.py:616
  113.9 358.9 %all-gather.14.cloned.1.call-start = ((), (), s32[]{:S(2)}) async-start(), calls=%async_computation.10 | async-start | bytes 6488064 | tf_op jit(solution)/shard_map/all_gather | solution.py:617
  127.1 107.8 %copy-start.105 = (f32[2048]{0:T(1024)}, f32[2048]{0:T(1024)S(1)}, u32[]{:S(2)}) copy-start(f32[2048]{0:T(1024)S(1)} %get-tuple-element.306) | copy-start | bytes 24580
  127.1 107.8 %copy-start.107 = (f32[2048]{0:T(1024)}, f32[2048]{0:T(1024)S(1)}, u32[]{:S(2)}) copy-start(f32[2048]{0:T(1024)S(1)} %get-tuple-element.307) | copy-start | bytes 24580
  127.4 211.8 %copy-start.12 = (f32[32,64,64]{1,2,0:T(8,128)}, f32[32,64,64]{1,2,0:T(8,128)S(1)}, u32[]{:S(2)}) copy-start(f32[32,64,64]{1,2,0:T(8,128)S(1)} %get-tuple-element.297) | copy-start | bytes 1572868
  127.4 211.8 %copy-start.39 = (pred[32,64,64]{1,2,0:T(8,128)(4,1)}, pred[32,64,64]{1,2,0:T(8,128)(4,1)S(1)}, u32[]{:S(2)}) copy-start(pred[32,64,64]{1,2,0:T(8,128)(4,1)S(1)} %get-tuple-element.296) | copy-start | bytes 393220
  127.5 379.0 %all-gather.16.cloned.1.call-start = ((), (), s32[]{:S(2)}) async-start(), calls=%async_computation.11 | async-start | bytes 5242880 | tf_op jit(solution)/shard_map/all_gather | solution.py:653
  153.1 107.4 %copy-start.75 = (f32[2,32,64]{2,1,0:T(8,128)}, f32[2,32,64]{2,1,0:T(8,128)S(1)}, u32[]{:S(2)}) copy-start(f32[2,32,64]{2,1,0:T(8,128)S(1)} %mul.977) | copy-start | bytes 49156
  155.2 184.1 %copy-start.61 = (f32[2,32,64]{2,1,0:T(8,128)}, f32[2,32,64]{2,1,0:T(8,128)S(1)}, u32[]{:S(2)}) copy-start(f32[2,32,64]{2,1,0:T(8,128)S(1)} %reduce_window_sum.22) | copy-start | bytes 49156
  173.9 152.3 %copy-start.5 = (f32[2,2048,128]{2,1,0:T(8,128)}, f32[2,2048,128]{2,1,0:T(8,128)S(1)}, u32[]{:S(2)}) copy-start(f32[2,2048,128]{2,1,0:T(8,128)S(1)} %get-tuple-element.230) | copy-start | bytes 6291460
  367.0 102.1 %copy-start.42 = (bf16[1,256,2048]{2,1,0:T(8,128)(2,1)S(1)}, bf16[1,256,2048]{2,1,0:T(8,128)(2,1)}, u32[]{:S(2)}) copy-start(bf16[1,256,2048]{2,1,0:T(8,128)(2,1)} %param.22) | copy-start | bytes 3145732
  471.1 131.9 %copy-start.20 = (f32[256,2048]{1,0:T(8,128)}, f32[256,2048]{1,0:T(8,128)S(1)}, u32[]{:S(2)}) copy-start(f32[256,2048]{1,0:T(8,128)S(1)} %get-tuple-element.228) | copy-start | bytes 6291460
  471.2 131.8 %copy-start.141 = (f32[256]{0:T(256)}, f32[256]{0:T(256)S(1)}, u32[]{:S(2)}) copy-start(f32[256]{0:T(256)S(1)} %fusion.124) | copy-start | bytes 3076
  472.7 127.7 %reduce-scatter.12.cloned.1.call-start = ((), (), s32[]{:S(2)}) async-start(), calls=%async_computation.12 | async-start | bytes 5242880 | tf_op jit(solution)/shard_map/reduce_scatter | solution.py:666
  555.8 384.3 %reduce-scatter.14.cloned.1.call-start = ((), (), s32[]{:S(2)}) async-start(), calls=%async_computation.13 | async-start | bytes 5242880 | tf_op jit(solution)/shard_map/reduce_scatter | solution.py:681
  566.8 441.4 %reduce-scatter.18.cloned.1.call-start = ((), (), s32[]{:S(2)}) async-start(), calls=%async_computation.15 | async-start | bytes 19464192 | tf_op jit(solution)/shard_map/reduce_scatter | solution.py:683
  694.3 400.4 %reduce-scatter.24.cloned.1.call-start = ((), (), s32[]{:S(2)}) async-start(), calls=%async_computation.19 | async-start | bytes 327680
  941.3 155.7 %reduce-scatter.22.cloned.1.call-start = ((), (), s32[]{:S(2)}) async-start(), calls=%async_computation.18 | async-start | bytes 655360
  947.2 151.4 %reduce-scatter.16.cloned.1.call-start = ((), (), s32[]{:S(2)}) async-start(), calls=%async_computation.14 | async-start | bytes 2621440 | tf_op jit(solution)/shard_map/reduce_scatter | solution.py:686
  957.4 201.0 %reduce-scatter.20.cloned.1.call-start = ((), (), s32[]{:S(2)}) async-start(), calls=%async_computation.16 | async-start | bytes 7864320 | tf_op jit(solution)/shard_map/reduce_scatter | solution.py:713
  1008.2 90.4 %copy-start.43 = (bf16[1,256,2048]{2,1,0:T(8,128)(2,1)S(1)}, bf16[1,256,2048]{2,1,0:T(8,128)(2,1)}, u32[]{:S(2)}) copy-start(bf16[1,256,2048]{2,1,0:T(8,128)(2,1)} %param.22) | copy-start | bytes 3145732
  (181 other events, 1610.4 us)
Sparse Core Ops, SparseCore 0:
  10.2 25.2 all-gather.7
  37.7 49.3 all-gather.9
  88.7 34.5 all-gather.17
  125.9 163.6 all-gather.11
  292.0 99.5 all-gather.13
  472.9 33.5 all-gather.15
  555.9 44.4 reduce-scatter.11
  603.1 44.4 reduce-scatter.13
  694.4 291.4 reduce-scatter.17
  989.0 19.0 reduce-scatter.23
  1011.2 21.6 reduce-scatter.21
  1035.4 31.4 reduce-scatter.15
  1069.4 59.0 reduce-scatter.19

commit v15 on v14

--- a/solution.py
+++ b/solution.py
@@ -739,9 +739,18 @@
     grad_dt_full = lax.dynamic_update_slice_in_dim(
         jnp.zeros((head_total,), jnp.float32), core_grads[10], head_first, 0
     )
-    small_sums = lax.psum(
-        (grad_gain_in, grad_gain_ffn, core_grads[11], grad_a_full, grad_dt_full), ("head", "row")
-    )
+    small_parts = (grad_gain_in, grad_gain_ffn, core_grads[11], grad_a_full, grad_dt_full)
+    small_edges = [0]
+    for part in small_parts:
+        small_edges.append(small_edges[-1] + part.shape[0])
+    small_width = 384
+    small_rows = -(-small_edges[-1] // (16 * small_width)) * 16
+    small_local = jnp.pad(
+        jnp.concatenate(small_parts), (0, small_rows * small_width - small_edges[-1])
+    ).reshape(small_rows, small_width)
+    small_heads = ring_gather(small_local, ring, 5).reshape(-1, small_rows, small_width)
+    small_all = lax.psum(jnp.sum(small_heads, axis=0), "row").reshape(-1)
+    small_sums = [small_all[small_edges[i] : small_edges[i + 1]] for i in range(5)]
     return (
         final_out[None],
         grad_input[None],

time: 1170 us -> 1170 us (level)
  blocking collectives: 46.7 us -> 15.7 us
  Pallas kernels: 464 us -> 487 us
    psum x1, blocking collectives: 41.6 us -> 10.5 us  [on_device(): small_all = lax.psum(jnp.sum(small_heads, axis=0), 'row').reshape(-1)]
    pallas_call x2 -> x3, Pallas kernels: 180 us -> 202 us  [ring_gather(): pl.pallas_call(partial(_ring_gather_kernel, major, minor), out_shape=jax....]
  transfers between devices with their start and end apart: 13 -> 13, of which waited for: 2 -> 2; matrix products, arithmetic and copies ran while one was open for 46% -> 46% of each run, Pallas kernels for 40% -> 42%
where the time goes in v15:
time: 1170 us; the launch traced here: 1160 us
  Pallas kernels  487 us (42%)
  matrix products  343 us (29%)
  other arithmetic  143 us (12%)
  local copies, waits for them, and re-layouts  132 us (11%)
  waiting for transfers between devices  25.9 us (2%)
  between operations  17.3 us (1%)
  blocking collectives  15.7 us (1%)
    pallas_call x3, Pallas kernels, ring_gather(): pl.pallas_call(partial(_ring_gather_kernel, major, minor), out_shape=jax....  202 us
    pallas_call x2, Pallas kernels, ring_scatter(): pl.pallas_call(partial(_ring_scatter_kernel, major, minor), out_shape=jax...  190 us
    dot_general x6, matrix products, contract_cols(): lax.dot_general(left, right, (((1,), (1,)), ((), ())), preferred_element_...  71 us
    dot_general x6, matrix products, contract_rows(): lax.dot_general(left, right, (((0,), (0,)), ((), ())), preferred_element_...  54.9 us
    pallas_call x1, Pallas kernels, _recur_forward(): pl.pallas_call(partial(_recur_fwd_kernel, nb), grid=(heads, blocks), in_s...  49.3 us
    unnamed x410, local copies, waits for them, and re-layouts  49.2 us
    pallas_call x1, Pallas kernels, delta_rule(): states, updates = state_recurrence(u0, w, kt, c)  46.3 us
    dot_general x3, matrix products, chunk_finish(): jnp.einsum('nid,nvd->niv', q, states, precision=precise)  34.7 us
  transfers between devices with their start and end apart: 13, of which 2 were waited for; matrix products, arithmetic and copies ran while one was open for 46% of the time, Pallas kernels for 42%

profile of v15, /device:TPU:0, one launch (start us, length us, event | category | flops | bytes accessed | tf_op | source)
XLA Modules:
  0.0 1163.9 jit_solution(12914991086864502428)
XLA Ops:
  19.1 91.1 %ring_gather_head.3 = bf16[2048,2048]{1,0:T(8,128)(2,1)} custom-call(bf16[256,2048]{1,0:T(8,128)(2,1)} %fusion.33.x_ref), custom_call_target="tpu_custom_call" | custom-call | tf_op jit(solution)/shard_map/ring_gather_head/pallas_call | solution.py:498
  127.6 18.3 %fusion.173 = f32[2048,1540]{0,1:T(8,128)S(1)} fusion(bf16[2048,2048]{1,0:T(8,128)(2,1)} %ring_gather_head.3, bf16[2048,1540]{1,0:T(8,128)(2,1)} %all-gather.10.cloned.1.call-done), kind=kOutput, calls=%fused_computation.357 | convolution fusion | flops 12918456320 | bytes 27312128 | tf_op jit(solution)/shard_map/dot_general | solution.py:618
  274.4 49.3 %jvp_delta_state_forward_.1 = (f32[2,32,256,128]{3,2,1,0:T(8,128)}, f32[2,32,64,256]{3,2,1,0:T(8,128)}) custom-call(f32[2,32,64,256]{3,2,1,0:T(8,128)} %slice.384.u0_ref, f32[2,32,64,128]{3,2,1,0:T(8,128)} %slice.385.w_ref, f32[2,32,64,128]{3,2,1,0:T(8,128)} %get-tuple-element.224.kt_ref, f32[2,32,1,128]{3,2,1,0:T(1,128)} %broadcast_in_dim.34.c_ref), custom_call_target="tpu_custom_call" | custom-call | flops 3221225472 | bytes 20971520 | tf_op jit(solution)/shard_map/jvp(delta_state_forward)/pallas_call | solution.py:121
  329.6 9.5 fusion.175
  366.8 102.1 %ring_scatter_head.2 = f32[256,2048]{1,0:T(8,128)} custom-call(bf16[2048,2048]{1,0:T(8,128)(2,1)} %convolution_convert_fusion.3.y_ref), custom_call_target="tpu_custom_call" | custom-call | tf_op jit(solution)/shard_map/ring_scatter_head/pallas_call | solution.py:517
  472.5 12.1 %fusion.177 = f32[1024,1408]{1,0:T(8,128)} fusion(bf16[1024,2048]{1,0:T(8,128)(2,1)} %bitcast.377, bf16[2048,1408]{0,1:T(8,128)(2,1)} %all-gather.14.cloned.1.call-done), kind=kOutput, calls=%fused_computation.361 | convolution fusion | flops 5905580032 | bytes 15728640 | tf_op jit(solution)/shard_map/dot_general | solution.py:659
  484.7 21.5 %all-gather.16.cloned.1.call-done = bf16[1024,2048]{1,0:T(8,128)(2,1)} async-done(((bf16[256,2048]{1,0:T(8,128)(2,1)}), bf16[1024,2048]{1,0:T(8,128)(2,1)}) %all-gather.16.cloned.1.call-update) | async-done | bytes 4194320 | tf_op jit(solution)/shard_map/all_gather | solution.py:653
  506.2 11.8 %fusion.11 = f32[1024,1408]{1,0:T(8,128)} fusion(bf16[1024,2048]{1,0:T(8,128)(2,1)} %all-gather.16.cloned.1.call-done, bf16[2048,2816]{1,0:T(8,128)(2,1)} %all-gather.12.cloned.1.call-done), kind=kOutput, calls=%fused_computation.29 | convolution fusion | flops 5905580032 | bytes 15728640 | tf_op jit(solution)/shard_map/dot_general | solution.py:654
  518.0 16.5 %multiply_convert_fusion = (bf16[1024,1408]{1,0:T(8,128)(2,1)}, bf16[1024,1408]{1,0:T(8,128)(2,1)}, bf16[1024,1408]{1,0:T(8,128)(2,1)}) fusion(f32[1024,1408]{1,0:T(8,128)} %fusion.11, f32[1024,1408]{1,0:T(8,128)} %fusion.177, bf16[1024,2048]{1,0:T(8,128)(2,1)} %all-gather.16.cloned.1.call-done, bf16[2048,2816]{1,0:T(8,128)(2,1)} %all-gather.12.cloned.1.call-done), kind=kOutput, calls=%fused_computation.20 | convolution fusion | flops 5928648704 | bytes 30146560 | tf_op jit(solution)/shard_map/dot_general | solution.py:655
  534.5 10.4 fusion.9
  544.9 10.5 add_convert_fusion.1
  555.5 11.0 convolution_convert_fusion.5
  566.5 9.2 convolution_convert_fusion
  605.0 88.9 %ring_gather_head.4 = bf16[2048,2048]{1,0:T(8,128)(2,1)} custom-call(bf16[256,2048]{1,0:T(8,128)(2,1)} %fusion.147.x_ref), custom_call_target="tpu_custom_call" | custom-call | tf_op jit(solution)/shard_map/ring_gather_head/pallas_call | solution.py:498
  724.1 17.8 %fusion.23.ds_ref = f32[2,32,256,128]{3,2,1,0:T(8,128)} fusion(f32[2,32,64,128]{3,2,1,0:T(8,128)S(1)} %bitcast.326, f32[2,32,64,256]{3,2,1,0:T(8,128)S(1)} %bitcast.318, f32[2,32,64]{2,1,0:T(8,128)S(1)} %copy-done.94), kind=kOutput, calls=%fused_computation.67 | convolution fusion | flops 1611661312 | bytes 14696448 | tf_op jit(solution)/shard_map/transpose(jvp(vmap(nid,nvd->niv)))/dot_general | solution.py:298
  742.0 46.3 %transpose_jvp_delta_state_backward__.1 = (f32[2,32,64,256]{3,2,1,0:T(8,128)}, f32[2,32,64,128]{3,2,1,0:T(8,128)}, f32[2,32,64,128]{3,2,1,0:T(8,128)}, f32[2,32,1,128]{3,2,1,0:T(1,128)}) custom-call(f32[2,32,256,128]{3,2,1,0:T(8,128)} %get-tuple-element.55.s_ref, f32[2,32,64,256]{3,2,1,0:T(8,128)} %get-tuple-element.56.u_ref, ...), custom_call_target="tpu_custom_call" | custom-call | flops 6442450944 | bytes 41943040 | tf_op jit(solution)/shard_map/transpose(jvp(delta_state_backward))/pallas_call | solution.py:309
  816.9 10.8 fusion.6
  947.0 10.2 convolution_convert_fusion.6
  958.3 20.0 %fusion = f32[2048,2048]{1,0:T(8,128)} fusion(bf16[2048,1540]{1,0:T(8,128)(2,1)} %all-gather.10.cloned.1.call-done, bf16[2048,512]{0,1:T(8,128)(2,1)} %bitcast.339, bf16[2048,512]{0,1:T(8,128)(2,1)S(1)} %bitcast.335, bf16[2048,256]{0,1:T(8,128)(2,1)} %bitcast.343, bf16[2048,256]{0,1:T(8,128)(2,1)S(1)} %bitcast.341), kind=kOutput, calls=%fused_computation.9 | convolution fusion | flops 12910067712 | bytes 29360128 | tf_op jit(solution)/shard_map/dot_general | solution.py:554
  978.3 11.9 %add_convert_fusion.y_ref = bf16[2048,2048]{1,0:T(8,128)(2,1)} fusion(f32[2048,2048]{1,0:T(8,128)} %fusion, bf16[2048,1540]{1,0:T(8,128)(2,1)} %all-gather.10.cloned.1.call-done, bf16[2048,2]{0,1:T(2,128)(2,1)S(1)} %fusion.108, bf16[2048,2]{0,1:T(2,128)(2,1)S(1)} %bitcast.353), kind=kOutput, calls=%fused_computation.1 | convolution fusion | flops 41975808 | bytes 25706496 | tf_op jit(solution)/shard_map/dot_general | solution.py:554
  990.2 17.6 %convolution_convert_fusion.4 = bf16[2048,1536]{1,0:T(8,128)(2,1)} fusion(bf16[2048,2048]{1,0:T(8,128)(2,1)} %ring_gather_head.3, bf16[2048,512]{0,1:T(8,128)(2,1)S(1)} %bitcast.340, bf16[2048,512]{0,1:T(8,128)(2,1)S(1)} %bitcast.336, bf16[2048,256]{0,1:T(8,128)(2,1)S(1)} %bitcast.344, bf16[2048,256]{0,1:T(8,128)(2,1)S(1)} %bitcast.342), kind=kOutput, calls=%fused_computation.8 | convolution fusion | flops 12913213440 | bytes 20971520 | tf_op jit(solution)/shard_map/dot_general | solution.py:548
  1007.8 87.6 %ring_scatter_head.3 = f32[256,2048]{1,0:T(8,128)} custom-call(bf16[2048,2048]{1,0:T(8,128)(2,1)} %add_convert_fusion.y_ref), custom_call_target="tpu_custom_call" | custom-call | tf_op jit(solution)/shard_map/ring_scatter_head/pallas_call | solution.py:517
  1102.9 21.5 %ring_gather_head.5 = f32[128,384]{1,0:T(8,128)} custom-call(f32[16,384]{1,0:T(8,128)} %reshape.511.x_ref), custom_call_target="tpu_custom_call" | custom-call | tf_op jit(solution)/shard_map/ring_gather_head/pallas_call | solution.py:498
  1125.4 10.5 psum.7
  (648 shorter events, 430.2 us)
Async XLA Ops:
  7.2 106.5 %all-gather.8.cloned.1.call-start = ((), (), s32[]{:S(2)}) async-start(), calls=%async_computation.7 | async-start | bytes 2621440 | tf_op jit(solution)/shard_map/all_gather | solution.py:606
  9.5 118.0 %all-gather.10.cloned.1.call-start = ((), (), s32[]{:S(2)}) async-start(), calls=%async_computation.8 | async-start | bytes 8519680 | tf_op jit(solution)/shard_map/all_gather | solution.py:596
  13.5 344.3 %all-gather.18.cloned.1.call-start = ((), (), s32[]{:S(2)}) async-start(), calls=%async_computation.17 | async-start | bytes 5242880 | tf_op jit(solution)/shard_map/all_gather | solution.py:611
  14.2 343.6 %all-gather.12.cloned.1.call-start = ((), (), s32[]{:S(2)}) async-start(), calls=%async_computation.9 | async-start | bytes 12976128 | tf_op jit(solution)/shard_map/all_gather | solution.py:616
  113.8 358.8 %all-gather.14.cloned.1.call-start = ((), (), s32[]{:S(2)}) async-start(), calls=%async_computation.10 | async-start | bytes 6488064 | tf_op jit(solution)/shard_map/all_gather | solution.py:617
  126.9 107.8 %copy-start.105 = (f32[2048]{0:T(1024)}, f32[2048]{0:T(1024)S(1)}, u32[]{:S(2)}) copy-start(f32[2048]{0:T(1024)S(1)} %get-tuple-element.305) | copy-start | bytes 24580
  126.9 107.8 %copy-start.107 = (f32[2048]{0:T(1024)}, f32[2048]{0:T(1024)S(1)}, u32[]{:S(2)}) copy-start(f32[2048]{0:T(1024)S(1)} %get-tuple-element.306) | copy-start | bytes 24580
  127.3 211.8 %copy-start.12 = (f32[32,64,64]{1,2,0:T(8,128)}, f32[32,64,64]{1,2,0:T(8,128)S(1)}, u32[]{:S(2)}) copy-start(f32[32,64,64]{1,2,0:T(8,128)S(1)} %get-tuple-element.296) | copy-start | bytes 1572868
  127.3 211.8 %copy-start.39 = (pred[32,64,64]{1,2,0:T(8,128)(4,1)}, pred[32,64,64]{1,2,0:T(8,128)(4,1)S(1)}, u32[]{:S(2)}) copy-start(pred[32,64,64]{1,2,0:T(8,128)(4,1)S(1)} %get-tuple-element.295) | copy-start | bytes 393220
  127.3 378.9 %all-gather.16.cloned.1.call-start = ((), (), s32[]{:S(2)}) async-start(), calls=%async_computation.11 | async-start | bytes 5242880 | tf_op jit(solution)/shard_map/all_gather | solution.py:653
  152.9 107.4 %copy-start.75 = (f32[2,32,64]{2,1,0:T(8,128)}, f32[2,32,64]{2,1,0:T(8,128)S(1)}, u32[]{:S(2)}) copy-start(f32[2,32,64]{2,1,0:T(8,128)S(1)} %mul.977) | copy-start | bytes 49156
  155.0 184.1 %copy-start.61 = (f32[2,32,64]{2,1,0:T(8,128)}, f32[2,32,64]{2,1,0:T(8,128)S(1)}, u32[]{:S(2)}) copy-start(f32[2,32,64]{2,1,0:T(8,128)S(1)} %reduce_window_sum.22) | copy-start | bytes 49156
  173.7 152.4 %copy-start.5 = (f32[2,2048,128]{2,1,0:T(8,128)}, f32[2,2048,128]{2,1,0:T(8,128)S(1)}, u32[]{:S(2)}) copy-start(f32[2,2048,128]{2,1,0:T(8,128)S(1)} %get-tuple-element.225) | copy-start | bytes 6291460
  366.8 102.1 %copy-start.42 = (bf16[1,256,2048]{2,1,0:T(8,128)(2,1)S(1)}, bf16[1,256,2048]{2,1,0:T(8,128)(2,1)}, u32[]{:S(2)}) copy-start(bf16[1,256,2048]{2,1,0:T(8,128)(2,1)} %param.22) | copy-start | bytes 3145732
  470.9 131.8 %copy-start.20 = (f32[256,2048]{1,0:T(8,128)}, f32[256,2048]{1,0:T(8,128)S(1)}, u32[]{:S(2)}) copy-start(f32[256,2048]{1,0:T(8,128)S(1)} %get-tuple-element.223) | copy-start | bytes 6291460
  470.9 131.8 %copy-start.141 = (f32[256]{0:T(256)}, f32[256]{0:T(256)S(1)}, u32[]{:S(2)}) copy-start(f32[256]{0:T(256)S(1)} %fusion.124) | copy-start | bytes 3076
  472.5 127.6 %reduce-scatter.12.cloned.1.call-start = ((), (), s32[]{:S(2)}) async-start(), calls=%async_computation.12 | async-start | bytes 5242880 | tf_op jit(solution)/shard_map/reduce_scatter | solution.py:666
  555.4 384.3 %reduce-scatter.14.cloned.1.call-start = ((), (), s32[]{:S(2)}) async-start(), calls=%async_computation.13 | async-start | bytes 5242880 | tf_op jit(solution)/shard_map/reduce_scatter | solution.py:681
  566.5 441.3 %reduce-scatter.18.cloned.1.call-start = ((), (), s32[]{:S(2)}) async-start(), calls=%async_computation.15 | async-start | bytes 19464192 | tf_op jit(solution)/shard_map/reduce_scatter | solution.py:683
  694.0 402.0 %reduce-scatter.24.cloned.1.call-start = ((), (), s32[]{:S(2)}) async-start(), calls=%async_computation.19 | async-start | bytes 327680
  941.0 157.2 %reduce-scatter.22.cloned.1.call-start = ((), (), s32[]{:S(2)}) async-start(), calls=%async_computation.18 | async-start | bytes 655360
  946.9 152.9 %reduce-scatter.16.cloned.1.call-start = ((), (), s32[]{:S(2)}) async-start(), calls=%async_computation.14 | async-start | bytes 2621440 | tf_op jit(solution)/shard_map/reduce_scatter | solution.py:686
  957.1 196.2 %reduce-scatter.20.cloned.1.call-start = ((), (), s32[]{:S(2)}) async-start(), calls=%async_computation.16 | async-start | bytes 7864320 | tf_op jit(solution)/shard_map/reduce_scatter | solution.py:713
  1007.8 92.0 %copy-start.43 = (bf16[1,256,2048]{2,1,0:T(8,128)(2,1)S(1)}, bf16[1,256,2048]{2,1,0:T(8,128)(2,1)}, u32[]{:S(2)}) copy-start(bf16[1,256,2048]{2,1,0:T(8,128)(2,1)} %param.22) | copy-start | bytes 3145732
  (181 other events, 1582.9 us)
Sparse Core Ops, SparseCore 0:
  10.2 25.2 all-gather.7
  37.7 49.3 all-gather.9
  88.6 34.5 all-gather.17
  125.8 163.6 all-gather.11
  292.0 99.3 all-gather.13
  472.6 33.5 all-gather.15
  555.6 44.4 reduce-scatter.11
  602.8 44.4 reduce-scatter.13
  694.1 291.4 reduce-scatter.17
  988.6 19.0 reduce-scatter.23
  1010.8 21.6 reduce-scatter.21
  1035.1 31.4 reduce-scatter.15
  1069.1 58.3 reduce-scatter.19
